TPU v7x, 256 devices: a whole 4x4x8 slice. The times are simulated.
256 devices in a mesh: expert: 64 (over x, z, core), replica: 4 (over y).
Axes of the slice: x: 4, y: 4, z: 8, core: 2. Of those that a mesh axis runs over, the one named last changes fastest.
Arguments:
- tokens: bfloat16 [16384, 2048], P(('expert', 'replica')), may hold values from -6 to 6
- route_ids: int32 [16384, 6], P(('expert', 'replica')), may hold values from 0 to 63, all different within a row; in each aligned block of 64 rows (0 to 63, 64 to 127, ...) at most 8 rows name the same one
- gate_probs: float32 [16384, 6], P(('expert', 'replica')), may hold values from 0.05 to 0.35
- out_cot: bfloat16 [16384, 2048], P(('expert', 'replica')), may hold values from -6 to 6
- w_gate: bfloat16 [64, 2048, 768], P('expert'), may hold values from -0.125 to 0.125
- w_up: bfloat16 [64, 2048, 768], P('expert'), may hold values from -0.125 to 0.125
- w_down: bfloat16 [64, 768, 2048], P('expert'), may hold values from -0.21875 to 0.21875
Outputs:
- combined: bfloat16 [16384, 2048], P(('expert', 'replica'))
- grad_tokens: bfloat16 [16384, 2048], P(('expert', 'replica'))
- grad_gate: bfloat16 [64, 2048, 768], P('expert', 'replica')
- grad_up: bfloat16 [64, 2048, 768], P('expert', 'replica')
- grad_down: bfloat16 [64, 768, 2048], P('expert', 'replica')
Inputs may be any that keep to these rules, and one draw needn't show every extreme that they name: `route_ids`: A token's 6 experts differ. Among the 64 tokens of one device, at most 8 choose any one expert, and in every draw some device's tokens choose some expert exactly 8 times.
All inputs are finite; a program needn't handle non-finite values.
Results may differ from a plain program's by a relative error of at most 0.0095.
Values may be sent and summed in bfloat16 or wider, within the bound.
A program may use at most 128 MiB of HBM per device.

v0:
```python
import jax
import jax.numpy as jnp
from jax import lax
from jax.sharding import PartitionSpec as P


def slots(routes, experts, capacity):
    flat_ids = routes.reshape(-1)
    one_hot = (flat_ids[:, None] == jnp.arange(experts, dtype=jnp.int32)[None, :]).astype(jnp.int32)
    before = jnp.cumsum(one_hot, axis=0) - one_hot
    slot_rank = jnp.sum(before * one_hot, axis=1)
    return flat_ids * capacity + slot_rank


def place(token_rows, positions, total_rows):
    return (
        jnp.zeros((total_rows, token_rows.shape[1]), token_rows.dtype).at[positions].set(token_rows)
    )


def hidden_rows(token_rows, gate_weight, up_weight):
    pre_gate = jnp.dot(token_rows, gate_weight, preferred_element_type=jnp.float32)
    pre_up = jnp.dot(token_rows, up_weight, preferred_element_type=jnp.float32)
    activation = (jax.nn.silu(pre_gate) * pre_up).astype(jnp.bfloat16)
    return (pre_gate, pre_up, activation)


def backward_rows(grad_rows, pre_gate, pre_up, gate_weight, up_weight, down_weight):
    contract = (((1,), (1,)), ((), ()))
    d_hidden = lax.dot_general(grad_rows, down_weight, contract, preferred_element_type=jnp.float32)
    sigmoid_gate = jax.nn.sigmoid(pre_gate)
    d_gate = (d_hidden * pre_up * sigmoid_gate * (1.0 + pre_gate * (1.0 - sigmoid_gate))).astype(
        jnp.bfloat16
    )
    d_up = (d_hidden * pre_gate * sigmoid_gate).astype(jnp.bfloat16)
    back_rows = lax.dot_general(d_gate, gate_weight, contract, preferred_element_type=jnp.float32)
    back_rows = back_rows + lax.dot_general(
        d_up, up_weight, contract, preferred_element_type=jnp.float32
    )
    return (back_rows.astype(jnp.bfloat16), d_gate, d_up)


def outer_sum(left, right):
    return lax.dot_general(
        left, right, (((0,), (0,)), ((), ())), preferred_element_type=jnp.float32
    )


def per_device(tokens, route_ids, gate_probs, out_cot, w_gate, w_up, w_down):
    experts = lax.axis_size("expert")
    tok_rows, features = tokens.shape
    top_count = route_ids.shape[1]
    hidden = w_gate.shape[2]
    capacity = max(2, tok_rows * top_count * 4 // (3 * experts))
    total_rows = experts * capacity
    positions = slots(route_ids, experts, capacity)
    gate_weight = w_gate[0]
    up_weight = w_up[0]
    down_weight = w_down[0]
    outgoing = place(jnp.repeat(tokens, top_count, axis=0), positions, total_rows).reshape(
        experts, capacity, features
    )
    slot_rows = lax.all_to_all(outgoing, "expert", split_axis=0, concat_axis=0, tiled=True)
    length = slot_rows.shape[1]
    flat_rows = slot_rows.reshape(-1, features)
    pre_gate, pre_up, expert_activation = hidden_rows(flat_rows, gate_weight, up_weight)
    result = jnp.dot(expert_activation, down_weight, preferred_element_type=jnp.float32).astype(
        jnp.bfloat16
    )
    returned = lax.all_to_all(
        result.reshape(experts, length, features), "expert", split_axis=0, concat_axis=0, tiled=True
    )
    results = (
        returned,
        slot_rows,
        pre_gate.reshape(experts, length, hidden),
        pre_up.reshape(experts, length, hidden),
        expert_activation.reshape(experts, length, hidden),
    )
    returned = results[0].reshape(-1, features)
    received = results[1].reshape(-1, features)
    pre_gate = results[2].reshape(-1, hidden)
    pre_up = results[3].reshape(-1, hidden)
    activation = results[4].reshape(-1, hidden)
    picked = returned[positions].reshape(tok_rows, top_count, features)
    combined = jnp.einsum("tk,tkd->td", gate_probs, picked.astype(jnp.float32)).astype(jnp.bfloat16)
    scaled = (gate_probs[:, :, None] * out_cot[:, None, :].astype(jnp.float32)).astype(jnp.bfloat16)
    grad_out = place(scaled.reshape(-1, features), positions, total_rows).reshape(
        experts, capacity, features
    )
    grads_in = lax.all_to_all(grad_out, "expert", split_axis=0, concat_axis=0, tiled=True).reshape(
        -1, features
    )
    back_rows, d_gate, d_up = backward_rows(
        grads_in, pre_gate, pre_up, gate_weight, up_weight, down_weight
    )
    returned_grad = lax.all_to_all(
        back_rows.reshape(experts, capacity, features),
        "expert",
        split_axis=0,
        concat_axis=0,
        tiled=True,
    )
    returned_grad = returned_grad.reshape(-1, features)
    grad_tokens = jnp.sum(
        returned_grad[positions].reshape(tok_rows, top_count, features).astype(jnp.float32), axis=1
    )
    grad_tokens = grad_tokens.astype(jnp.bfloat16)
    gate_up_grad = jnp.concatenate([d_gate, d_up], axis=1)
    gate_up_sum = lax.psum_scatter(
        outer_sum(received, gate_up_grad).astype(jnp.bfloat16),
        "replica",
        scatter_dimension=0,
        tiled=True,
    ).astype(jnp.float32)
    down_sum = lax.psum_scatter(
        outer_sum(activation, grads_in).astype(jnp.bfloat16),
        "replica",
        scatter_dimension=0,
        tiled=True,
    )
    grad_gate = gate_up_sum[:, :hidden].astype(jnp.bfloat16)[None]
    grad_up = gate_up_sum[:, hidden:].astype(jnp.bfloat16)[None]
    grad_down = down_sum[None]
    return (combined, grad_tokens, grad_gate, grad_up, grad_down)


def solution(mesh):
    placed = (
        P(("expert", "replica"), None),
        P(("expert", "replica"), None),
        P(("expert", "replica"), None),
        P(("expert", "replica"), None),
        P("expert", None, None),
        P("expert", None, None),
        P("expert", None, None),
    )
    return jax.shard_map(
        per_device,
        mesh=mesh,
        in_specs=placed,
        out_specs=(
            P(("expert", "replica"), None),
            P(("expert", "replica"), None),
            P("expert", "replica", None),
            P("expert", "replica", None),
            P("expert", "replica", None),
        ),
        check_vma=False,
    )
```

profile of v0, /device:TPU:1, one launch (start us, length us, event | category | flops | bytes accessed | tf_op | source)
XLA Modules:
  0.0 304.9 jit_solution(6450701354044942094)
XLA Ops:
  7.2 0.0 copy-start
  7.2 0.8 broadcast_multiply_fusion
  8.0 0.9 copy.13
  8.9 0.1 eq.29
  9.0 0.1 eq.25
  9.2 0.1 copy.12
  9.3 0.1 mul.64
  9.4 0.9 reduce-window.6
  10.4 0.2 slice_reduce_fusion
  10.6 2.6 broadcast_in_dim.8
  13.2 3.7 %reshape.129 = bf16[384,2048]{1,0:T(8,128)(2,1)} reshape(bf16[64,6,2048]{2,1,0:T(8,128)(2,1)} %broadcast_in_dim.8) | data formatting | bytes 3145728 | tf_op jit(solution)/shard_map/reshape | solution.py:60
  16.9 0.1 fusion.38
  17.1 5.3 %scatter_custom_fusion = bf16[512,2048]{1,0:T(8,128)(2,1)} fusion(s32[384]{0:T(512)S(1)} %fusion.40, bf16[384,2048]{1,0:T(8,128)(2,1)} %reshape.129, bf16[]{:T(256)} %constant.5.clone.1), kind=kCustom, calls=%fused_computation.38 | custom fusion | bytes 2097664 | tf_op jit(solution)/shard_map/scatter | solution.py:17
  22.3 0.0 copy-start.2
  22.3 0.0 copy-start.1
  22.3 13.3 %all-to-all-start = ((bf16[64,8,2048]{2,1,0:T(8,128)(2,1)}), bf16[64,8,2048]{2,1,0:T(8,128)(2,1)}, u32[]{:S(2)}, u32[]{:S(2)}) async-start(bf16[64,8,2048]{2,1,0:T(8,128)(2,1)} %bitcast.85), calls=%async_computation | async-start | bytes 4194304 | tf_op jit(solution)/shard_map/all_to_all | solution.py:63
  35.7 0.0 copy-done.2
  35.7 0.1 copy.16
  35.8 0.1 mul.68
  35.9 0.0 copy-done.1
  35.9 2.4 mul.70
  38.4 4.8 %mul.71 = f32[384,2048]{1,0:T(8,128)} reshape(f32[64,6,2048]{2,1,0:T(8,128)} %mul.70) | data formatting | bytes 6291456 | tf_op jit(solution)/shard_map/mul | solution.py:87
  43.1 5.8 %scatter_custom_fusion.1 = bf16[512,2048]{1,0:T(8,128)(2,1)} fusion(s32[384]{0:T(512)S(1)} %fusion.40, f32[384,2048]{1,0:T(8,128)} %mul.71, f32[384]{0:T(512)S(1)} %mul.68, bf16[]{:T(256)} %constant.5.clone.1), kind=kCustom, calls=%fused_computation.28 | custom fusion | flops 1572864 | bytes 5244930 | tf_op jit(solution)/shard_map/scatter | solution.py:17
  49.0 37.9 %all-to-all-done = bf16[64,8,2048]{2,1,0:T(8,128)(2,1)} async-done(((bf16[64,8,2048]{2,1,0:T(8,128)(2,1)}), bf16[64,8,2048]{2,1,0:T(8,128)(2,1)}, u32[]{:S(2)}, u32[]{:S(2)}) %all-to-all-start) | async-done | bytes 2097184 | tf_op jit(solution)/shard_map/all_to_all | solution.py:63
  86.8 6.0 %all-to-all-start.2 = ((bf16[64,8,2048]{2,1,0:T(8,128)(2,1)}), bf16[64,8,2048]{2,1,0:T(8,128)(2,1)}, u32[]{:S(2)}, u32[]{:S(2)}) async-start(bf16[64,8,2048]{2,1,0:T(8,128)(2,1)} %bitcast.84), calls=%async_computation.2 | async-start | bytes 4194304 | tf_op jit(solution)/shard_map/all_to_all | solution.py:91
  92.8 0.2 reduce-scatter.3.cloned.1.call-start
  93.1 5.5 %fusion.6 = f32[512,768]{1,0:T(8,128)} fusion(bf16[1,2048,768]{2,1,0:T(8,128)(2,1)} %param.12, bf16[64,8,2048]{2,1,0:T(8,128)(2,1)} %all-to-all-done), kind=kOutput, calls=%fused_computation.13 | convolution fusion | flops 1610612736 | bytes 6815744 | tf_op jit(solution)/shard_map/dot_general | solution.py:23
  98.5 45.5 %all-to-all-done.2 = bf16[64,8,2048]{2,1,0:T(8,128)(2,1)} async-done(((bf16[64,8,2048]{2,1,0:T(8,128)(2,1)}), bf16[64,8,2048]{2,1,0:T(8,128)(2,1)}, u32[]{:S(2)}, u32[]{:S(2)}) %all-to-all-start.2) | async-done | bytes 2097184 | tf_op jit(solution)/shard_map/all_to_all | solution.py:91
  144.0 0.0 copy-start.6
  144.0 4.5 %fusion = f32[512,768]{1,0:T(8,128)S(1)} fusion(bf16[1,768,2048]{2,1,0:T(8,128)(2,1)} %param.13, bf16[64,8,2048]{2,1,0:T(8,128)(2,1)} %all-to-all-done.2), kind=kOutput, calls=%fused_computation.7 | convolution fusion | flops 1610612736 | bytes 6815744 | tf_op jit(solution)/shard_map/dot_general | solution.py:30
  148.5 0.0 copy-done
  148.5 0.0 copy-done.6
  148.5 4.8 %multiply_convert_fusion.3 = (bf16[512,768]{1,0:T(8,128)(2,1)S(1)}, bf16[512,768]{1,0:T(8,128)(2,1)}, bf16[512,768]{1,0:T(8,128)(2,1)S(1)}) fusion(f32[512,768]{1,0:T(8,128)S(1)} %fusion, f32[512,768]{1,0:T(8,128)S(1)} %copy-done.6, bf16[1,2048,768]{2,1,0:T(8,128)(2,1)S(1)} %copy-done, bf16[64,8,2048]{2,1,0:T(8,128)(2,1)} %all-to-all-done), kind=kOutput, calls=%fused_computation.33 | convolution fusion | flops 1616904192 | bytes 10747904 | tf_op jit(solution)/shard_map/dot_general | solution.py:22
  153.3 0.0 copy-start.3
  153.3 0.0 copy-start.5
  153.3 0.9 copy-done.3
  154.2 0.3 copy-done.5
  154.5 7.1 %convolution_convert_fusion = bf16[2048,1536]{1,0:T(8,128)(2,1)} fusion(bf16[64,8,2048]{2,1,0:T(8,128)(2,1)} %all-to-all-done, bf16[512,768]{1,0:T(8,128)(2,1)S(1)} %get-tuple-element.7, bf16[512,768]{1,0:T(8,128)(2,1)S(1)} %get-tuple-element.5), kind=kOutput, calls=%fused_computation.4 | convolution fusion | flops 3227516928 | bytes 9961472 | tf_op jit(solution)/shard_map/dot_general | solution.py:44
  161.6 0.0 reduce-scatter.3.cloned.1.call-update
  161.6 5.2 %fusion.17 = bf16[64,8,2048]{2,1,0:T(8,128)(2,1)} fusion(bf16[512,768]{1,0:T(8,128)(2,1)} %get-tuple-element.6, bf16[1,768,2048]{2,1,0:T(8,128)(2,1)} %param.13), kind=kOutput, calls=%fused_computation.21 | convolution fusion | flops 1611661312 | bytes 6029312 | tf_op jit(solution)/shard_map/dot_general | solution.py:67
  166.9 6.0 %all-to-all-start.1 = ((bf16[64,8,2048]{2,1,0:T(8,128)(2,1)}), bf16[64,8,2048]{2,1,0:T(8,128)(2,1)}, u32[]{:S(2)}, u32[]{:S(2)}) async-start(bf16[64,8,2048]{2,1,0:T(8,128)(2,1)} %fusion.17), calls=%async_computation.1 | async-start | bytes 4194304 | tf_op jit(solution)/shard_map/all_to_all | solution.py:70
  172.9 0.3 reduce-scatter.5.cloned.1.call-start
  173.1 5.4 %convolution_convert_fusion.1 = bf16[768,2048]{1,0:T(8,128)(2,1)} fusion(bf16[512,768]{1,0:T(8,128)(2,1)} %get-tuple-element.6, bf16[64,8,2048]{2,1,0:T(8,128)(2,1)} %all-to-all-done.2), kind=kOutput, calls=%fused_computation.6 | convolution fusion | flops 1612185600 | bytes 6029312 | tf_op jit(solution)/shard_map/dot_general | solution.py:44
  178.5 0.0 reduce-scatter.5.cloned.1.call-update
  178.5 0.0 copy-start.4
  178.5 4.0 %fusion.4 = f32[512,2048]{1,0:T(8,128)S(1)} fusion(bf16[512,768]{1,0:T(8,128)(2,1)} %copy-done.5, bf16[1,2048,768]{2,1,0:T(8,128)(2,1)} %param.12), kind=kOutput, calls=%fused_computation.11 | convolution fusion | flops 1610612736 | bytes 8126464 | tf_op jit(solution)/shard_map/dot_general | solution.py:37
  182.6 0.0 copy-done.4
  182.6 3.3 %fusion.20 = bf16[64,8,2048]{2,1,0:T(8,128)(2,1)} fusion(f32[512,2048]{1,0:T(8,128)S(1)} %fusion.4, bf16[512,768]{1,0:T(8,128)(2,1)S(1)} %copy-done.4, bf16[1,2048,768]{2,1,0:T(8,128)(2,1)S(1)} %copy-done), kind=kOutput, calls=%fused_computation.22 | convolution fusion | flops 1612709888 | bytes 10223616 | tf_op jit(solution)/shard_map/dot_general | solution.py:36
  185.8 38.2 %all-to-all-done.1 = bf16[64,8,2048]{2,1,0:T(8,128)(2,1)} async-done(((bf16[64,8,2048]{2,1,0:T(8,128)(2,1)}), bf16[64,8,2048]{2,1,0:T(8,128)(2,1)}, u32[]{:S(2)}, u32[]{:S(2)}) %all-to-all-start.1) | async-done | bytes 2097184 | tf_op jit(solution)/shard_map/all_to_all | solution.py:70
  224.0 6.0 %all-to-all-start.3 = ((bf16[64,8,2048]{2,1,0:T(8,128)(2,1)}), bf16[64,8,2048]{2,1,0:T(8,128)(2,1)}, u32[]{:S(2)}, u32[]{:S(2)}) async-start(bf16[64,8,2048]{2,1,0:T(8,128)(2,1)} %fusion.20), calls=%async_computation.3 | async-start | bytes 4194304 | tf_op jit(solution)/shard_map/all_to_all | solution.py:97
  230.1 0.1 copy.17
  230.2 6.9 %gather_fusion = bf16[384,2048]{1,0:T(8,128)(2,1)} fusion(bf16[512,2048]{1,0:T(8,128)(2,1)} %bitcast.7, s32[1024]{0:T(1024)S(1)} %pad_clamp_fusion), kind=kCustom, calls=%fused_computation | custom fusion | bytes 3147264 | tf_op jit(solution)/shard_map/gather | solution.py:85
  237.1 3.7 %reshape.103 = bf16[64,6,2048]{2,1,0:T(8,128)(2,1)} reshape(bf16[384,2048]{1,0:T(8,128)(2,1)} %gather_fusion) | data formatting | bytes 3145728 | tf_op jit(solution)/shard_map/reshape | solution.py:85
  240.8 2.3 fusion.42
  243.1 0.9 copy.22
  244.0 37.2 %all-to-all-done.3 = bf16[64,8,2048]{2,1,0:T(8,128)(2,1)} async-done(((bf16[64,8,2048]{2,1,0:T(8,128)(2,1)}), bf16[64,8,2048]{2,1,0:T(8,128)(2,1)}, u32[]{:S(2)}, u32[]{:S(2)}) %all-to-all-start.3) | async-done | bytes 2097184 | tf_op jit(solution)/shard_map/all_to_all | solution.py:97
  281.2 6.9 %gather_fusion.1 = bf16[384,2048]{1,0:T(8,128)(2,1)} fusion(bf16[512,2048]{1,0:T(8,128)(2,1)} %bitcast.13, s32[1024]{0:T(1024)S(1)} %pad_clamp_fusion), kind=kCustom, calls=%fused_computation.1 | custom fusion | bytes 3147264 | tf_op jit(solution)/shard_map/gather | solution.py:106
  288.1 3.7 %reshape.108 = bf16[64,6,2048]{2,1,0:T(8,128)(2,1)} reshape(bf16[384,2048]{1,0:T(8,128)(2,1)} %gather_fusion.1) | data formatting | bytes 3145728 | tf_op jit(solution)/shard_map/reshape | solution.py:106
  291.8 3.6 %reduce_sum.25 = bf16[64,2048]{1,0:T(8,128)(2,1)} reduce(bf16[64,6,2048]{2,1,0:T(8,128)(2,1)} %reshape.108, bf16[]{:T(256)} %constant.5.clone.1), dimensions={1}, to_apply=%region_5.6 | reduce | flops 655360 | bytes 1835010 | tf_op jit(solution)/shard_map/reduce_sum | solution.py:105
  295.4 0.0 reduce-scatter.3.cloned.1.call-done
  295.4 2.6 slice_bitcast_fusion
  298.1 0.0 reduce-scatter.5.cloned.1.call-done
  (4 shorter events, 0.1 us)
Async XLA Ops:
  7.2 141.3 %copy-start = (bf16[1,2048,768]{2,1,0:T(8,128)(2,1)S(1)}, bf16[1,2048,768]{2,1,0:T(8,128)(2,1)}, u32[]{:S(2)}) copy-start(bf16[1,2048,768]{2,1,0:T(8,128)(2,1)} %param.11) | copy-start | bytes 9437188
  22.3 13.3 %copy-start.2 = (f32[64,6]{0,1:T(8,128)S(1)}, f32[64,6]{0,1:T(8,128)}, u32[]{:S(2)}) copy-start(f32[64,6]{0,1:T(8,128)} %param.9) | copy-start | bytes 4612
  22.3 13.6 %copy-start.1 = (bf16[64,2048]{1,0:T(8,128)(2,1)S(1)}, bf16[64,2048]{1,0:T(8,128)(2,1)}, u32[]{:S(2)}) copy-start(bf16[64,2048]{1,0:T(8,128)(2,1)} %param.10) | copy-start | bytes 786436
  22.3 64.5 %all-to-all-start = ((bf16[64,8,2048]{2,1,0:T(8,128)(2,1)}), bf16[64,8,2048]{2,1,0:T(8,128)(2,1)}, u32[]{:S(2)}, u32[]{:S(2)}) async-start(bf16[64,8,2048]{2,1,0:T(8,128)(2,1)} %bitcast.85), calls=%async_computation | async-start | bytes 4194304 | tf_op jit(solution)/shard_map/all_to_all | solution.py:63
  86.8 57.2 %all-to-all-start.2 = ((bf16[64,8,2048]{2,1,0:T(8,128)(2,1)}), bf16[64,8,2048]{2,1,0:T(8,128)(2,1)}, u32[]{:S(2)}, u32[]{:S(2)}) async-start(bf16[64,8,2048]{2,1,0:T(8,128)(2,1)} %bitcast.84), calls=%async_computation.2 | async-start | bytes 4194304 | tf_op jit(solution)/shard_map/all_to_all | solution.py:91
  92.8 202.6 %reduce-scatter.3.cloned.1.call-start = ((), (), s32[]{:S(2)}) async-start(), calls=%async_computation.6 | async-start | bytes 7864320 | tf_op jit(solution)/shard_map/reduce_scatter | solution.py:110
  144.0 4.5 %copy-start.6 = (f32[512,768]{1,0:T(8,128)S(1)}, f32[512,768]{1,0:T(8,128)}, u32[]{:S(2)}) copy-start(f32[512,768]{1,0:T(8,128)} %fusion.6) | copy-start | bytes 4718596
  153.3 0.9 copy-start.3
  153.3 1.1 copy-start.5
  166.9 57.2 %all-to-all-start.1 = ((bf16[64,8,2048]{2,1,0:T(8,128)(2,1)}), bf16[64,8,2048]{2,1,0:T(8,128)(2,1)}, u32[]{:S(2)}, u32[]{:S(2)}) async-start(bf16[64,8,2048]{2,1,0:T(8,128)(2,1)} %fusion.17), calls=%async_computation.1 | async-start | bytes 4194304 | tf_op jit(solution)/shard_map/all_to_all | solution.py:70
  172.9 125.2 %reduce-scatter.5.cloned.1.call-start = ((), (), s32[]{:S(2)}) async-start(), calls=%async_computation.7 | async-start | bytes 3932160 | tf_op jit(solution)/shard_map/reduce_scatter | solution.py:116
  178.5 4.0 %copy-start.4 = (bf16[512,768]{1,0:T(8,128)(2,1)S(1)}, bf16[512,768]{1,0:T(8,128)(2,1)}, u32[]{:S(2)}) copy-start(bf16[512,768]{1,0:T(8,128)(2,1)} %copy-done.3) | copy-start | bytes 2359300
  224.0 57.2 %all-to-all-start.3 = ((bf16[64,8,2048]{2,1,0:T(8,128)(2,1)}), bf16[64,8,2048]{2,1,0:T(8,128)(2,1)}, u32[]{:S(2)}, u32[]{:S(2)}) async-start(bf16[64,8,2048]{2,1,0:T(8,128)(2,1)} %fusion.20), calls=%async_computation.3 | async-start | bytes 4194304 | tf_op jit(solution)/shard_map/all_to_all | solution.py:97
Sparse Core Ops, SparseCore 0:
  161.7 63.1 reduce-scatter.2
  228.1 40.5 reduce-scatter.4
where the time goes:
time: 306 us; the launch traced here: 305 us
  waiting for transfers between devices  159 us (52%)
  local copies, waits for them, and re-layouts  46.6 us (15%)
  matrix products  42.1 us (14%)
  starting transfers between devices  31.8 us (10%)
  between operations  14.2 us (5%)
  other arithmetic  11.4 us (4%)
    all_to_all x1, waiting for transfers between devices, per_device(): lax.all_to_all(grad_out, 'expert', split_axis=0, concat_axis=0, tiled=True)  45.5 us
    all_to_all x1, waiting for transfers between devices, per_device(): lax.all_to_all(result.reshape(experts, length, features), 'expert', split...  38.2 us
    all_to_all x1, waiting for transfers between devices, per_device(): lax.all_to_all(outgoing, 'expert', split_axis=0, concat_axis=0, tiled=True)  37.9 us
    all_to_all x1, waiting for transfers between devices, per_device(): lax.all_to_all(back_rows.reshape(experts, capacity, features), 'expert',...  37.2 us
    all_to_all x1, starting transfers between devices, per_device(): lax.all_to_all(outgoing, 'expert', split_axis=0, concat_axis=0, tiled=True)  13.3 us
    dot_general x2, matrix products, outer_sum(): lax.dot_general(left, right, (((0,), (0,)), ((), ())), preferred_element_...  12.5 us
    mul x3, local copies, waits for them, and re-layouts, per_device(): gate_probs[:, :, None] * out_cot[:, None, :].astype(jnp.float32)  7.34 us
    gather x1, local copies, waits for them, and re-layouts, per_device(): returned_grad[positions].reshape(tok_rows, top_count, features)  6.94 us
  transfers between devices with their start and end apart: 6, of which 4 were waited for; matrix products, arithmetic and copies ran while one was open for 22% of the time, Pallas kernels for 0%

commit v1 on v0

--- a/solution.py
+++ b/solution.py
@@ -10,12 +10,6 @@
     before = jnp.cumsum(one_hot, axis=0) - one_hot
     slot_rank = jnp.sum(before * one_hot, axis=1)
     return flat_ids * capacity + slot_rank
-
-
-def place(token_rows, positions, total_rows):
-    return (
-        jnp.zeros((total_rows, token_rows.shape[1]), token_rows.dtype).at[positions].set(token_rows)
-    )
 
 
 def hidden_rows(token_rows, gate_weight, up_weight):
@@ -46,6 +40,10 @@
     )
 
 
+def exchange(blocks):
+    return lax.all_to_all(blocks, "expert", split_axis=0, concat_axis=0, tiled=True)
+
+
 def per_device(tokens, route_ids, gate_probs, out_cot, w_gate, w_up, w_down):
     experts = lax.axis_size("expert")
     tok_rows, features = tokens.shape
@@ -57,58 +55,38 @@
     gate_weight = w_gate[0]
     up_weight = w_up[0]
     down_weight = w_down[0]
-    outgoing = place(jnp.repeat(tokens, top_count, axis=0), positions, total_rows).reshape(
-        experts, capacity, features
-    )
-    slot_rows = lax.all_to_all(outgoing, "expert", split_axis=0, concat_axis=0, tiled=True)
-    length = slot_rows.shape[1]
-    flat_rows = slot_rows.reshape(-1, features)
-    pre_gate, pre_up, expert_activation = hidden_rows(flat_rows, gate_weight, up_weight)
-    result = jnp.dot(expert_activation, down_weight, preferred_element_type=jnp.float32).astype(
+    pick = (positions[:, None] == jnp.arange(total_rows, dtype=positions.dtype)[None, :]).astype(
         jnp.bfloat16
     )
-    returned = lax.all_to_all(
-        result.reshape(experts, length, features), "expert", split_axis=0, concat_axis=0, tiled=True
+    pick3 = pick.reshape(tok_rows, top_count, total_rows)
+    owner = jnp.sum(pick3, axis=1)
+    outgoing = jnp.dot(owner.T, tokens, preferred_element_type=jnp.float32).astype(jnp.bfloat16)
+    slot_rows = exchange(outgoing.reshape(experts, capacity, features)).reshape(-1, features)
+    scaled = (gate_probs[:, :, None] * out_cot[:, None, :].astype(jnp.float32)).astype(jnp.bfloat16)
+    grad_out = jnp.dot(
+        pick.T, scaled.reshape(-1, features), preferred_element_type=jnp.float32
+    ).astype(jnp.bfloat16)
+    grads_in = exchange(grad_out.reshape(experts, capacity, features)).reshape(-1, features)
+
+    pre_gate, pre_up, activation = hidden_rows(slot_rows, gate_weight, up_weight)
+    result = jnp.dot(activation, down_weight, preferred_element_type=jnp.float32).astype(
+        jnp.bfloat16
     )
-    results = (
-        returned,
-        slot_rows,
-        pre_gate.reshape(experts, length, hidden),
-        pre_up.reshape(experts, length, hidden),
-        expert_activation.reshape(experts, length, hidden),
-    )
-    returned = results[0].reshape(-1, features)
-    received = results[1].reshape(-1, features)
-    pre_gate = results[2].reshape(-1, hidden)
-    pre_up = results[3].reshape(-1, hidden)
-    activation = results[4].reshape(-1, hidden)
-    picked = returned[positions].reshape(tok_rows, top_count, features)
-    combined = jnp.einsum("tk,tkd->td", gate_probs, picked.astype(jnp.float32)).astype(jnp.bfloat16)
-    scaled = (gate_probs[:, :, None] * out_cot[:, None, :].astype(jnp.float32)).astype(jnp.bfloat16)
-    grad_out = place(scaled.reshape(-1, features), positions, total_rows).reshape(
-        experts, capacity, features
-    )
-    grads_in = lax.all_to_all(grad_out, "expert", split_axis=0, concat_axis=0, tiled=True).reshape(
-        -1, features
-    )
+    returned = exchange(result.reshape(experts, capacity, features)).reshape(-1, features)
     back_rows, d_gate, d_up = backward_rows(
         grads_in, pre_gate, pre_up, gate_weight, up_weight, down_weight
     )
-    returned_grad = lax.all_to_all(
-        back_rows.reshape(experts, capacity, features),
-        "expert",
-        split_axis=0,
-        concat_axis=0,
-        tiled=True,
+    returned_grad = exchange(back_rows.reshape(experts, capacity, features)).reshape(-1, features)
+
+    picked = jnp.einsum("tkp,pd->tkd", pick3, returned, preferred_element_type=jnp.float32)
+    combined = jnp.einsum("tk,tkd->td", gate_probs, picked).astype(jnp.bfloat16)
+    grad_tokens = jnp.dot(owner, returned_grad, preferred_element_type=jnp.float32).astype(
+        jnp.bfloat16
     )
-    returned_grad = returned_grad.reshape(-1, features)
-    grad_tokens = jnp.sum(
-        returned_grad[positions].reshape(tok_rows, top_count, features).astype(jnp.float32), axis=1
-    )
-    grad_tokens = grad_tokens.astype(jnp.bfloat16)
+
     gate_up_grad = jnp.concatenate([d_gate, d_up], axis=1)
     gate_up_sum = lax.psum_scatter(
-        outer_sum(received, gate_up_grad).astype(jnp.bfloat16),
+        outer_sum(slot_rows, gate_up_grad).astype(jnp.bfloat16),
         "replica",
         scatter_dimension=0,
         tiled=True,

time: 306 us -> 286 us (0.935)
  local copies, waits for them, and re-layouts: 46.6 us -> 13.8 us
  matrix products: 42.1 us -> 54 us
  waiting for transfers between devices: 159 us -> 169 us
  other arithmetic: 11.4 us -> 1.93 us
    gather x2 -> x0, local copies, waits for them, and re-layouts: 13.9 us -> none  [the longest x1 6.94 us: per_device(): returned_grad[positions].reshape(tok_rows, top_count, features)]
    dot_general x2 -> x6, matrix products: 7.53 us -> 19.6 us  [the longest x1 5.25 us: per_device(): jnp.dot(activation, down_weight, preferred_element_type=jnp.float32)]
    reshape x3 -> x0, local copies, waits for them, and re-layouts: 11.1 us -> none  [the longest x1 3.72 us: per_device(): picked = returned[positions].reshape(tok_rows, top_count, features)]
    all_to_all x4, waiting for transfers between devices: 159 us -> 169 us  [exchange(): lax.all_to_all(blocks, 'expert', split_axis=0, concat_axis=0, tiled=True)]
    scatter x1 -> x0, other arithmetic: 5.84 us -> none  [place(): jnp.zeros((total_rows, token_rows.shape[1]), token_rows.dtype).at[positions]]
    scatter x1 -> x0, local copies, waits for them, and re-layouts: 5.26 us -> none  [place(): jnp.zeros((total_rows, token_rows.shape[1]), token_rows.dtype).at[positions]]
    reduce_sum x1, other arithmetic: 3.64 us -> 0.14 us  [per_device(): owner = jnp.sum(pick3, axis=1)]
  transfers between devices with their start and end apart: 6 -> 6, of which waited for: 4 -> 4; matrix products, arithmetic and copies ran while one was open for 22% -> 16% of each run, Pallas kernels for 0% -> 0%
where the time goes in v1:
time: 286 us; the launch traced here: 285 us
  waiting for transfers between devices  169 us (59%)
  matrix products  54 us (19%)
  starting transfers between devices  31.8 us (11%)
  between operations  14.2 us (5%)
  local copies, waits for them, and re-layouts  13.8 us (5%)
    all_to_all x4, waiting for transfers between devices, exchange(): lax.all_to_all(blocks, 'expert', split_axis=0, concat_axis=0, tiled=True)  169 us
    all_to_all x4, starting transfers between devices, exchange(): lax.all_to_all(blocks, 'expert', split_axis=0, concat_axis=0, tiled=True)  31.3 us
    dot_general x2, matrix products, outer_sum(): lax.dot_general(left, right, (((0,), (0,)), ((), ())), preferred_element_...  12.5 us
    mul x3, local copies, waits for them, and re-layouts, per_device(): gate_probs[:, :, None] * out_cot[:, None, :].astype(jnp.float32)  7.34 us
  transfers between devices with their start and end apart: 6, of which 4 were waited for; matrix products, arithmetic and copies ran while one was open for 16% of the time, Pallas kernels for 0%

profile of v1, /device:TPU:1, one launch (start us, length us, event | category | flops | bytes accessed | tf_op | source)
XLA Modules:
  0.0 284.9 jit_solution(10542710008946446603)
XLA Ops:
  7.2 0.0 copy-start
  7.2 0.9 copy.29
  8.1 0.1 eq.67
  8.2 0.1 eq.71
  8.4 0.9 reduce-window.6
  9.3 0.2 slice_reduce_fusion
  9.6 0.1 fusion.47
  9.7 0.1 reduce_sum.24
  9.8 0.1 copy.32
  9.9 0.7 multiply_add_fusion
  10.6 0.1 fusion.42
  10.8 3.0 %fusion.19 = bf16[64,8,2048]{2,1,0:T(8,128)(2,1)} fusion(bf16[64,512]{1,0:T(8,128)(2,1)S(1)} %fusion.42, bf16[64,2048]{1,0:T(8,128)(2,1)} %param.7), kind=kOutput, calls=%fused_computation.21 | convolution fusion | flops 135266304 | bytes 2424832 | tf_op jit(solution)/shard_map/dot_general | solution.py:63
  13.8 0.0 copy-start.2
  13.8 0.0 copy-start.1
  13.8 13.3 %all-to-all-start = ((bf16[64,8,2048]{2,1,0:T(8,128)(2,1)}), bf16[64,8,2048]{2,1,0:T(8,128)(2,1)}, u32[]{:S(2)}, u32[]{:S(2)}) async-start(bf16[64,8,2048]{2,1,0:T(8,128)(2,1)} %fusion.19), calls=%async_computation | async-start | bytes 4194304 | tf_op jit(solution)/shard_map/all_to_all | solution.py:44
  27.1 0.0 copy-done.2
  27.1 0.1 copy.33
  27.2 0.1 mul.68
  27.3 0.0 copy-done.1
  27.3 2.4 mul.70
  29.8 4.8 %mul.71 = f32[384,2048]{1,0:T(8,128)} reshape(f32[64,6,2048]{2,1,0:T(8,128)} %mul.70) | data formatting | bytes 6291456 | tf_op jit(solution)/shard_map/mul | solution.py:65
  34.5 4.6 %fusion.20 = bf16[64,8,2048]{2,1,0:T(8,128)(2,1)} fusion(f32[384,2048]{1,0:T(8,128)} %mul.71, f32[384]{0:T(512)S(1)} %mul.68, s32[384]{0:T(512)S(1)} %multiply_add_fusion.1), kind=kOutput, calls=%fused_computation.22 | convolution fusion | flops 808124416 | bytes 5245952 | tf_op jit(solution)/shard_map/dot_general | solution.py:66
  39.2 39.1 %all-to-all-done = bf16[64,8,2048]{2,1,0:T(8,128)(2,1)} async-done(((bf16[64,8,2048]{2,1,0:T(8,128)(2,1)}), bf16[64,8,2048]{2,1,0:T(8,128)(2,1)}, u32[]{:S(2)}, u32[]{:S(2)}) %all-to-all-start) | async-done | bytes 2097184 | tf_op jit(solution)/shard_map/all_to_all | solution.py:44
  78.2 6.0 %all-to-all-start.2 = ((bf16[64,8,2048]{2,1,0:T(8,128)(2,1)}), bf16[64,8,2048]{2,1,0:T(8,128)(2,1)}, u32[]{:S(2)}, u32[]{:S(2)}) async-start(bf16[64,8,2048]{2,1,0:T(8,128)(2,1)} %fusion.20), calls=%async_computation.2 | async-start | bytes 4194304 | tf_op jit(solution)/shard_map/all_to_all | solution.py:44
  84.3 0.2 reduce-scatter.3.cloned.1.call-start
  84.5 5.5 %fusion.8 = f32[512,768]{1,0:T(8,128)} fusion(bf16[1,2048,768]{2,1,0:T(8,128)(2,1)} %param.12, bf16[64,8,2048]{2,1,0:T(8,128)(2,1)} %all-to-all-done), kind=kOutput, calls=%fused_computation.11 | convolution fusion | flops 1610612736 | bytes 6815744 | tf_op jit(solution)/shard_map/dot_general | solution.py:17
  90.0 45.5 %all-to-all-done.2 = bf16[64,8,2048]{2,1,0:T(8,128)(2,1)} async-done(((bf16[64,8,2048]{2,1,0:T(8,128)(2,1)}), bf16[64,8,2048]{2,1,0:T(8,128)(2,1)}, u32[]{:S(2)}, u32[]{:S(2)}) %all-to-all-start.2) | async-done | bytes 2097184 | tf_op jit(solution)/shard_map/all_to_all | solution.py:44
  135.4 0.0 copy-start.6
  135.4 4.5 %fusion.2 = f32[512,768]{1,0:T(8,128)S(1)} fusion(bf16[1,768,2048]{2,1,0:T(8,128)(2,1)} %param.13, bf16[64,8,2048]{2,1,0:T(8,128)(2,1)} %all-to-all-done.2), kind=kOutput, calls=%fused_computation.5 | convolution fusion | flops 1610612736 | bytes 6815744 | tf_op jit(solution)/shard_map/dot_general | solution.py:24
  139.9 0.0 copy-done
  139.9 0.0 copy-done.6
  139.9 4.8 %multiply_convert_fusion.3 = (bf16[512,768]{1,0:T(8,128)(2,1)S(1)}, bf16[512,768]{1,0:T(8,128)(2,1)}, bf16[512,768]{1,0:T(8,128)(2,1)S(1)}) fusion(f32[512,768]{1,0:T(8,128)S(1)} %fusion.2, f32[512,768]{1,0:T(8,128)S(1)} %copy-done.6, bf16[1,2048,768]{2,1,0:T(8,128)(2,1)S(1)} %copy-done, bf16[64,8,2048]{2,1,0:T(8,128)(2,1)} %all-to-all-done), kind=kOutput, calls=%fused_computation.38 | convolution fusion | flops 1616904192 | bytes 10747904 | tf_op jit(solution)/shard_map/dot_general | solution.py:16
  144.8 0.0 copy-start.3
  144.8 0.0 copy-start.5
  144.8 0.9 copy-done.3
  145.6 0.3 copy-done.5
  145.9 7.1 %convolution_convert_fusion = bf16[2048,1536]{1,0:T(8,128)(2,1)} fusion(bf16[64,8,2048]{2,1,0:T(8,128)(2,1)} %all-to-all-done, bf16[512,768]{1,0:T(8,128)(2,1)S(1)} %get-tuple-element.7, bf16[512,768]{1,0:T(8,128)(2,1)S(1)} %get-tuple-element.5), kind=kOutput, calls=%fused_computation | convolution fusion | flops 3227516928 | bytes 9961472 | tf_op jit(solution)/shard_map/dot_general | solution.py:38
  153.0 0.0 reduce-scatter.3.cloned.1.call-update
  153.0 5.3 %fusion.21 = bf16[64,8,2048]{2,1,0:T(8,128)(2,1)} fusion(bf16[512,768]{1,0:T(8,128)(2,1)} %get-tuple-element.6, bf16[1,768,2048]{2,1,0:T(8,128)(2,1)} %param.13), kind=kOutput, calls=%fused_computation.23 | convolution fusion | flops 1611661312 | bytes 6029312 | tf_op jit(solution)/shard_map/dot_general | solution.py:72
  158.3 6.0 %all-to-all-start.1 = ((bf16[64,8,2048]{2,1,0:T(8,128)(2,1)}), bf16[64,8,2048]{2,1,0:T(8,128)(2,1)}, u32[]{:S(2)}, u32[]{:S(2)}) async-start(bf16[64,8,2048]{2,1,0:T(8,128)(2,1)} %fusion.21), calls=%async_computation.1 | async-start | bytes 4194304 | tf_op jit(solution)/shard_map/all_to_all | solution.py:44
  164.3 0.3 reduce-scatter.5.cloned.1.call-start
  164.6 5.4 %convolution_convert_fusion.1 = bf16[768,2048]{1,0:T(8,128)(2,1)} fusion(bf16[512,768]{1,0:T(8,128)(2,1)} %get-tuple-element.6, bf16[64,8,2048]{2,1,0:T(8,128)(2,1)} %all-to-all-done.2), kind=kOutput, calls=%fused_computation.4 | convolution fusion | flops 1612185600 | bytes 6029312 | tf_op jit(solution)/shard_map/dot_general | solution.py:38
  169.9 0.0 reduce-scatter.5.cloned.1.call-update
  170.0 0.0 copy-start.4
  170.0 4.0 %fusion.6 = f32[512,2048]{1,0:T(8,128)S(1)} fusion(bf16[512,768]{1,0:T(8,128)(2,1)} %copy-done.5, bf16[1,2048,768]{2,1,0:T(8,128)(2,1)} %param.12), kind=kOutput, calls=%fused_computation.9 | convolution fusion | flops 1610612736 | bytes 8126464 | tf_op jit(solution)/shard_map/dot_general | solution.py:31
  174.0 0.0 copy-done.4
  174.0 3.2 %fusion.24 = bf16[64,8,2048]{2,1,0:T(8,128)(2,1)} fusion(f32[512,2048]{1,0:T(8,128)S(1)} %fusion.6, bf16[512,768]{1,0:T(8,128)(2,1)S(1)} %copy-done.4, bf16[1,2048,768]{2,1,0:T(8,128)(2,1)S(1)} %copy-done), kind=kOutput, calls=%fused_computation.24 | convolution fusion | flops 1612709888 | bytes 10223616 | tf_op jit(solution)/shard_map/dot_general | solution.py:30
  177.2 38.3 %all-to-all-done.1 = bf16[64,8,2048]{2,1,0:T(8,128)(2,1)} async-done(((bf16[64,8,2048]{2,1,0:T(8,128)(2,1)}), bf16[64,8,2048]{2,1,0:T(8,128)(2,1)}, u32[]{:S(2)}, u32[]{:S(2)}) %all-to-all-start.1) | async-done | bytes 2097184 | tf_op jit(solution)/shard_map/all_to_all | solution.py:44
  215.4 6.0 %all-to-all-start.3 = ((bf16[64,8,2048]{2,1,0:T(8,128)(2,1)}), bf16[64,8,2048]{2,1,0:T(8,128)(2,1)}, u32[]{:S(2)}, u32[]{:S(2)}) async-start(bf16[64,8,2048]{2,1,0:T(8,128)(2,1)} %fusion.24), calls=%async_computation.3 | async-start | bytes 4194304 | tf_op jit(solution)/shard_map/all_to_all | solution.py:44
  221.5 0.1 copy.35
  221.6 2.6 fusion.27
  224.2 1.3 fusion
  225.6 0.9 copy.42
  226.4 46.2 %all-to-all-done.3 = bf16[64,8,2048]{2,1,0:T(8,128)(2,1)} async-done(((bf16[64,8,2048]{2,1,0:T(8,128)(2,1)}), bf16[64,8,2048]{2,1,0:T(8,128)(2,1)}, u32[]{:S(2)}, u32[]{:S(2)}) %all-to-all-start.3) | async-done | bytes 2097184 | tf_op jit(solution)/shard_map/all_to_all | solution.py:44
  272.6 2.8 convolution_convert_fusion.4
  275.4 0.0 reduce-scatter.3.cloned.1.call-done
  275.4 2.6 slice_bitcast_fusion
  278.0 0.0 reduce-scatter.5.cloned.1.call-done
  (3 shorter events, 0.1 us)
Async XLA Ops:
  7.2 132.7 %copy-start = (bf16[1,2048,768]{2,1,0:T(8,128)(2,1)S(1)}, bf16[1,2048,768]{2,1,0:T(8,128)(2,1)}, u32[]{:S(2)}) copy-start(bf16[1,2048,768]{2,1,0:T(8,128)(2,1)} %param.11) | copy-start | bytes 9437188
  13.8 13.3 %copy-start.2 = (f32[64,6]{0,1:T(8,128)S(1)}, f32[64,6]{0,1:T(8,128)}, u32[]{:S(2)}) copy-start(f32[64,6]{0,1:T(8,128)} %param.9) | copy-start | bytes 4612
  13.8 13.6 %copy-start.1 = (bf16[64,2048]{1,0:T(8,128)(2,1)S(1)}, bf16[64,2048]{1,0:T(8,128)(2,1)}, u32[]{:S(2)}) copy-start(bf16[64,2048]{1,0:T(8,128)(2,1)} %param.10) | copy-start | bytes 786436
  13.8 64.5 %all-to-all-start = ((bf16[64,8,2048]{2,1,0:T(8,128)(2,1)}), bf16[64,8,2048]{2,1,0:T(8,128)(2,1)}, u32[]{:S(2)}, u32[]{:S(2)}) async-start(bf16[64,8,2048]{2,1,0:T(8,128)(2,1)} %fusion.19), calls=%async_computation | async-start | bytes 4194304 | tf_op jit(solution)/shard_map/all_to_all | solution.py:44
  78.2 57.2 %all-to-all-start.2 = ((bf16[64,8,2048]{2,1,0:T(8,128)(2,1)}), bf16[64,8,2048]{2,1,0:T(8,128)(2,1)}, u32[]{:S(2)}, u32[]{:S(2)}) async-start(bf16[64,8,2048]{2,1,0:T(8,128)(2,1)} %fusion.20), calls=%async_computation.2 | async-start | bytes 4194304 | tf_op jit(solution)/shard_map/all_to_all | solution.py:44
  84.3 191.1 %reduce-scatter.3.cloned.1.call-start = ((), (), s32[]{:S(2)}) async-start(), calls=%async_computation.6 | async-start | bytes 7864320 | tf_op jit(solution)/shard_map/reduce_scatter | solution.py:88
  135.4 4.5 %copy-start.6 = (f32[512,768]{1,0:T(8,128)S(1)}, f32[512,768]{1,0:T(8,128)}, u32[]{:S(2)}) copy-start(f32[512,768]{1,0:T(8,128)} %fusion.8) | copy-start | bytes 4718596
  144.8 0.9 copy-start.3
  144.8 1.1 copy-start.5
  158.3 57.2 %all-to-all-start.1 = ((bf16[64,8,2048]{2,1,0:T(8,128)(2,1)}), bf16[64,8,2048]{2,1,0:T(8,128)(2,1)}, u32[]{:S(2)}, u32[]{:S(2)}) async-start(bf16[64,8,2048]{2,1,0:T(8,128)(2,1)} %fusion.21), calls=%async_computation.1 | async-start | bytes 4194304 | tf_op jit(solution)/shard_map/all_to_all | solution.py:44
  164.3 113.7 %reduce-scatter.5.cloned.1.call-start = ((), (), s32[]{:S(2)}) async-start(), calls=%async_computation.7 | async-start | bytes 3932160 | tf_op jit(solution)/shard_map/reduce_scatter | solution.py:94
  170.0 4.0 %copy-start.4 = (bf16[512,768]{1,0:T(8,128)(2,1)S(1)}, bf16[512,768]{1,0:T(8,128)(2,1)}, u32[]{:S(2)}) copy-start(bf16[512,768]{1,0:T(8,128)(2,1)} %copy-done.3) | copy-start | bytes 2359300
  215.4 57.2 %all-to-all-start.3 = ((bf16[64,8,2048]{2,1,0:T(8,128)(2,1)}), bf16[64,8,2048]{2,1,0:T(8,128)(2,1)}, u32[]{:S(2)}, u32[]{:S(2)}) async-start(bf16[64,8,2048]{2,1,0:T(8,128)(2,1)} %fusion.24), calls=%async_computation.3 | async-start | bytes 4194304 | tf_op jit(solution)/shard_map/all_to_all | solution.py:44
Sparse Core Ops, SparseCore 0:
  153.1 63.1 reduce-scatter.2
  219.5 40.5 reduce-scatter.4

commit v2 on v1

--- a/solution.py
+++ b/solution.py
@@ -72,6 +72,9 @@
     result = jnp.dot(activation, down_weight, preferred_element_type=jnp.float32).astype(
         jnp.bfloat16
     )
+    pre_gate, pre_up, activation, result = lax.optimization_barrier(
+        (pre_gate, pre_up, activation, result)
+    )
     returned = exchange(result.reshape(experts, capacity, features)).reshape(-1, features)
     back_rows, d_gate, d_up = backward_rows(
         grads_in, pre_gate, pre_up, gate_weight, up_weight, down_weight
@@ -83,7 +86,6 @@
     grad_tokens = jnp.dot(owner, returned_grad, preferred_element_type=jnp.float32).astype(
         jnp.bfloat16
     )
-
     gate_up_grad = jnp.concatenate([d_gate, d_up], axis=1)
     gate_up_sum = lax.psum_scatter(
         outer_sum(slot_rows, gate_up_grad).astype(jnp.bfloat16),

time: 286 us -> 276 us (0.965)
  waiting for transfers between devices: 169 us -> 162 us
    all_to_all x4, waiting for transfers between devices: 169 us -> 161 us  [exchange(): lax.all_to_all(blocks, 'expert', split_axis=0, concat_axis=0, tiled=True)]
  transfers between devices with their start and end apart: 6 -> 6, of which waited for: 4 -> 4; matrix products, arithmetic and copies ran while one was open for 16% -> 17% of each run, Pallas kernels for 0% -> 0%
where the time goes in v2:
time: 276 us; the launch traced here: 275 us
  waiting for transfers between devices  162 us (59%)
  matrix products  51.8 us (19%)
  starting transfers between devices  31.8 us (12%)
  between operations  14.3 us (5%)
  local copies, waits for them, and re-layouts  13.8 us (5%)
    all_to_all x4, waiting for transfers between devices, exchange(): lax.all_to_all(blocks, 'expert', split_axis=0, concat_axis=0, tiled=True)  161 us
    all_to_all x4, starting transfers between devices, exchange(): lax.all_to_all(blocks, 'expert', split_axis=0, concat_axis=0, tiled=True)  31.3 us
    dot_general x2, matrix products, outer_sum(): lax.dot_general(left, right, (((0,), (0,)), ((), ())), preferred_element_...  12.5 us
    mul x3, local copies, waits for them, and re-layouts, per_device(): gate_probs[:, :, None] * out_cot[:, None, :].astype(jnp.float32)  7.35 us
  transfers between devices with their start and end apart: 6, of which 4 were waited for; matrix products, arithmetic and copies ran while one was open for 17% of the time, Pallas kernels for 0%

profile of v2, /device:TPU:1, one launch (start us, length us, event | category | flops | bytes accessed | tf_op | source)
XLA Modules:
  0.0 275.1 jit_solution(16454541746022376883)
XLA Ops:
  7.2 0.0 copy-start
  7.2 0.9 copy.29
  8.1 0.1 eq.67
  8.2 0.1 eq.71
  8.4 0.9 reduce-window.6
  9.3 0.2 slice_reduce_fusion
  9.6 0.1 fusion.44
  9.7 0.1 reduce_sum.24
  9.8 0.1 copy.32
  9.9 0.7 multiply_add_fusion
  10.6 0.1 fusion.39
  10.8 3.0 %fusion.19 = bf16[64,8,2048]{2,1,0:T(8,128)(2,1)} fusion(bf16[64,512]{1,0:T(8,128)(2,1)S(1)} %fusion.39, bf16[64,2048]{1,0:T(8,128)(2,1)} %param.7), kind=kOutput, calls=%fused_computation.21 | convolution fusion | flops 135266304 | bytes 2424832 | tf_op jit(solution)/shard_map/dot_general | solution.py:63
  13.8 0.0 copy-start.2
  13.8 0.0 copy-start.1
  13.8 13.3 %all-to-all-start = ((bf16[64,8,2048]{2,1,0:T(8,128)(2,1)}), bf16[64,8,2048]{2,1,0:T(8,128)(2,1)}, u32[]{:S(2)}, u32[]{:S(2)}) async-start(bf16[64,8,2048]{2,1,0:T(8,128)(2,1)} %fusion.19), calls=%async_computation | async-start | bytes 4194304 | tf_op jit(solution)/shard_map/all_to_all | solution.py:44
  27.1 0.0 copy-done.2
  27.1 0.1 copy.33
  27.2 0.1 mul.68
  27.3 0.0 copy-done.1
  27.3 2.5 mul.70
  29.8 4.7 %mul.71 = f32[384,2048]{1,0:T(8,128)} reshape(f32[64,6,2048]{2,1,0:T(8,128)} %mul.70) | data formatting | bytes 6291456 | tf_op jit(solution)/shard_map/mul | solution.py:65
  34.5 4.6 %fusion.20 = bf16[64,8,2048]{2,1,0:T(8,128)(2,1)} fusion(f32[384,2048]{1,0:T(8,128)} %mul.71, f32[384]{0:T(512)S(1)} %mul.68, s32[384]{0:T(512)S(1)} %multiply_add_fusion.1), kind=kOutput, calls=%fused_computation.22 | convolution fusion | flops 808124416 | bytes 5245952 | tf_op jit(solution)/shard_map/dot_general | solution.py:66
  39.2 39.1 %all-to-all-done = bf16[64,8,2048]{2,1,0:T(8,128)(2,1)} async-done(((bf16[64,8,2048]{2,1,0:T(8,128)(2,1)}), bf16[64,8,2048]{2,1,0:T(8,128)(2,1)}, u32[]{:S(2)}, u32[]{:S(2)}) %all-to-all-start) | async-done | bytes 2097184 | tf_op jit(solution)/shard_map/all_to_all | solution.py:44
  78.2 6.0 %all-to-all-start.2 = ((bf16[64,8,2048]{2,1,0:T(8,128)(2,1)}), bf16[64,8,2048]{2,1,0:T(8,128)(2,1)}, u32[]{:S(2)}, u32[]{:S(2)}) async-start(bf16[64,8,2048]{2,1,0:T(8,128)(2,1)} %fusion.20), calls=%async_computation.2 | async-start | bytes 4194304 | tf_op jit(solution)/shard_map/all_to_all | solution.py:44
  84.3 0.2 reduce-scatter.3.cloned.1.call-start
  84.5 0.0 copy-start.3
  84.5 4.5 %fusion.12 = f32[512,768]{1,0:T(8,128)S(1)} fusion(bf16[1,2048,768]{2,1,0:T(8,128)(2,1)} %param.11, bf16[64,8,2048]{2,1,0:T(8,128)(2,1)} %all-to-all-done), kind=kOutput, calls=%fused_computation.15 | convolution fusion | flops 1610612736 | bytes 6815744 | tf_op jit(solution)/shard_map/dot_general | solution.py:16
  89.0 0.0 copy-done.3
  89.0 0.0 copy-start.9
  89.0 5.2 %multiply_convert_fusion.4 = (bf16[512,768]{1,0:T(8,128)(2,1)S(1)}, f32[512,768]{1,0:T(8,128)}) fusion(f32[512,768]{1,0:T(8,128)S(1)} %fusion.12, bf16[1,2048,768]{2,1,0:T(8,128)(2,1)S(1)} %copy-done.3, bf16[64,8,2048]{2,1,0:T(8,128)(2,1)} %all-to-all-done), kind=kOutput, calls=%fused_computation.40 | convolution fusion | flops 1612972032 | bytes 9175040 | tf_op jit(solution)/shard_map/dot_general | solution.py:17
  94.1 0.0 copy-done.9
  94.1 0.0 copy-start.8
  94.1 0.0 copy-done
  94.2 3.3 %fusion.14 = bf16[512,2048]{1,0:T(8,128)(2,1)} fusion(bf16[512,768]{1,0:T(8,128)(2,1)S(1)} %get-tuple-element.12, bf16[1,768,2048]{2,1,0:T(8,128)(2,1)S(1)} %copy-done), kind=kOutput, calls=%fused_computation.18 | convolution fusion | flops 1611661312 | bytes 6029312 | tf_op jit(solution)/shard_map/dot_general | solution.py:72
  97.4 0.0 copy-done.8
  97.4 38.0 %all-to-all-done.2 = bf16[64,8,2048]{2,1,0:T(8,128)(2,1)} async-done(((bf16[64,8,2048]{2,1,0:T(8,128)(2,1)}), bf16[64,8,2048]{2,1,0:T(8,128)(2,1)}, u32[]{:S(2)}, u32[]{:S(2)}) %all-to-all-start.2) | async-done | bytes 2097184 | tf_op jit(solution)/shard_map/all_to_all | solution.py:44
  135.4 4.7 %multiply_convert_fusion.3 = (bf16[512,768]{1,0:T(8,128)(2,1)S(1)}, bf16[512,768]{1,0:T(8,128)(2,1)S(1)}) fusion(f32[512,768]{1,0:T(8,128)} %copy-done.9, f32[512,768]{1,0:T(8,128)} %get-tuple-element.10, bf16[1,768,2048]{2,1,0:T(8,128)(2,1)S(1)} %copy-done, bf16[64,8,2048]{2,1,0:T(8,128)(2,1)} %all-to-all-done.2), kind=kOutput, calls=%fused_computation.37 | convolution fusion | flops 1615724544 | bytes 9961472 | tf_op jit(solution)/shard_map/dot_general | solution.py:24
  140.2 0.0 copy-start.5
  140.2 0.0 copy-start.7
  140.2 0.9 copy-done.5
  141.0 0.3 copy-done.7
  141.3 7.2 %convolution_convert_fusion = bf16[2048,1536]{1,0:T(8,128)(2,1)} fusion(bf16[64,8,2048]{2,1,0:T(8,128)(2,1)} %all-to-all-done, bf16[512,768]{1,0:T(8,128)(2,1)S(1)} %get-tuple-element.14, bf16[512,768]{1,0:T(8,128)(2,1)S(1)} %get-tuple-element.13), kind=kOutput, calls=%fused_computation | convolution fusion | flops 3227516928 | bytes 9961472 | tf_op jit(solution)/shard_map/dot_general | solution.py:38
  148.5 0.0 reduce-scatter.3.cloned.1.call-update
  148.5 6.0 %all-to-all-start.1 = ((bf16[64,8,2048]{2,1,0:T(8,128)(2,1)}), bf16[64,8,2048]{2,1,0:T(8,128)(2,1)}, u32[]{:S(2)}, u32[]{:S(2)}) async-start(bf16[64,8,2048]{2,1,0:T(8,128)(2,1)} %bitcast.96), calls=%async_computation.1 | async-start | bytes 4194304 | tf_op jit(solution)/shard_map/all_to_all | solution.py:44
  154.5 0.3 reduce-scatter.5.cloned.1.call-start
  154.8 5.4 %convolution_convert_fusion.1 = bf16[768,2048]{1,0:T(8,128)(2,1)} fusion(bf16[512,768]{1,0:T(8,128)(2,1)} %copy-done.8, bf16[64,8,2048]{2,1,0:T(8,128)(2,1)} %all-to-all-done.2), kind=kOutput, calls=%fused_computation.4 | convolution fusion | flops 1612185600 | bytes 6029312 | tf_op jit(solution)/shard_map/dot_general | solution.py:38
  160.2 0.0 reduce-scatter.5.cloned.1.call-update
  160.2 0.0 copy-start.4
  160.2 0.0 copy-start.6
  160.2 4.1 %fusion.6 = f32[512,2048]{1,0:T(8,128)S(1)} fusion(bf16[512,768]{1,0:T(8,128)(2,1)} %copy-done.7, bf16[1,2048,768]{2,1,0:T(8,128)(2,1)} %param.12), kind=kOutput, calls=%fused_computation.9 | convolution fusion | flops 1610612736 | bytes 8126464 | tf_op jit(solution)/shard_map/dot_general | solution.py:31
  164.3 0.0 copy-done.4
  164.3 0.0 copy-done.6
  164.3 3.1 %fusion.21 = bf16[64,8,2048]{2,1,0:T(8,128)(2,1)} fusion(f32[512,2048]{1,0:T(8,128)S(1)} %fusion.6, bf16[512,768]{1,0:T(8,128)(2,1)S(1)} %copy-done.6, bf16[1,2048,768]{2,1,0:T(8,128)(2,1)S(1)} %copy-done.4), kind=kOutput, calls=%fused_computation.23 | convolution fusion | flops 1612709888 | bytes 10223616 | tf_op jit(solution)/shard_map/dot_general | solution.py:30
  167.5 38.2 %all-to-all-done.1 = bf16[64,8,2048]{2,1,0:T(8,128)(2,1)} async-done(((bf16[64,8,2048]{2,1,0:T(8,128)(2,1)}), bf16[64,8,2048]{2,1,0:T(8,128)(2,1)}, u32[]{:S(2)}, u32[]{:S(2)}) %all-to-all-start.1) | async-done | bytes 2097184 | tf_op jit(solution)/shard_map/all_to_all | solution.py:44
  205.7 6.0 %all-to-all-start.3 = ((bf16[64,8,2048]{2,1,0:T(8,128)(2,1)}), bf16[64,8,2048]{2,1,0:T(8,128)(2,1)}, u32[]{:S(2)}, u32[]{:S(2)}) async-start(bf16[64,8,2048]{2,1,0:T(8,128)(2,1)} %fusion.21), calls=%async_computation.3 | async-start | bytes 4194304 | tf_op jit(solution)/shard_map/all_to_all | solution.py:44
  211.7 0.1 copy.35
  211.8 2.6 fusion.24
  214.4 1.3 fusion
  215.8 0.9 copy.42
  216.6 46.2 %all-to-all-done.3 = bf16[64,8,2048]{2,1,0:T(8,128)(2,1)} async-done(((bf16[64,8,2048]{2,1,0:T(8,128)(2,1)}), bf16[64,8,2048]{2,1,0:T(8,128)(2,1)}, u32[]{:S(2)}, u32[]{:S(2)}) %all-to-all-start.3) | async-done | bytes 2097184 | tf_op jit(solution)/shard_map/all_to_all | solution.py:44
  262.8 2.8 %convolution_convert_fusion.4 = bf16[64,2048]{1,0:T(8,128)(2,1)} fusion(bf16[64,512]{1,0:T(8,128)(2,1)S(1)} %fusion.39, bf16[64,8,2048]{2,1,0:T(8,128)(2,1)} %all-to-all-done.3), kind=kOutput, calls=%fused_computation.24 | convolution fusion | flops 134348800 | bytes 2424832 | tf_op jit(solution)/shard_map/dot_general | solution.py:86
  265.6 0.0 reduce-scatter.3.cloned.1.call-done
  265.6 2.6 slice_bitcast_fusion
  268.2 0.0 reduce-scatter.5.cloned.1.call-done
  (3 shorter events, 0.1 us)
Async XLA Ops:
  7.2 87.0 %copy-start = (bf16[1,768,2048]{2,1,0:T(8,128)(2,1)S(1)}, bf16[1,768,2048]{2,1,0:T(8,128)(2,1)}, u32[]{:S(2)}) copy-start(bf16[1,768,2048]{2,1,0:T(8,128)(2,1)} %param.13) | copy-start | bytes 9437188
  13.8 13.3 %copy-start.2 = (f32[64,6]{0,1:T(8,128)S(1)}, f32[64,6]{0,1:T(8,128)}, u32[]{:S(2)}) copy-start(f32[64,6]{0,1:T(8,128)} %param.9) | copy-start | bytes 4612
  13.8 13.6 %copy-start.1 = (bf16[64,2048]{1,0:T(8,128)(2,1)S(1)}, bf16[64,2048]{1,0:T(8,128)(2,1)}, u32[]{:S(2)}) copy-start(bf16[64,2048]{1,0:T(8,128)(2,1)} %param.10) | copy-start | bytes 786436
  13.8 64.5 %all-to-all-start = ((bf16[64,8,2048]{2,1,0:T(8,128)(2,1)}), bf16[64,8,2048]{2,1,0:T(8,128)(2,1)}, u32[]{:S(2)}, u32[]{:S(2)}) async-start(bf16[64,8,2048]{2,1,0:T(8,128)(2,1)} %fusion.19), calls=%async_computation | async-start | bytes 4194304 | tf_op jit(solution)/shard_map/all_to_all | solution.py:44
  78.2 57.2 %all-to-all-start.2 = ((bf16[64,8,2048]{2,1,0:T(8,128)(2,1)}), bf16[64,8,2048]{2,1,0:T(8,128)(2,1)}, u32[]{:S(2)}, u32[]{:S(2)}) async-start(bf16[64,8,2048]{2,1,0:T(8,128)(2,1)} %fusion.20), calls=%async_computation.2 | async-start | bytes 4194304 | tf_op jit(solution)/shard_map/all_to_all | solution.py:44
  84.3 181.4 %reduce-scatter.3.cloned.1.call-start = ((), (), s32[]{:S(2)}) async-start(), calls=%async_computation.6 | async-start | bytes 7864320 | tf_op jit(solution)/shard_map/reduce_scatter | solution.py:90
  84.5 4.5 %copy-start.3 = (bf16[1,2048,768]{2,1,0:T(8,128)(2,1)S(1)}, bf16[1,2048,768]{2,1,0:T(8,128)(2,1)}, u32[]{:S(2)}) copy-start(bf16[1,2048,768]{2,1,0:T(8,128)(2,1)} %param.12) | copy-start | bytes 9437188
  89.0 5.2 %copy-start.9 = (f32[512,768]{1,0:T(8,128)}, f32[512,768]{1,0:T(8,128)S(1)}, u32[]{:S(2)}) copy-start(f32[512,768]{1,0:T(8,128)S(1)} %fusion.12) | copy-start | bytes 4718596
  94.1 3.3 %copy-start.8 = (bf16[512,768]{1,0:T(8,128)(2,1)}, bf16[512,768]{1,0:T(8,128)(2,1)S(1)}, u32[]{:S(2)}) copy-start(bf16[512,768]{1,0:T(8,128)(2,1)S(1)} %get-tuple-element.12) | copy-start | bytes 2359300
  140.2 0.9 copy-start.5
  140.2 1.1 copy-start.7
  148.5 57.2 %all-to-all-start.1 = ((bf16[64,8,2048]{2,1,0:T(8,128)(2,1)}), bf16[64,8,2048]{2,1,0:T(8,128)(2,1)}, u32[]{:S(2)}, u32[]{:S(2)}) async-start(bf16[64,8,2048]{2,1,0:T(8,128)(2,1)} %bitcast.96), calls=%async_computation.1 | async-start | bytes 4194304 | tf_op jit(solution)/shard_map/all_to_all | solution.py:44
  154.5 113.7 %reduce-scatter.5.cloned.1.call-start = ((), (), s32[]{:S(2)}) async-start(), calls=%async_computation.7 | async-start | bytes 3932160 | tf_op jit(solution)/shard_map/reduce_scatter | solution.py:96
  160.2 4.1 %copy-start.4 = (bf16[1,2048,768]{2,1,0:T(8,128)(2,1)S(1)}, bf16[1,2048,768]{2,1,0:T(8,128)(2,1)}, u32[]{:S(2)}) copy-start(bf16[1,2048,768]{2,1,0:T(8,128)(2,1)} %param.11) | copy-start | bytes 9437188
  160.2 4.1 %copy-start.6 = (bf16[512,768]{1,0:T(8,128)(2,1)S(1)}, bf16[512,768]{1,0:T(8,128)(2,1)}, u32[]{:S(2)}) copy-start(bf16[512,768]{1,0:T(8,128)(2,1)} %copy-done.5) | copy-start | bytes 2359300
  205.7 57.2 %all-to-all-start.3 = ((bf16[64,8,2048]{2,1,0:T(8,128)(2,1)}), bf16[64,8,2048]{2,1,0:T(8,128)(2,1)}, u32[]{:S(2)}, u32[]{:S(2)}) async-start(bf16[64,8,2048]{2,1,0:T(8,128)(2,1)} %fusion.21), calls=%async_computation.3 | async-start | bytes 4194304 | tf_op jit(solution)/shard_map/all_to_all | solution.py:44
Sparse Core Ops, SparseCore 0:
  148.6 63.2 reduce-scatter.2
  215.0 40.5 reduce-scatter.4

commit v3 on v2

--- a/solution.py
+++ b/solution.py
@@ -44,6 +44,22 @@
     return lax.all_to_all(blocks, "expert", split_axis=0, concat_axis=0, tiled=True)
 
 
+def ring_reduce_scatter(part, direction):
+    n = lax.axis_size("replica")
+    me = lax.axis_index("replica")
+    table = part.reshape((n, part.shape[0] // n) + part.shape[1:])
+    perm = [(i, (i + direction) % n) for i in range(n)]
+
+    def own(step):
+        return lax.dynamic_index_in_dim(table, (me - direction * (step + 1)) % n, 0, False)
+
+    acc = own(0)
+    for step in range(1, n):
+        acc = lax.ppermute(acc, "replica", perm)
+        acc = (acc.astype(jnp.float32) + own(step).astype(jnp.float32)).astype(jnp.bfloat16)
+    return acc
+
+
 def per_device(tokens, route_ids, gate_probs, out_cot, w_gate, w_up, w_down):
     experts = lax.axis_size("expert")
     tok_rows, features = tokens.shape
@@ -86,22 +102,17 @@
     grad_tokens = jnp.dot(owner, returned_grad, preferred_element_type=jnp.float32).astype(
         jnp.bfloat16
     )
-    gate_up_grad = jnp.concatenate([d_gate, d_up], axis=1)
-    gate_up_sum = lax.psum_scatter(
-        outer_sum(slot_rows, gate_up_grad).astype(jnp.bfloat16),
-        "replica",
-        scatter_dimension=0,
-        tiled=True,
-    ).astype(jnp.float32)
-    down_sum = lax.psum_scatter(
-        outer_sum(activation, grads_in).astype(jnp.bfloat16),
-        "replica",
-        scatter_dimension=0,
-        tiled=True,
-    )
-    grad_gate = gate_up_sum[:, :hidden].astype(jnp.bfloat16)[None]
-    grad_up = gate_up_sum[:, hidden:].astype(jnp.bfloat16)[None]
-    grad_down = down_sum[None]
+    half = features // 2
+    grad_gate = ring_reduce_scatter(outer_sum(slot_rows, d_gate).astype(jnp.bfloat16), 1)[None]
+    grad_up = ring_reduce_scatter(outer_sum(slot_rows, d_up).astype(jnp.bfloat16), -1)[None]
+    part_down = outer_sum(activation, grads_in).astype(jnp.bfloat16)
+    grad_down = jnp.concatenate(
+        [
+            ring_reduce_scatter(part_down[:, :half], 1),
+            ring_reduce_scatter(part_down[:, half:], -1),
+        ],
+        axis=1,
+    )[None]
     return (combined, grad_tokens, grad_gate, grad_up, grad_down)
 
 

time: 276 us -> 279 us (1.011)
  waiting for transfers between devices: 162 us -> 142 us
  other arithmetic: 1.93 us -> 20.1 us
  starting transfers between devices: 31.8 us -> 49.9 us
  between operations: 14.3 us -> 1.03 us
  matrix products: 51.8 us -> 47.6 us
    all_to_all x4, waiting for transfers between devices: 161 us -> 105 us  [exchange(): lax.all_to_all(blocks, 'expert', split_axis=0, concat_axis=0, tiled=True)]
    ppermute x0 -> x12, waiting for transfers between devices: none -> 37.3 us  [ring_reduce_scatter(): acc = lax.ppermute(acc, 'replica', perm)]
    ppermute x0 -> x12, starting transfers between devices: none -> 18.6 us  [ring_reduce_scatter(): acc = lax.ppermute(acc, 'replica', perm)]
    convert_element_type x0 -> x10, other arithmetic: none -> 14 us  [ring_reduce_scatter(): (acc.astype(jnp.float32) + own(step).astype(jnp.float32)).astype(jnp.bflo...]
    broadcast_in_dim x0 -> x3, other arithmetic: none -> 4.2 us  [the longest x1 2.19 us: per_device(): ring_reduce_scatter(outer_sum(slot_rows, d_gate).astype(jnp.bfloat16), 1)]
    squeeze x0 -> x4, local copies, waits for them, and re-layouts: none -> 3.49 us  [own(): lax.dynamic_index_in_dim(table, (me - direction * (step + 1)) % n, 0, False)]
    dot_general x2 -> x3, matrix products: 12.5 us -> 10.8 us  [outer_sum(): lax.dot_general(left, right, (((0,), (0,)), ((), ())), preferred_element_...]
  transfers between devices with their start and end apart: 6 -> 16, of which waited for: 4 -> 10; matrix products, arithmetic and copies ran while one was open for 17% -> 26% of each run, Pallas kernels for 0% -> 0%
where the time goes in v3:
time: 279 us; the launch traced here: 277 us
  waiting for transfers between devices  142 us (51%)
  starting transfers between devices  49.9 us (18%)
  matrix products  47.6 us (17%)
  other arithmetic  20.1 us (7%)
  local copies, waits for them, and re-layouts  15.6 us (6%)
    all_to_all x4, waiting for transfers between devices, exchange(): lax.all_to_all(blocks, 'expert', split_axis=0, concat_axis=0, tiled=True)  105 us
    ppermute x12, waiting for transfers between devices, ring_reduce_scatter(): acc = lax.ppermute(acc, 'replica', perm)  37.3 us
    all_to_all x4, starting transfers between devices, exchange(): lax.all_to_all(blocks, 'expert', split_axis=0, concat_axis=0, tiled=True)  31.3 us
    ppermute x12, starting transfers between devices, ring_reduce_scatter(): acc = lax.ppermute(acc, 'replica', perm)  18.6 us
    convert_element_type x10, other arithmetic, ring_reduce_scatter(): (acc.astype(jnp.float32) + own(step).astype(jnp.float32)).astype(jnp.bflo...  14 us
    dot_general x3, matrix products, outer_sum(): lax.dot_general(left, right, (((0,), (0,)), ((), ())), preferred_element_...  10.8 us
    mul x3, local copies, waits for them, and re-layouts, per_device(): gate_probs[:, :, None] * out_cot[:, None, :].astype(jnp.float32)  7.33 us
  transfers between devices with their start and end apart: 16, of which 10 were waited for; matrix products, arithmetic and copies ran while one was open for 26% of the time, Pallas kernels for 0%

profile of v3, /device:TPU:1, one launch (start us, length us, event | category | flops | bytes accessed | tf_op | source)
XLA Modules:
  0.0 276.6 jit_solution(13649930694999168762)
XLA Ops:
  0.6 0.9 copy.29
  1.7 0.1 eq.88
  1.9 0.9 reduce-window.6
  2.8 0.2 slice_reduce_fusion
  3.4 0.7 multiply_add_fusion
  4.1 0.1 fusion.51
  4.2 3.0 %fusion.19 = bf16[64,8,2048]{2,1,0:T(8,128)(2,1)} fusion(bf16[64,512]{1,0:T(8,128)(2,1)S(1)} %fusion.51, bf16[64,2048]{1,0:T(8,128)(2,1)} %param.7), kind=kOutput, calls=%fused_computation.22 | convolution fusion | flops 135266304 | bytes 2424832 | tf_op jit(solution)/shard_map/dot_general | solution.py:79
  7.2 13.3 %all-to-all-start = ((bf16[64,8,2048]{2,1,0:T(8,128)(2,1)}), bf16[64,8,2048]{2,1,0:T(8,128)(2,1)}, u32[]{:S(2)}, u32[]{:S(2)}) async-start(bf16[64,8,2048]{2,1,0:T(8,128)(2,1)} %fusion.19), calls=%async_computation | async-start | bytes 4194304 | tf_op jit(solution)/shard_map/all_to_all | solution.py:44
  20.6 2.5 mul.70
  23.0 4.7 %mul.71 = f32[384,2048]{1,0:T(8,128)} reshape(f32[64,6,2048]{2,1,0:T(8,128)} %mul.70) | data formatting | bytes 6291456 | tf_op jit(solution)/shard_map/mul | solution.py:81
  27.9 0.1 mul.68
  28.0 4.6 %fusion.20 = bf16[64,8,2048]{2,1,0:T(8,128)(2,1)} fusion(f32[384,2048]{1,0:T(8,128)} %mul.71, f32[384]{0:T(512)S(1)} %mul.68, s32[384]{0:T(512)S(1)} %multiply_add_fusion.1), kind=kOutput, calls=%fused_computation.23 | convolution fusion | flops 808124416 | bytes 5245952 | tf_op jit(solution)/shard_map/dot_general | solution.py:82
  32.6 39.1 %all-to-all-done = bf16[64,8,2048]{2,1,0:T(8,128)(2,1)} async-done(((bf16[64,8,2048]{2,1,0:T(8,128)(2,1)}), bf16[64,8,2048]{2,1,0:T(8,128)(2,1)}, u32[]{:S(2)}, u32[]{:S(2)}) %all-to-all-start) | async-done | bytes 2097184 | tf_op jit(solution)/shard_map/all_to_all | solution.py:44
  71.7 6.0 %all-to-all-start.2 = ((bf16[64,8,2048]{2,1,0:T(8,128)(2,1)}), bf16[64,8,2048]{2,1,0:T(8,128)(2,1)}, u32[]{:S(2)}, u32[]{:S(2)}) async-start(bf16[64,8,2048]{2,1,0:T(8,128)(2,1)} %fusion.20), calls=%async_computation.2 | async-start | bytes 4194304 | tf_op jit(solution)/shard_map/all_to_all | solution.py:44
  77.7 4.5 %fusion.12 = f32[512,768]{1,0:T(8,128)S(1)} fusion(bf16[1,2048,768]{2,1,0:T(8,128)(2,1)} %param.11, bf16[64,8,2048]{2,1,0:T(8,128)(2,1)} %all-to-all-done), kind=kOutput, calls=%fused_computation.16 | convolution fusion | flops 1610612736 | bytes 6815744 | tf_op jit(solution)/shard_map/dot_general | solution.py:16
  82.2 5.2 %multiply_convert_fusion.4 = (bf16[512,768]{1,0:T(8,128)(2,1)S(1)}, f32[512,768]{1,0:T(8,128)}) fusion(f32[512,768]{1,0:T(8,128)S(1)} %fusion.12, bf16[1,2048,768]{2,1,0:T(8,128)(2,1)S(1)} %copy-done.7, bf16[64,8,2048]{2,1,0:T(8,128)(2,1)} %all-to-all-done), kind=kOutput, calls=%fused_computation.51 | convolution fusion | flops 1612972032 | bytes 9175040 | tf_op jit(solution)/shard_map/dot_general | solution.py:17
  87.4 3.2 %fusion.14 = bf16[512,2048]{1,0:T(8,128)(2,1)} fusion(bf16[512,768]{1,0:T(8,128)(2,1)S(1)} %get-tuple-element.12, bf16[1,768,2048]{2,1,0:T(8,128)(2,1)S(1)} %copy-done), kind=kOutput, calls=%fused_computation.19 | convolution fusion | flops 1611661312 | bytes 6029312 | tf_op jit(solution)/shard_map/dot_general | solution.py:88
  90.6 38.3 %all-to-all-done.2 = bf16[64,8,2048]{2,1,0:T(8,128)(2,1)} async-done(((bf16[64,8,2048]{2,1,0:T(8,128)(2,1)}), bf16[64,8,2048]{2,1,0:T(8,128)(2,1)}, u32[]{:S(2)}, u32[]{:S(2)}) %all-to-all-start.2) | async-done | bytes 2097184 | tf_op jit(solution)/shard_map/all_to_all | solution.py:44
  128.9 6.0 %all-to-all-start.1 = ((bf16[64,8,2048]{2,1,0:T(8,128)(2,1)}), bf16[64,8,2048]{2,1,0:T(8,128)(2,1)}, u32[]{:S(2)}, u32[]{:S(2)}) async-start(bf16[64,8,2048]{2,1,0:T(8,128)(2,1)} %bitcast.165), calls=%async_computation.1 | async-start | bytes 4194304 | tf_op jit(solution)/shard_map/all_to_all | solution.py:44
  135.0 4.7 %multiply_convert_fusion.3 = (bf16[512,768]{1,0:T(8,128)(2,1)S(1)}, bf16[512,768]{1,0:T(8,128)(2,1)S(1)}) fusion(f32[512,768]{1,0:T(8,128)} %copy-done.13, f32[512,768]{1,0:T(8,128)} %get-tuple-element.10, bf16[1,768,2048]{2,1,0:T(8,128)(2,1)S(1)} %copy-done, bf16[64,8,2048]{2,1,0:T(8,128)(2,1)} %all-to-all-done.2), kind=kOutput, calls=%fused_computation.48 | convolution fusion | flops 1615724544 | bytes 9961472 | tf_op jit(solution)/shard_map/dot_general | solution.py:24
  139.7 3.7 %convolution_convert_fusion.2 = bf16[2048,768]{1,0:T(8,128)(2,1)S(1)} fusion(bf16[512,768]{1,0:T(8,128)(2,1)S(1)} %get-tuple-element.15, bf16[64,8,2048]{2,1,0:T(8,128)(2,1)} %all-to-all-done), kind=kOutput, calls=%fused_computation.5 | convolution fusion | flops 1612185600 | bytes 6029312 | tf_op jit(solution)/shard_map/dot_general | solution.py:38
  143.5 1.0 dynamic-slice_bitcast_fusion.1
  144.5 1.3 collective-permute-start
  145.8 3.4 %convolution_convert_fusion = bf16[768,2048]{1,0:T(8,128)(2,1)S(1)} fusion(bf16[512,768]{1,0:T(8,128)(2,1)S(1)} %copy-done.12, bf16[64,8,2048]{2,1,0:T(8,128)(2,1)} %all-to-all-done.2), kind=kOutput, calls=%fused_computation.3 | convolution fusion | flops 1612185600 | bytes 6029312 | tf_op jit(solution)/shard_map/dot_general | solution.py:38
  149.2 0.3 fusion.58
  149.6 0.8 dynamic-slice_bitcast_fusion.2
  150.3 2.3 collective-permute-start.9
  152.6 0.8 dynamic-slice_bitcast_fusion.3
  153.4 1.8 fusion.6
  155.3 3.2 %fusion.21 = bf16[64,8,2048]{2,1,0:T(8,128)(2,1)} fusion(f32[512,2048]{1,0:T(8,128)S(1)} %fusion.6, bf16[512,768]{1,0:T(8,128)(2,1)S(1)} %get-tuple-element.15, bf16[1,2048,768]{2,1,0:T(8,128)(2,1)S(1)} %copy-done.9), kind=kOutput, calls=%fused_computation.24 | convolution fusion | flops 1612709888 | bytes 10223616 | tf_op jit(solution)/shard_map/dot_general | solution.py:30
  158.4 27.6 %all-to-all-done.1 = bf16[64,8,2048]{2,1,0:T(8,128)(2,1)} async-done(((bf16[64,8,2048]{2,1,0:T(8,128)(2,1)}), bf16[64,8,2048]{2,1,0:T(8,128)(2,1)}, u32[]{:S(2)}, u32[]{:S(2)}) %all-to-all-start.1) | async-done | bytes 2097184 | tf_op jit(solution)/shard_map/all_to_all | solution.py:44
  186.1 6.0 %all-to-all-start.3 = ((bf16[64,8,2048]{2,1,0:T(8,128)(2,1)}), bf16[64,8,2048]{2,1,0:T(8,128)(2,1)}, u32[]{:S(2)}, u32[]{:S(2)}) async-start(bf16[64,8,2048]{2,1,0:T(8,128)(2,1)} %fusion.21), calls=%async_computation.3 | async-start | bytes 4194304 | tf_op jit(solution)/shard_map/all_to_all | solution.py:44
  192.1 3.6 %convolution_convert_fusion.1 = bf16[2048,768]{1,0:T(8,128)(2,1)S(1)} fusion(bf16[512,768]{1,0:T(8,128)(2,1)} %copy-done.10, bf16[64,8,2048]{2,1,0:T(8,128)(2,1)} %all-to-all-done), kind=kOutput, calls=%fused_computation.4 | convolution fusion | flops 1612185600 | bytes 6029312 | tf_op jit(solution)/shard_map/dot_general | solution.py:38
  195.7 1.7 copy-done.3
  197.4 0.9 dynamic-slice_bitcast_fusion
  198.3 2.7 collective-permute-start.3
  201.0 1.9 fusion.44
  202.9 0.5 collective-permute-start.10
  203.4 1.9 fusion.47
  205.3 1.0 collective-permute-start.7
  206.3 2.4 fusion.38
  208.7 8.8 %collective-permute-done.3 = bf16[512,768]{1,0:T(8,128)(2,1)} collective-permute-done((bf16[512,768]{1,0:T(8,128)(2,1)}, bf16[512,768]{1,0:T(8,128)(2,1)}, u32[]{:S(2)}, u32[]{:S(2)}) %collective-permute-start.3) | collective-permute-done | bytes 786464 | tf_op jit(solution)/shard_map/ppermute | solution.py:58
  217.5 2.4 fusion.35
  219.9 3.4 %collective-permute-start.4 = (bf16[512,768]{1,0:T(8,128)(2,1)}, bf16[512,768]{1,0:T(8,128)(2,1)}, u32[]{:S(2)}, u32[]{:S(2)}) collective-permute-start(bf16[512,768]{1,0:T(8,128)(2,1)} %fusion.35), channel_id=1, source_target_pairs={{0,3},{1,0},{2,1},{3,2},{4,7},{5,4},{6,5},{7,6},{8,11},{9,8},{10,9... | collective-permute-start | bytes 2359304 | tf_op jit(solution)/shard_map/ppermute | solution.py:58
  223.5 2.4 collective-permute-done.10
  225.9 1.1 fusion.43
  227.0 3.5 %collective-permute-start.11 = (bf16[192,1024]{1,0:T(8,128)(2,1)S(1)}, bf16[192,1024]{1,0:T(8,128)(2,1)S(1)}, u32[]{:S(2)}, u32[]{:S(2)}) collective-permute-start(bf16[192,1024]{1,0:T(8,128)(2,1)S(1)} %fusion.43), channel_id=1, source_target_pairs={{0,3},{1,0},{2,1},{3,2},{4,7},{5,4},{6,5},{7,6},{8,11},{9,8},{10,9... | collective-permute-start | bytes 1179656 | tf_op jit(solution)/shard_map/ppermute | solution.py:58
  230.5 1.1 fusion.46
  231.8 1.2 collective-permute-done.1
  232.9 1.6 fusion.37
  234.6 8.2 %collective-permute-done.4 = bf16[512,768]{1,0:T(8,128)(2,1)} collective-permute-done((bf16[512,768]{1,0:T(8,128)(2,1)}, bf16[512,768]{1,0:T(8,128)(2,1)}, u32[]{:S(2)}, u32[]{:S(2)}) %collective-permute-start.4) | collective-permute-done | bytes 786464 | tf_op jit(solution)/shard_map/ppermute | solution.py:58
  242.8 1.3 fusion.34
  244.1 3.7 %collective-permute-start.5 = (bf16[512,768]{1,0:T(8,128)(2,1)S(1)}, bf16[512,768]{1,0:T(8,128)(2,1)S(1)}, u32[]{:S(2)}, u32[]{:S(2)}) collective-permute-start(bf16[512,768]{1,0:T(8,128)(2,1)S(1)} %fusion.34), channel_id=1, source_target_pairs={{0,3},{1,0},{2,1},{3,2},{4,7},{5,4},{6,5},{7,6},{8,11},{9,8},{10,9... | collective-permute-start | bytes 2359304 | tf_op jit(solution)/shard_map/ppermute | solution.py:58
  247.8 3.2 %collective-permute-done.11 = bf16[192,1024]{1,0:T(8,128)(2,1)S(1)} collective-permute-done((bf16[192,1024]{1,0:T(8,128)(2,1)S(1)}, bf16[192,1024]{1,0:T(8,128)(2,1)S(1)}, u32[]{:S(2)}, u32[]{:S(2)}) %collective-permute-start.11) | collective-permute-done | bytes 393248 | tf_op jit(solution)/shard_map/ppermute | solution.py:58
  251.2 0.1 fusion.45
  251.4 0.9 maximum_bitcast_fusion
  252.3 5.0 %collective-permute-done.2 = bf16[512,768]{1,0:T(8,128)(2,1)S(1)} collective-permute-done((bf16[512,768]{1,0:T(8,128)(2,1)S(1)}, bf16[512,768]{1,0:T(8,128)(2,1)S(1)}, u32[]{:S(2)}, u32[]{:S(2)}) %collective-permute-start.2) | collective-permute-done | bytes 786464 | tf_op jit(solution)/shard_map/ppermute | solution.py:58
  257.3 2.2 fusion.40
  259.5 8.5 %collective-permute-done.5 = bf16[512,768]{1,0:T(8,128)(2,1)S(1)} collective-permute-done((bf16[512,768]{1,0:T(8,128)(2,1)S(1)}, bf16[512,768]{1,0:T(8,128)(2,1)S(1)}, u32[]{:S(2)}, u32[]{:S(2)}) %collective-permute-start.5) | collective-permute-done | bytes 786464 | tf_op jit(solution)/shard_map/ppermute | solution.py:58
  267.9 1.1 fusion.41
  269.0 2.6 fusion.24
  271.6 1.3 fusion
  273.0 0.9 copy.42
  273.8 2.8 %convolution_convert_fusion.5 = bf16[64,2048]{1,0:T(8,128)(2,1)} fusion(bf16[64,512]{1,0:T(8,128)(2,1)S(1)} %fusion.51, bf16[64,8,2048]{2,1,0:T(8,128)(2,1)} %all-to-all-done.3), kind=kOutput, calls=%fused_computation.25 | convolution fusion | flops 134348800 | bytes 2424832 | tf_op jit(solution)/shard_map/dot_general | solution.py:102
  (47 shorter events, 1.2 us)
Async XLA Ops:
  0.6 86.8 %copy-start = (bf16[1,768,2048]{2,1,0:T(8,128)(2,1)S(1)}, bf16[1,768,2048]{2,1,0:T(8,128)(2,1)}, u32[]{:S(2)}) copy-start(bf16[1,768,2048]{2,1,0:T(8,128)(2,1)} %param.13) | copy-start | bytes 9437188
  7.2 13.3 %copy-start.5 = (bf16[64,2048]{1,0:T(8,128)(2,1)S(1)}, bf16[64,2048]{1,0:T(8,128)(2,1)}, u32[]{:S(2)}) copy-start(bf16[64,2048]{1,0:T(8,128)(2,1)} %param.10) | copy-start | bytes 786436
  7.2 64.5 %all-to-all-start = ((bf16[64,8,2048]{2,1,0:T(8,128)(2,1)}), bf16[64,8,2048]{2,1,0:T(8,128)(2,1)}, u32[]{:S(2)}, u32[]{:S(2)}) async-start(bf16[64,8,2048]{2,1,0:T(8,128)(2,1)} %fusion.19), calls=%async_computation | async-start | bytes 4194304 | tf_op jit(solution)/shard_map/all_to_all | solution.py:44
  23.0 4.7 %copy-start.6 = (f32[64,6]{0,1:T(8,128)S(1)}, f32[64,6]{0,1:T(8,128)}, u32[]{:S(2)}) copy-start(f32[64,6]{0,1:T(8,128)} %param.9) | copy-start | bytes 4612
  71.7 57.2 %all-to-all-start.2 = ((bf16[64,8,2048]{2,1,0:T(8,128)(2,1)}), bf16[64,8,2048]{2,1,0:T(8,128)(2,1)}, u32[]{:S(2)}, u32[]{:S(2)}) async-start(bf16[64,8,2048]{2,1,0:T(8,128)(2,1)} %fusion.20), calls=%async_computation.2 | async-start | bytes 4194304 | tf_op jit(solution)/shard_map/all_to_all | solution.py:44
  77.7 4.5 %copy-start.7 = (bf16[1,2048,768]{2,1,0:T(8,128)(2,1)S(1)}, bf16[1,2048,768]{2,1,0:T(8,128)(2,1)}, u32[]{:S(2)}) copy-start(bf16[1,2048,768]{2,1,0:T(8,128)(2,1)} %param.12) | copy-start | bytes 9437188
  82.2 5.2 %copy-start.13 = (f32[512,768]{1,0:T(8,128)}, f32[512,768]{1,0:T(8,128)S(1)}, u32[]{:S(2)}) copy-start(f32[512,768]{1,0:T(8,128)S(1)} %fusion.12) | copy-start | bytes 4718596
  87.4 3.2 %copy-start.11 = (bf16[512,768]{1,0:T(8,128)(2,1)}, bf16[512,768]{1,0:T(8,128)(2,1)S(1)}, u32[]{:S(2)}) copy-start(bf16[512,768]{1,0:T(8,128)(2,1)S(1)} %get-tuple-element.12) | copy-start | bytes 2359300
  128.9 57.2 %all-to-all-start.1 = ((bf16[64,8,2048]{2,1,0:T(8,128)(2,1)}), bf16[64,8,2048]{2,1,0:T(8,128)(2,1)}, u32[]{:S(2)}, u32[]{:S(2)}) async-start(bf16[64,8,2048]{2,1,0:T(8,128)(2,1)} %bitcast.165), calls=%async_computation.1 | async-start | bytes 4194304 | tf_op jit(solution)/shard_map/all_to_all | solution.py:44
  139.7 13.7 %copy-start.10 = (bf16[512,768]{1,0:T(8,128)(2,1)}, bf16[512,768]{1,0:T(8,128)(2,1)S(1)}, u32[]{:S(2)}) copy-start(bf16[512,768]{1,0:T(8,128)(2,1)S(1)} %get-tuple-element.16) | copy-start | bytes 2359300
  139.7 6.1 %copy-start.12 = (bf16[512,768]{1,0:T(8,128)(2,1)S(1)}, bf16[512,768]{1,0:T(8,128)(2,1)}, u32[]{:S(2)}) copy-start(bf16[512,768]{1,0:T(8,128)(2,1)} %copy-done.11) | copy-start | bytes 2359300
  143.5 2.3 copy-start.2
  144.5 61.8 %collective-permute-start = (bf16[512,768]{1,0:T(8,128)(2,1)}, bf16[512,768]{1,0:T(8,128)(2,1)}, u32[]{:S(2)}, u32[]{:S(2)}) collective-permute-start(bf16[512,768]{1,0:T(8,128)(2,1)} %dynamic-slice_bitcast_fusion.1), channel_id=1, source_target_pairs={{0,1},{1,2},{2,3},{3,0},{4,5},{5,6},{6,7},{7,4},{8,9},{9,10},{10,1... | collective-permute-start | bytes 2359304 | tf_op jit(solution)/shard_map/ppermute | solution.py:58
  149.2 4.2 %copy-start.8 = (bf16[1,2048,768]{2,1,0:T(8,128)(2,1)S(1)}, bf16[1,2048,768]{2,1,0:T(8,128)(2,1)}, u32[]{:S(2)}) copy-start(bf16[1,2048,768]{2,1,0:T(8,128)(2,1)} %param.12) | copy-start | bytes 9437188
  150.3 50.7 %collective-permute-start.9 = (bf16[192,1024]{1,0:T(8,128)(2,1)}, bf16[192,1024]{1,0:T(8,128)(2,1)}, u32[]{:S(2)}, u32[]{:S(2)}) collective-permute-start(bf16[192,1024]{1,0:T(8,128)(2,1)} %dynamic-slice_bitcast_fusion.2), channel_id=1, source_target_pairs={{0,3},{1,0},{2,1},{3,2},{4,7},{5,4},{6,5},{7,6},{8,11},{9,8},{10,9... | collective-permute-start | bytes 1179656 | tf_op jit(solution)/shard_map/ppermute | solution.py:58
  153.4 50.0 %collective-permute-start.6 = (bf16[192,1024]{1,0:T(8,128)(2,1)}, bf16[192,1024]{1,0:T(8,128)(2,1)}, u32[]{:S(2)}, u32[]{:S(2)}) collective-permute-start(bf16[192,1024]{1,0:T(8,128)(2,1)} %dynamic-slice_bitcast_fusion.3), channel_id=1, source_target_pairs={{0,1},{1,2},{2,3},{3,0},{4,5},{5,6},{6,7},{7,4},{8,9},{9,10},{10,1... | collective-permute-start | bytes 1179656 | tf_op jit(solution)/shard_map/ppermute | solution.py:58
  153.4 1.9 copy-start.9
  186.1 87.8 %all-to-all-start.3 = ((bf16[64,8,2048]{2,1,0:T(8,128)(2,1)}), bf16[64,8,2048]{2,1,0:T(8,128)(2,1)}, u32[]{:S(2)}, u32[]{:S(2)}) async-start(bf16[64,8,2048]{2,1,0:T(8,128)(2,1)} %fusion.21), calls=%async_computation.3 | async-start | bytes 4194304 | tf_op jit(solution)/shard_map/all_to_all | solution.py:44
  195.7 1.7 copy-start.3
  198.3 19.2 %collective-permute-start.3 = (bf16[512,768]{1,0:T(8,128)(2,1)}, bf16[512,768]{1,0:T(8,128)(2,1)}, u32[]{:S(2)}, u32[]{:S(2)}) collective-permute-start(bf16[512,768]{1,0:T(8,128)(2,1)} %dynamic-slice_bitcast_fusion), channel_id=1, source_target_pairs={{0,3},{1,0},{2,1},{3,2},{4,7},{5,4},{6,5},{7,6},{8,11},{9,8},{10,9... | collective-permute-start | bytes 2359304 | tf_op jit(solution)/shard_map/ppermute | solution.py:58
  202.9 23.0 %collective-permute-start.10 = (bf16[192,1024]{1,0:T(8,128)(2,1)}, bf16[192,1024]{1,0:T(8,128)(2,1)}, u32[]{:S(2)}, u32[]{:S(2)}) collective-permute-start(bf16[192,1024]{1,0:T(8,128)(2,1)} %fusion.44), channel_id=1, source_target_pairs={{0,3},{1,0},{2,1},{3,2},{4,7},{5,4},{6,5},{7,6},{8,11},{9,8},{10,9... | collective-permute-start | bytes 1179656 | tf_op jit(solution)/shard_map/ppermute | solution.py:58
  205.3 25.3 %collective-permute-start.7 = (bf16[192,1024]{1,0:T(8,128)(2,1)}, bf16[192,1024]{1,0:T(8,128)(2,1)}, u32[]{:S(2)}, u32[]{:S(2)}) collective-permute-start(bf16[192,1024]{1,0:T(8,128)(2,1)} %fusion.47), channel_id=1, source_target_pairs={{0,1},{1,2},{2,3},{3,0},{4,5},{5,6},{6,7},{7,4},{8,9},{9,10},{10,1... | collective-permute-start | bytes 1179656 | tf_op jit(solution)/shard_map/ppermute | solution.py:58
  208.7 24.2 %collective-permute-start.1 = (bf16[512,768]{1,0:T(8,128)(2,1)}, bf16[512,768]{1,0:T(8,128)(2,1)}, u32[]{:S(2)}, u32[]{:S(2)}) collective-permute-start(bf16[512,768]{1,0:T(8,128)(2,1)} %fusion.38), channel_id=1, source_target_pairs={{0,1},{1,2},{2,3},{3,0},{4,5},{5,6},{6,7},{7,4},{8,9},{9,10},{10,1... | collective-permute-start | bytes 2359304 | tf_op jit(solution)/shard_map/ppermute | solution.py:58
  219.9 22.8 %collective-permute-start.4 = (bf16[512,768]{1,0:T(8,128)(2,1)}, bf16[512,768]{1,0:T(8,128)(2,1)}, u32[]{:S(2)}, u32[]{:S(2)}) collective-permute-start(bf16[512,768]{1,0:T(8,128)(2,1)} %fusion.35), channel_id=1, source_target_pairs={{0,3},{1,0},{2,1},{3,2},{4,7},{5,4},{6,5},{7,6},{8,11},{9,8},{10,9... | collective-permute-start | bytes 2359304 | tf_op jit(solution)/shard_map/ppermute | solution.py:58
  223.5 19.3 %copy-start.4 = (bf16[2048,768]{1,0:T(8,128)(2,1)S(1)}, bf16[2048,768]{1,0:T(8,128)(2,1)}, u32[]{:S(2)}) copy-start(bf16[2048,768]{1,0:T(8,128)(2,1)} %copy-done.3) | copy-start | bytes 9437188
  227.0 24.0 %collective-permute-start.11 = (bf16[192,1024]{1,0:T(8,128)(2,1)S(1)}, bf16[192,1024]{1,0:T(8,128)(2,1)S(1)}, u32[]{:S(2)}, u32[]{:S(2)}) collective-permute-start(bf16[192,1024]{1,0:T(8,128)(2,1)S(1)} %fusion.43), channel_id=1, source_target_pairs={{0,3},{1,0},{2,1},{3,2},{4,7},{5,4},{6,5},{7,6},{8,11},{9,8},{10,9... | collective-permute-start | bytes 1179656 | tf_op jit(solution)/shard_map/ppermute | solution.py:58
  231.7 19.6 %collective-permute-start.8 = (bf16[192,1024]{1,0:T(8,128)(2,1)S(1)}, bf16[192,1024]{1,0:T(8,128)(2,1)S(1)}, u32[]{:S(2)}, u32[]{:S(2)}) collective-permute-start(bf16[192,1024]{1,0:T(8,128)(2,1)S(1)} %fusion.46), channel_id=1, source_target_pairs={{0,1},{1,2},{2,3},{3,0},{4,5},{5,6},{6,7},{7,4},{8,9},{9,10},{10,1... | collective-permute-start | bytes 1179656 | tf_op jit(solution)/shard_map/ppermute | solution.py:58
  234.5 22.8 %collective-permute-start.2 = (bf16[512,768]{1,0:T(8,128)(2,1)S(1)}, bf16[512,768]{1,0:T(8,128)(2,1)S(1)}, u32[]{:S(2)}, u32[]{:S(2)}) collective-permute-start(bf16[512,768]{1,0:T(8,128)(2,1)S(1)} %fusion.37), channel_id=1, source_target_pairs={{0,1},{1,2},{2,3},{3,0},{4,5},{5,6},{6,7},{7,4},{8,9},{9,10},{10,1... | collective-permute-start | bytes 2359304 | tf_op jit(solution)/shard_map/ppermute | solution.py:58
  244.1 23.9 %collective-permute-start.5 = (bf16[512,768]{1,0:T(8,128)(2,1)S(1)}, bf16[512,768]{1,0:T(8,128)(2,1)S(1)}, u32[]{:S(2)}, u32[]{:S(2)}) collective-permute-start(bf16[512,768]{1,0:T(8,128)(2,1)S(1)} %fusion.34), channel_id=1, source_target_pairs={{0,3},{1,0},{2,1},{3,2},{4,7},{5,4},{6,5},{7,6},{8,11},{9,8},{10,9... | collective-permute-start | bytes 2359304 | tf_op jit(solution)/shard_map/ppermute | solution.py:58
  271.6 5.0 %copy-start.1 = (bf16[1,768,2048]{2,1,0:T(8,128)(2,1)S(1)}, bf16[1,768,2048]{2,1,0:T(8,128)(2,1)}, u32[]{:S(2)}) copy-start(bf16[1,768,2048]{2,1,0:T(8,128)(2,1)} %param.13) | copy-start | bytes 9437188

commit v4 on v3

--- a/solution.py
+++ b/solution.py
@@ -102,16 +102,24 @@
     grad_tokens = jnp.dot(owner, returned_grad, preferred_element_type=jnp.float32).astype(
         jnp.bfloat16
     )
+    replicas = lax.axis_size("replica")
     half = features // 2
-    grad_gate = ring_reduce_scatter(outer_sum(slot_rows, d_gate).astype(jnp.bfloat16), 1)[None]
-    grad_up = ring_reduce_scatter(outer_sum(slot_rows, d_up).astype(jnp.bfloat16), -1)[None]
     part_down = outer_sum(activation, grads_in).astype(jnp.bfloat16)
+    down_rows = part_down.shape[0] // replicas
+    down_halves = [
+        part_down[:, :half].reshape(replicas, down_rows * half // hidden, hidden),
+        part_down[:, half:].reshape(replicas, down_rows * half // hidden, hidden),
+    ]
+    sums = []
+    for direction, wide, down_half in zip((1, -1), (d_gate, d_up), down_halves):
+        part = outer_sum(slot_rows, wide).astype(jnp.bfloat16)
+        table = jnp.concatenate([part.reshape(replicas, -1, hidden), down_half], axis=1)
+        sums.append(ring_reduce_scatter(table.reshape(-1, hidden), direction))
+    rows = features // replicas
+    grad_gate = sums[0][:rows][None]
+    grad_up = sums[1][:rows][None]
     grad_down = jnp.concatenate(
-        [
-            ring_reduce_scatter(part_down[:, :half], 1),
-            ring_reduce_scatter(part_down[:, half:], -1),
-        ],
-        axis=1,
+        [sums[0][rows:].reshape(down_rows, half), sums[1][rows:].reshape(down_rows, half)], axis=1
     )[None]
     return (combined, grad_tokens, grad_gate, grad_up, grad_down)
 

time: 279 us -> 277 us (level)
  waiting for transfers between devices: 142 us -> 125 us
  local copies, waits for them, and re-layouts: 15.6 us -> 26.5 us
  matrix products: 47.6 us -> 51.9 us
  starting transfers between devices: 49.9 us -> 46.4 us
    all_to_all x4, waiting for transfers between devices: 105 us -> 77.4 us  [exchange(): lax.all_to_all(blocks, 'expert', split_axis=0, concat_axis=0, tiled=True)]
    ppermute x12 -> x6, waiting for transfers between devices: 37.3 us -> 48.1 us  [ring_reduce_scatter(): acc = lax.ppermute(acc, 'replica', perm)]
    ppermute x12 -> x6, starting transfers between devices: 18.6 us -> 8.85 us  [ring_reduce_scatter(): acc = lax.ppermute(acc, 'replica', perm)]
    reshape x0 -> x4, local copies, waits for them, and re-layouts: none -> 9.2 us  [the longest x1 3.92 us: per_device(): part_down[:, half:].reshape(replicas, down_rows * half // hidden, hidden)]
    all_to_all x4, starting transfers between devices: 31.3 us -> 37.6 us  [exchange(): lax.all_to_all(blocks, 'expert', split_axis=0, concat_axis=0, tiled=True)]
    squeeze x4 -> x0, local copies, waits for them, and re-layouts: 3.49 us -> none  [own(): lax.dynamic_index_in_dim(table, (me - direction * (step + 1)) % n, 0, False)]
    squeeze x0 -> x2, other arithmetic: none -> 3.44 us  [own(): lax.dynamic_index_in_dim(table, (me - direction * (step + 1)) % n, 0, False)]
    broadcast_in_dim x3 -> x1, other arithmetic: 4.2 us -> 0.94 us  [per_device(): jnp.concatenate([sums[0][rows:].reshape(down_rows, half), sums[1][rows:]....]
  transfers between devices with their start and end apart: 16 -> 10, of which waited for: 10 -> 7; matrix products, arithmetic and copies ran while one was open for 26% -> 32% of each run, Pallas kernels for 0% -> 0%
where the time goes in v4:
time: 277 us; the launch traced here: 272 us
  waiting for transfers between devices  125 us (45%)
  matrix products  51.9 us (19%)
  starting transfers between devices  46.4 us (17%)
  local copies, waits for them, and re-layouts  26.5 us (10%)
  other arithmetic  20.7 us (7%)
    all_to_all x4, waiting for transfers between devices, exchange(): lax.all_to_all(blocks, 'expert', split_axis=0, concat_axis=0, tiled=True)  77.4 us
    ppermute x6, waiting for transfers between devices, ring_reduce_scatter(): acc = lax.ppermute(acc, 'replica', perm)  48.1 us
    all_to_all x4, starting transfers between devices, exchange(): lax.all_to_all(blocks, 'expert', split_axis=0, concat_axis=0, tiled=True)  37.6 us
    convert_element_type x6, other arithmetic, ring_reduce_scatter(): (acc.astype(jnp.float32) + own(step).astype(jnp.float32)).astype(jnp.bflo...  14.4 us
    dot_general x3, matrix products, outer_sum(): lax.dot_general(left, right, (((0,), (0,)), ((), ())), preferred_element_...  12.7 us
    ppermute x6, starting transfers between devices, ring_reduce_scatter(): acc = lax.ppermute(acc, 'replica', perm)  8.85 us
    mul x3, local copies, waits for them, and re-layouts, per_device(): gate_probs[:, :, None] * out_cot[:, None, :].astype(jnp.float32)  7.34 us
  transfers between devices with their start and end apart: 10, of which 7 were waited for; matrix products, arithmetic and copies ran while one was open for 32% of the time, Pallas kernels for 0%

profile of v4, /device:TPU:1, one launch (start us, length us, event | category | flops | bytes accessed | tf_op | source)
XLA Modules:
  0.0 272.0 jit_solution(5836292256586765108)
XLA Ops:
  0.6 0.9 copy.29
  1.6 0.1 eq.76
  1.7 0.1 eq.80
  1.9 0.9 reduce-window.6
  2.8 0.2 slice_reduce_fusion
  3.0 0.1 fusion.64
  3.2 0.1 reduce_sum.24
  3.3 0.1 copy.32
  3.4 0.7 multiply_add_fusion
  4.1 0.1 fusion.59
  4.2 0.6 copy-done.11
  4.9 3.0 %fusion.19 = bf16[64,8,2048]{2,1,0:T(8,128)(2,1)} fusion(bf16[64,512]{1,0:T(8,128)(2,1)S(1)} %fusion.59, bf16[64,2048]{1,0:T(8,128)(2,1)} %param.7), kind=kOutput, calls=%fused_computation.38 | convolution fusion | flops 135266304 | bytes 2424832 | tf_op jit(solution)/shard_map/dot_general | solution.py:79
  7.9 13.3 %all-to-all-start = ((bf16[64,8,2048]{2,1,0:T(8,128)(2,1)}), bf16[64,8,2048]{2,1,0:T(8,128)(2,1)}, u32[]{:S(2)}, u32[]{:S(2)}) async-start(bf16[64,8,2048]{2,1,0:T(8,128)(2,1)} %fusion.19), calls=%async_computation | async-start | bytes 4194304 | tf_op jit(solution)/shard_map/all_to_all | solution.py:44
  21.2 2.5 mul.70
  23.6 4.7 %mul.71 = f32[384,2048]{1,0:T(8,128)} reshape(f32[64,6,2048]{2,1,0:T(8,128)} %mul.70) | data formatting | bytes 6291456 | tf_op jit(solution)/shard_map/mul | solution.py:81
  28.4 0.1 copy.33
  28.5 0.1 mul.68
  28.6 4.6 %fusion.20 = bf16[64,8,2048]{2,1,0:T(8,128)(2,1)} fusion(f32[384,2048]{1,0:T(8,128)} %mul.71, f32[384]{0:T(512)S(1)} %mul.68, s32[384]{0:T(512)S(1)} %multiply_add_fusion.1), kind=kOutput, calls=%fused_computation.39 | convolution fusion | flops 808124416 | bytes 5245952 | tf_op jit(solution)/shard_map/dot_general | solution.py:82
  33.2 39.1 %all-to-all-done = bf16[64,8,2048]{2,1,0:T(8,128)(2,1)} async-done(((bf16[64,8,2048]{2,1,0:T(8,128)(2,1)}), bf16[64,8,2048]{2,1,0:T(8,128)(2,1)}, u32[]{:S(2)}, u32[]{:S(2)}) %all-to-all-start) | async-done | bytes 2097184 | tf_op jit(solution)/shard_map/all_to_all | solution.py:44
  72.3 6.0 %all-to-all-start.2 = ((bf16[64,8,2048]{2,1,0:T(8,128)(2,1)}), bf16[64,8,2048]{2,1,0:T(8,128)(2,1)}, u32[]{:S(2)}, u32[]{:S(2)}) async-start(bf16[64,8,2048]{2,1,0:T(8,128)(2,1)} %fusion.20), calls=%async_computation.2 | async-start | bytes 4194304 | tf_op jit(solution)/shard_map/all_to_all | solution.py:44
  78.4 4.5 %fusion.12 = f32[512,768]{1,0:T(8,128)S(1)} fusion(bf16[1,2048,768]{2,1,0:T(8,128)(2,1)} %param.11, bf16[64,8,2048]{2,1,0:T(8,128)(2,1)} %all-to-all-done), kind=kOutput, calls=%fused_computation.32 | convolution fusion | flops 1610612736 | bytes 6815744 | tf_op jit(solution)/shard_map/dot_general | solution.py:16
  82.9 5.2 %multiply_convert_fusion.4 = (bf16[512,768]{1,0:T(8,128)(2,1)S(1)}, f32[512,768]{1,0:T(8,128)}) fusion(f32[512,768]{1,0:T(8,128)S(1)} %fusion.12, bf16[1,2048,768]{2,1,0:T(8,128)(2,1)S(1)} %copy-done.16, bf16[64,8,2048]{2,1,0:T(8,128)(2,1)} %all-to-all-done), kind=kOutput, calls=%fused_computation.67 | convolution fusion | flops 1612972032 | bytes 9175040 | tf_op jit(solution)/shard_map/dot_general | solution.py:17
  88.1 3.2 %fusion.14 = bf16[512,2048]{1,0:T(8,128)(2,1)} fusion(bf16[512,768]{1,0:T(8,128)(2,1)S(1)} %get-tuple-element.12, bf16[1,768,2048]{2,1,0:T(8,128)(2,1)S(1)} %copy-done), kind=kOutput, calls=%fused_computation.35 | convolution fusion | flops 1611661312 | bytes 6029312 | tf_op jit(solution)/shard_map/dot_general | solution.py:88
  91.3 38.3 %all-to-all-done.2 = bf16[64,8,2048]{2,1,0:T(8,128)(2,1)} async-done(((bf16[64,8,2048]{2,1,0:T(8,128)(2,1)}), bf16[64,8,2048]{2,1,0:T(8,128)(2,1)}, u32[]{:S(2)}, u32[]{:S(2)}) %all-to-all-start.2) | async-done | bytes 2097184 | tf_op jit(solution)/shard_map/all_to_all | solution.py:44
  129.5 6.0 %all-to-all-start.1 = ((bf16[64,8,2048]{2,1,0:T(8,128)(2,1)}), bf16[64,8,2048]{2,1,0:T(8,128)(2,1)}, u32[]{:S(2)}, u32[]{:S(2)}) async-start(bf16[64,8,2048]{2,1,0:T(8,128)(2,1)} %bitcast.145), calls=%async_computation.1 | async-start | bytes 4194304 | tf_op jit(solution)/shard_map/all_to_all | solution.py:44
  135.5 3.7 %convolution_convert_fusion.1 = bf16[768,2048]{1,0:T(8,128)(2,1)S(1)} fusion(bf16[512,768]{1,0:T(8,128)(2,1)} %copy-done.21, bf16[64,8,2048]{2,1,0:T(8,128)(2,1)} %all-to-all-done.2), kind=kOutput, calls=%fused_computation.20 | convolution fusion | flops 1612185600 | bytes 6029312 | tf_op jit(solution)/shard_map/dot_general | solution.py:38
  139.2 2.0 fusion.66
  141.2 3.9 %reshape.139 = bf16[4,256,768]{2,1,0:T(8,128)(2,1)} reshape(bf16[768,1024]{1,0:T(8,128)(2,1)} %get-tuple-element.14) | data formatting | bytes 3145728 | tf_op jit(solution)/shard_map/reshape | solution.py:110
  145.1 4.7 %multiply_convert_fusion.3 = (bf16[512,768]{1,0:T(8,128)(2,1)S(1)}, bf16[512,768]{1,0:T(8,128)(2,1)S(1)}) fusion(f32[512,768]{1,0:T(8,128)} %copy-done.22, f32[512,768]{1,0:T(8,128)} %get-tuple-element.10, bf16[1,768,2048]{2,1,0:T(8,128)(2,1)S(1)} %copy-done, bf16[64,8,2048]{2,1,0:T(8,128)(2,1)} %all-to-all-done.2), kind=kOutput, calls=%fused_computation.64 | convolution fusion | flops 1615724544 | bytes 9961472 | tf_op jit(solution)/shard_map/dot_general | solution.py:24
  149.9 4.0 %convolution_convert_fusion.2 = bf16[2048,768]{1,0:T(8,128)(2,1)S(1)} fusion(bf16[512,768]{1,0:T(8,128)(2,1)S(1)} %get-tuple-element.15, bf16[64,8,2048]{2,1,0:T(8,128)(2,1)} %all-to-all-done), kind=kOutput, calls=%fused_computation.21 | convolution fusion | flops 1612185600 | bytes 6029312 | tf_op jit(solution)/shard_map/dot_general | solution.py:38
  153.9 1.1 fusion.51
  155.0 1.3 collective-permute-start
  156.3 5.1 %convolution_convert_fusion = bf16[2048,768]{1,0:T(8,128)(2,1)} fusion(bf16[512,768]{1,0:T(8,128)(2,1)S(1)} %get-tuple-element.16, bf16[64,8,2048]{2,1,0:T(8,128)(2,1)} %all-to-all-done), kind=kOutput, calls=%fused_computation.19 | convolution fusion | flops 1612185600 | bytes 6029312 | tf_op jit(solution)/shard_map/dot_general | solution.py:38
  161.4 3.9 %reshape.141 = bf16[4,256,768]{2,1,0:T(8,128)(2,1)} reshape(bf16[768,1024]{1,0:T(8,128)(2,1)} %get-tuple-element.13) | data formatting | bytes 3145728 | tf_op jit(solution)/shard_map/reshape | solution.py:111
  165.3 2.3 fusion.43
  167.6 1.4 collective-permute-start.3
  169.1 4.1 %fusion.6 = f32[512,2048]{1,0:T(8,128)S(1)} fusion(bf16[512,768]{1,0:T(8,128)(2,1)} %copy-done.20, bf16[1,2048,768]{2,1,0:T(8,128)(2,1)} %param.12), kind=kOutput, calls=%fused_computation.26 | convolution fusion | flops 1610612736 | bytes 8126464 | tf_op jit(solution)/shard_map/dot_general | solution.py:31
  173.1 10.3 %collective-permute-done = bf16[768,768]{1,0:T(8,128)(2,1)} collective-permute-done((bf16[768,768]{1,0:T(8,128)(2,1)}, bf16[768,768]{1,0:T(8,128)(2,1)}, u32[]{:S(2)}, u32[]{:S(2)}) %collective-permute-start) | collective-permute-done | bytes 1179680 | tf_op jit(solution)/shard_map/ppermute | solution.py:58
  183.5 2.6 fusion.29
  186.1 8.3 %collective-permute-done.3 = bf16[768,768]{1,0:T(8,128)(2,1)} collective-permute-done((bf16[768,768]{1,0:T(8,128)(2,1)}, bf16[768,768]{1,0:T(8,128)(2,1)}, u32[]{:S(2)}, u32[]{:S(2)}) %collective-permute-start.3) | collective-permute-done | bytes 1179680 | tf_op jit(solution)/shard_map/ppermute | solution.py:58
  194.4 2.7 fusion.26
  197.1 2.7 collective-permute-start.4
  199.8 3.3 %fusion.21 = bf16[64,8,2048]{2,1,0:T(8,128)(2,1)} fusion(f32[512,2048]{1,0:T(8,128)S(1)} %fusion.6, bf16[512,768]{1,0:T(8,128)(2,1)S(1)} %copy-done.19, bf16[1,2048,768]{2,1,0:T(8,128)(2,1)S(1)} %copy-done.17), kind=kOutput, calls=%fused_computation.40 | convolution fusion | flops 1612709888 | bytes 10223616 | tf_op jit(solution)/shard_map/dot_general | solution.py:30
  203.1 12.3 %all-to-all-start.3 = ((bf16[64,8,2048]{2,1,0:T(8,128)(2,1)}), bf16[64,8,2048]{2,1,0:T(8,128)(2,1)}, u32[]{:S(2)}, u32[]{:S(2)}) async-start(bf16[64,8,2048]{2,1,0:T(8,128)(2,1)} %fusion.21), calls=%async_computation.3 | async-start | bytes 4194304 | tf_op jit(solution)/shard_map/all_to_all | solution.py:44
  215.4 8.2 %collective-permute-done.4 = bf16[768,768]{1,0:T(8,128)(2,1)} collective-permute-done((bf16[768,768]{1,0:T(8,128)(2,1)}, bf16[768,768]{1,0:T(8,128)(2,1)}, u32[]{:S(2)}, u32[]{:S(2)}) %collective-permute-start.4) | collective-permute-done | bytes 1179680 | tf_op jit(solution)/shard_map/ppermute | solution.py:58
  223.5 2.9 %fusion.25 = bf16[768,768]{1,0:T(8,128)(2,1)} fusion(bf16[768,768]{1,0:T(8,128)(2,1)} %collective-permute-done.4, s32[]{:T(128)S(6)} %select_n.73, bf16[4,512,768]{2,1,0:T(8,128)(2,1)} %bitcast.142, bf16[4,256,768]{2,1,0:T(8,128)(2,1)} %reshape.141), kind=kLoop, calls=%fused_computation.44 | loop fusion | flops 4718592 | bytes 7077892 | tf_op jit(solution)/shard_map/convert_element_type | solution.py:59
  226.4 3.4 %collective-permute-start.5 = (bf16[768,768]{1,0:T(8,128)(2,1)}, bf16[768,768]{1,0:T(8,128)(2,1)}, u32[]{:S(2)}, u32[]{:S(2)}) collective-permute-start(bf16[768,768]{1,0:T(8,128)(2,1)} %fusion.25), channel_id=1, source_target_pairs={{0,3},{1,0},{2,1},{3,2},{4,7},{5,4},{6,5},{7,6},{8,11},{9,8},{10,9... | collective-permute-start | bytes 3538952 | tf_op jit(solution)/shard_map/ppermute | solution.py:58
  229.8 2.7 fusion.28
  232.5 0.7 copy.35
  233.3 19.4 %collective-permute-done.5 = bf16[768,768]{1,0:T(8,128)(2,1)} collective-permute-done((bf16[768,768]{1,0:T(8,128)(2,1)}, bf16[768,768]{1,0:T(8,128)(2,1)}, u32[]{:S(2)}, u32[]{:S(2)}) %collective-permute-start.5) | collective-permute-done | bytes 1179680 | tf_op jit(solution)/shard_map/ppermute | solution.py:58
  252.7 1.9 fusion.24
  254.6 1.0 copy-done.6
  255.6 1.1 reshape.143
  256.7 1.8 collective-permute-done.2
  258.5 1.6 fusion.27
  260.1 1.1 copy-done.8
  261.2 0.3 reshape.142
  261.6 0.9 maximum_bitcast_fusion
  262.5 0.9 slice_bitcast_fusion.1
  263.5 0.9 slice_bitcast_fusion
  264.4 2.6 fusion.30
  267.1 1.3 fusion
  268.4 0.9 copy.42
  269.3 2.8 %convolution_convert_fusion.5 = bf16[64,2048]{1,0:T(8,128)(2,1)} fusion(bf16[64,512]{1,0:T(8,128)(2,1)S(1)} %copy-done.12, bf16[64,8,2048]{2,1,0:T(8,128)(2,1)} %all-to-all-done.3), kind=kOutput, calls=%fused_computation.53 | convolution fusion | flops 134348800 | bytes 2424832 | tf_op jit(solution)/shard_map/dot_general | solution.py:102
  (53 shorter events, 0.2 us)
Async XLA Ops:
  0.6 87.5 %copy-start = (bf16[1,768,2048]{2,1,0:T(8,128)(2,1)S(1)}, bf16[1,768,2048]{2,1,0:T(8,128)(2,1)}, u32[]{:S(2)}) copy-start(bf16[1,768,2048]{2,1,0:T(8,128)(2,1)} %param.13) | copy-start | bytes 9437188
  4.2 0.6 copy-start.11
  7.9 13.3 %copy-start.13 = (bf16[64,2048]{1,0:T(8,128)(2,1)S(1)}, bf16[64,2048]{1,0:T(8,128)(2,1)}, u32[]{:S(2)}) copy-start(bf16[64,2048]{1,0:T(8,128)(2,1)} %param.10) | copy-start | bytes 786436
  7.9 64.5 %all-to-all-start = ((bf16[64,8,2048]{2,1,0:T(8,128)(2,1)}), bf16[64,8,2048]{2,1,0:T(8,128)(2,1)}, u32[]{:S(2)}, u32[]{:S(2)}) async-start(bf16[64,8,2048]{2,1,0:T(8,128)(2,1)} %fusion.19), calls=%async_computation | async-start | bytes 4194304 | tf_op jit(solution)/shard_map/all_to_all | solution.py:44
  23.6 4.7 %copy-start.15 = (f32[64,6]{0,1:T(8,128)S(1)}, f32[64,6]{0,1:T(8,128)}, u32[]{:S(2)}) copy-start(f32[64,6]{0,1:T(8,128)} %param.9) | copy-start | bytes 4612
  72.3 57.2 %all-to-all-start.2 = ((bf16[64,8,2048]{2,1,0:T(8,128)(2,1)}), bf16[64,8,2048]{2,1,0:T(8,128)(2,1)}, u32[]{:S(2)}, u32[]{:S(2)}) async-start(bf16[64,8,2048]{2,1,0:T(8,128)(2,1)} %fusion.20), calls=%async_computation.2 | async-start | bytes 4194304 | tf_op jit(solution)/shard_map/all_to_all | solution.py:44
  78.4 4.5 %copy-start.16 = (bf16[1,2048,768]{2,1,0:T(8,128)(2,1)S(1)}, bf16[1,2048,768]{2,1,0:T(8,128)(2,1)}, u32[]{:S(2)}) copy-start(bf16[1,2048,768]{2,1,0:T(8,128)(2,1)} %param.12) | copy-start | bytes 9437188
  82.9 5.2 %copy-start.22 = (f32[512,768]{1,0:T(8,128)}, f32[512,768]{1,0:T(8,128)S(1)}, u32[]{:S(2)}) copy-start(f32[512,768]{1,0:T(8,128)S(1)} %fusion.12) | copy-start | bytes 4718596
  88.1 3.2 %copy-start.21 = (bf16[512,768]{1,0:T(8,128)(2,1)}, bf16[512,768]{1,0:T(8,128)(2,1)S(1)}, u32[]{:S(2)}) copy-start(bf16[512,768]{1,0:T(8,128)(2,1)S(1)} %get-tuple-element.12) | copy-start | bytes 2359300
  129.5 73.5 %all-to-all-start.1 = ((bf16[64,8,2048]{2,1,0:T(8,128)(2,1)}), bf16[64,8,2048]{2,1,0:T(8,128)(2,1)}, u32[]{:S(2)}, u32[]{:S(2)}) async-start(bf16[64,8,2048]{2,1,0:T(8,128)(2,1)} %bitcast.145), calls=%async_computation.1 | async-start | bytes 4194304 | tf_op jit(solution)/shard_map/all_to_all | solution.py:44
  149.8 4.1 %copy-start.18 = (bf16[512,768]{1,0:T(8,128)(2,1)}, bf16[512,768]{1,0:T(8,128)(2,1)S(1)}, u32[]{:S(2)}) copy-start(bf16[512,768]{1,0:T(8,128)(2,1)S(1)} %get-tuple-element.15) | copy-start | bytes 2359300
  149.8 6.5 %copy-start.20 = (bf16[512,768]{1,0:T(8,128)(2,1)}, bf16[512,768]{1,0:T(8,128)(2,1)S(1)}, u32[]{:S(2)}) copy-start(bf16[512,768]{1,0:T(8,128)(2,1)S(1)} %get-tuple-element.16) | copy-start | bytes 2359300
  149.8 4.0 %copy-start.3 = (bf16[4,256,768]{2,1,0:T(8,128)(2,1)S(1)}, bf16[4,256,768]{2,1,0:T(8,128)(2,1)}, u32[]{:S(2)}) copy-start(bf16[4,256,768]{2,1,0:T(8,128)(2,1)} %reshape.139) | copy-start | bytes 4718596
  155.0 28.5 %collective-permute-start = (bf16[768,768]{1,0:T(8,128)(2,1)}, bf16[768,768]{1,0:T(8,128)(2,1)}, u32[]{:S(2)}, u32[]{:S(2)}) collective-permute-start(bf16[768,768]{1,0:T(8,128)(2,1)} %fusion.51), channel_id=1, source_target_pairs={{0,1},{1,2},{2,3},{3,0},{4,5},{5,6},{6,7},{7,4},{8,9},{9,10},{10,1... | collective-permute-start | bytes 3538952 | tf_op jit(solution)/shard_map/ppermute | solution.py:58
  167.6 26.8 %collective-permute-start.3 = (bf16[768,768]{1,0:T(8,128)(2,1)}, bf16[768,768]{1,0:T(8,128)(2,1)}, u32[]{:S(2)}, u32[]{:S(2)}) collective-permute-start(bf16[768,768]{1,0:T(8,128)(2,1)} %fusion.43), channel_id=1, source_target_pairs={{0,3},{1,0},{2,1},{3,2},{4,7},{5,4},{6,5},{7,6},{8,11},{9,8},{10,9... | collective-permute-start | bytes 3538952 | tf_op jit(solution)/shard_map/ppermute | solution.py:58
  169.0 14.4 %copy-start.4 = (bf16[4,256,768]{2,1,0:T(8,128)(2,1)S(1)}, bf16[4,256,768]{2,1,0:T(8,128)(2,1)}, u32[]{:S(2)}) copy-start(bf16[4,256,768]{2,1,0:T(8,128)(2,1)} %reshape.139) | copy-start | bytes 4718596
  173.1 21.3 %copy-start.2 = (bf16[2048,768]{1,0:T(8,128)(2,1)S(1)}, bf16[2048,768]{1,0:T(8,128)(2,1)}, u32[]{:S(2)}) copy-start(bf16[2048,768]{1,0:T(8,128)(2,1)} %convolution_convert_fusion) | copy-start | bytes 9437188
  173.1 21.3 %copy-start.5 = (bf16[4,256,768]{2,1,0:T(8,128)(2,1)S(1)}, bf16[4,256,768]{2,1,0:T(8,128)(2,1)}, u32[]{:S(2)}) copy-start(bf16[4,256,768]{2,1,0:T(8,128)(2,1)} %reshape.141) | copy-start | bytes 4718596
  186.1 13.7 %copy-start.17 = (bf16[1,2048,768]{2,1,0:T(8,128)(2,1)S(1)}, bf16[1,2048,768]{2,1,0:T(8,128)(2,1)}, u32[]{:S(2)}) copy-start(bf16[1,2048,768]{2,1,0:T(8,128)(2,1)} %param.11) | copy-start | bytes 9437188
  186.1 13.7 %copy-start.19 = (bf16[512,768]{1,0:T(8,128)(2,1)S(1)}, bf16[512,768]{1,0:T(8,128)(2,1)}, u32[]{:S(2)}) copy-start(bf16[512,768]{1,0:T(8,128)(2,1)} %copy-done.18) | copy-start | bytes 2359300
  186.1 43.8 %collective-permute-start.1 = (bf16[768,768]{1,0:T(8,128)(2,1)}, bf16[768,768]{1,0:T(8,128)(2,1)}, u32[]{:S(2)}, u32[]{:S(2)}) collective-permute-start(bf16[768,768]{1,0:T(8,128)(2,1)} %fusion.29), channel_id=1, source_target_pairs={{0,1},{1,2},{2,3},{3,0},{4,5},{5,6},{6,7},{7,4},{8,9},{9,10},{10,1... | collective-permute-start | bytes 3538952 | tf_op jit(solution)/shard_map/ppermute | solution.py:58
  197.1 26.4 %collective-permute-start.4 = (bf16[768,768]{1,0:T(8,128)(2,1)}, bf16[768,768]{1,0:T(8,128)(2,1)}, u32[]{:S(2)}, u32[]{:S(2)}) collective-permute-start(bf16[768,768]{1,0:T(8,128)(2,1)} %fusion.26), channel_id=1, source_target_pairs={{0,3},{1,0},{2,1},{3,2},{4,7},{5,4},{6,5},{7,6},{8,11},{9,8},{10,9... | collective-permute-start | bytes 3538952 | tf_op jit(solution)/shard_map/ppermute | solution.py:58
  203.1 66.2 %all-to-all-start.3 = ((bf16[64,8,2048]{2,1,0:T(8,128)(2,1)}), bf16[64,8,2048]{2,1,0:T(8,128)(2,1)}, u32[]{:S(2)}, u32[]{:S(2)}) async-start(bf16[64,8,2048]{2,1,0:T(8,128)(2,1)} %fusion.21), calls=%async_computation.3 | async-start | bytes 4194304 | tf_op jit(solution)/shard_map/all_to_all | solution.py:44
  226.4 26.2 %collective-permute-start.5 = (bf16[768,768]{1,0:T(8,128)(2,1)}, bf16[768,768]{1,0:T(8,128)(2,1)}, u32[]{:S(2)}, u32[]{:S(2)}) collective-permute-start(bf16[768,768]{1,0:T(8,128)(2,1)} %fusion.25), channel_id=1, source_target_pairs={{0,3},{1,0},{2,1},{3,2},{4,7},{5,4},{6,5},{7,6},{8,11},{9,8},{10,9... | collective-permute-start | bytes 3538952 | tf_op jit(solution)/shard_map/ppermute | solution.py:58
  232.5 26.0 %collective-permute-start.2 = (bf16[768,768]{1,0:T(8,128)(2,1)}, bf16[768,768]{1,0:T(8,128)(2,1)}, u32[]{:S(2)}, u32[]{:S(2)}) collective-permute-start(bf16[768,768]{1,0:T(8,128)(2,1)} %fusion.28), channel_id=1, source_target_pairs={{0,1},{1,2},{2,3},{3,0},{4,5},{5,6},{6,7},{7,4},{8,9},{9,10},{10,1... | collective-permute-start | bytes 3538952 | tf_op jit(solution)/shard_map/ppermute | solution.py:58
  254.5 1.0 copy-start.6
  256.7 4.9 %copy-start.10 = (bf16[192,1024]{1,0:T(8,128)(2,1)S(1)}, bf16[192,1024]{1,0:T(8,128)(2,1)}, u32[]{:S(2)}) copy-start(bf16[192,1024]{1,0:T(8,128)(2,1)} %reshape.143) | copy-start | bytes 1179652
  260.1 1.1 copy-start.8
  261.2 1.3 copy-start.9
  261.2 2.2 copy-start.7
  264.4 2.6 copy-start.14
  267.0 2.2 copy-start.12
  267.0 5.0 %copy-start.1 = (bf16[1,768,2048]{2,1,0:T(8,128)(2,1)S(1)}, bf16[1,768,2048]{2,1,0:T(8,128)(2,1)}, u32[]{:S(2)}) copy-start(bf16[1,768,2048]{2,1,0:T(8,128)(2,1)} %param.13) | copy-start | bytes 9437188

commit v5 on v4

--- a/solution.py
+++ b/solution.py
@@ -95,13 +95,7 @@
     back_rows, d_gate, d_up = backward_rows(
         grads_in, pre_gate, pre_up, gate_weight, up_weight, down_weight
     )
-    returned_grad = exchange(back_rows.reshape(experts, capacity, features)).reshape(-1, features)
 
-    picked = jnp.einsum("tkp,pd->tkd", pick3, returned, preferred_element_type=jnp.float32)
-    combined = jnp.einsum("tk,tkd->td", gate_probs, picked).astype(jnp.bfloat16)
-    grad_tokens = jnp.dot(owner, returned_grad, preferred_element_type=jnp.float32).astype(
-        jnp.bfloat16
-    )
     replicas = lax.axis_size("replica")
     half = features // 2
     part_down = outer_sum(activation, grads_in).astype(jnp.bfloat16)
@@ -110,17 +104,25 @@
         part_down[:, :half].reshape(replicas, down_rows * half // hidden, hidden),
         part_down[:, half:].reshape(replicas, down_rows * half // hidden, hidden),
     ]
-    sums = []
-    for direction, wide, down_half in zip((1, -1), (d_gate, d_up), down_halves):
+    tables = []
+    for wide, down_half in zip((d_gate, d_up), down_halves):
         part = outer_sum(slot_rows, wide).astype(jnp.bfloat16)
         table = jnp.concatenate([part.reshape(replicas, -1, hidden), down_half], axis=1)
-        sums.append(ring_reduce_scatter(table.reshape(-1, hidden), direction))
+        tables.append(table.reshape(-1, hidden))
+    tables, back_rows = lax.optimization_barrier((tables, back_rows))
+    returned_grad = exchange(back_rows.reshape(experts, capacity, features)).reshape(-1, features)
+    sums = [ring_reduce_scatter(table, direction) for direction, table in zip((1, -1), tables)]
     rows = features // replicas
     grad_gate = sums[0][:rows][None]
     grad_up = sums[1][:rows][None]
     grad_down = jnp.concatenate(
         [sums[0][rows:].reshape(down_rows, half), sums[1][rows:].reshape(down_rows, half)], axis=1
     )[None]
+    picked = jnp.einsum("tkp,pd->tkd", pick3, returned, preferred_element_type=jnp.float32)
+    combined = jnp.einsum("tk,tkd->td", gate_probs, picked).astype(jnp.bfloat16)
+    grad_tokens = jnp.dot(owner, returned_grad, preferred_element_type=jnp.float32).astype(
+        jnp.bfloat16
+    )
     return (combined, grad_tokens, grad_gate, grad_up, grad_down)
 
 

time: 277 us -> 280 us (1.011)
  waiting for transfers between devices: 125 us -> 133 us
    ppermute x6, waiting for transfers between devices: 48.1 us -> 55.7 us  [ring_reduce_scatter(): acc = lax.ppermute(acc, 'replica', perm)]
    concatenate x0 -> x2, other arithmetic: none -> 4.69 us  [per_device(): jnp.concatenate([part.reshape(replicas, -1, hidden), down_half], axis=1)]
    squeeze x2 -> x0, other arithmetic: 3.44 us -> none  [own(): lax.dynamic_index_in_dim(table, (me - direction * (step + 1)) % n, 0, False)]
    convert_element_type x6, other arithmetic: 14.4 us -> 11.4 us  [ring_reduce_scatter(): (acc.astype(jnp.float32) + own(step).astype(jnp.float32)).astype(jnp.bflo...]
    unnamed x49 -> x39, local copies, waits for them, and re-layouts: 4.55 us -> 5.98 us
  transfers between devices with their start and end apart: 10 -> 10, of which waited for: 7 -> 6; matrix products, arithmetic and copies ran while one was open for 32% -> 29% of each run, Pallas kernels for 0% -> 0%
where the time goes in v5:
time: 280 us; the launch traced here: 276 us
  waiting for transfers between devices  133 us (48%)
  matrix products  49.6 us (18%)
  starting transfers between devices  47.9 us (17%)
  local copies, waits for them, and re-layouts  24.9 us (9%)
  other arithmetic  19 us (7%)
    all_to_all x4, waiting for transfers between devices, exchange(): lax.all_to_all(blocks, 'expert', split_axis=0, concat_axis=0, tiled=True)  77.4 us
    ppermute x6, waiting for transfers between devices, ring_reduce_scatter(): acc = lax.ppermute(acc, 'replica', perm)  55.7 us
    all_to_all x4, starting transfers between devices, exchange(): lax.all_to_all(blocks, 'expert', split_axis=0, concat_axis=0, tiled=True)  37.3 us
    dot_general x3, matrix products, outer_sum(): lax.dot_general(left, right, (((0,), (0,)), ((), ())), preferred_element_...  12.6 us
    convert_element_type x6, other arithmetic, ring_reduce_scatter(): (acc.astype(jnp.float32) + own(step).astype(jnp.float32)).astype(jnp.bflo...  11.4 us
    ppermute x6, starting transfers between devices, ring_reduce_scatter(): acc = lax.ppermute(acc, 'replica', perm)  10.5 us
    mul x3, local copies, waits for them, and re-layouts, per_device(): gate_probs[:, :, None] * out_cot[:, None, :].astype(jnp.float32)  7.34 us
    unnamed x39, local copies, waits for them, and re-layouts  5.98 us
  transfers between devices with their start and end apart: 10, of which 6 were waited for; matrix products, arithmetic and copies ran while one was open for 29% of the time, Pallas kernels for 0%

profile of v5, /device:TPU:1, one launch (start us, length us, event | category | flops | bytes accessed | tf_op | source)
XLA Modules:
  0.0 275.6 jit_solution(14966576977071597981)
XLA Ops:
  0.6 0.9 copy.29
  1.6 0.1 eq.76
  1.7 0.1 eq.80
  1.9 0.9 reduce-window.6
  2.8 0.2 slice_reduce_fusion
  3.0 0.1 fusion.45
  3.2 0.1 reduce_sum.24
  3.4 0.7 multiply_add_fusion
  4.1 0.1 fusion.40
  4.2 0.6 copy-done.3
  4.9 3.1 %fusion.19 = bf16[64,8,2048]{2,1,0:T(8,128)(2,1)} fusion(bf16[64,512]{1,0:T(8,128)(2,1)S(1)} %fusion.40, bf16[64,2048]{1,0:T(8,128)(2,1)} %param.7), kind=kOutput, calls=%fused_computation.24 | convolution fusion | flops 135266304 | bytes 2424832 | tf_op jit(solution)/shard_map/dot_general | solution.py:79
  8.0 13.3 %all-to-all-start = ((bf16[64,8,2048]{2,1,0:T(8,128)(2,1)}), bf16[64,8,2048]{2,1,0:T(8,128)(2,1)}, u32[]{:S(2)}, u32[]{:S(2)}) async-start(bf16[64,8,2048]{2,1,0:T(8,128)(2,1)} %fusion.19), calls=%async_computation | async-start | bytes 4194304 | tf_op jit(solution)/shard_map/all_to_all | solution.py:44
  21.3 2.5 mul.70
  23.7 4.7 %mul.71 = f32[384,2048]{1,0:T(8,128)} reshape(f32[64,6,2048]{2,1,0:T(8,128)} %mul.70) | data formatting | bytes 6291456 | tf_op jit(solution)/shard_map/mul | solution.py:81
  28.5 0.1 copy.33
  28.6 0.1 mul.68
  28.7 4.6 %fusion.20 = bf16[64,8,2048]{2,1,0:T(8,128)(2,1)} fusion(f32[384,2048]{1,0:T(8,128)} %mul.71, f32[384]{0:T(512)S(1)} %mul.68, s32[384]{0:T(512)S(1)} %multiply_add_fusion.1), kind=kOutput, calls=%fused_computation.25 | convolution fusion | flops 808124416 | bytes 5245952 | tf_op jit(solution)/shard_map/dot_general | solution.py:82
  33.3 39.1 %all-to-all-done = bf16[64,8,2048]{2,1,0:T(8,128)(2,1)} async-done(((bf16[64,8,2048]{2,1,0:T(8,128)(2,1)}), bf16[64,8,2048]{2,1,0:T(8,128)(2,1)}, u32[]{:S(2)}, u32[]{:S(2)}) %all-to-all-start) | async-done | bytes 2097184 | tf_op jit(solution)/shard_map/all_to_all | solution.py:44
  72.4 6.0 %all-to-all-start.2 = ((bf16[64,8,2048]{2,1,0:T(8,128)(2,1)}), bf16[64,8,2048]{2,1,0:T(8,128)(2,1)}, u32[]{:S(2)}, u32[]{:S(2)}) async-start(bf16[64,8,2048]{2,1,0:T(8,128)(2,1)} %fusion.20), calls=%async_computation.2 | async-start | bytes 4194304 | tf_op jit(solution)/shard_map/all_to_all | solution.py:44
  78.5 4.5 %fusion.12 = f32[512,768]{1,0:T(8,128)S(1)} fusion(bf16[1,2048,768]{2,1,0:T(8,128)(2,1)} %param.11, bf16[64,8,2048]{2,1,0:T(8,128)(2,1)} %all-to-all-done), kind=kOutput, calls=%fused_computation.18 | convolution fusion | flops 1610612736 | bytes 6815744 | tf_op jit(solution)/shard_map/dot_general | solution.py:16
  83.0 5.2 %multiply_convert_fusion.4 = (bf16[512,768]{1,0:T(8,128)(2,1)S(1)}, f32[512,768]{1,0:T(8,128)}) fusion(f32[512,768]{1,0:T(8,128)S(1)} %fusion.12, bf16[1,2048,768]{2,1,0:T(8,128)(2,1)S(1)} %copy-done.8, bf16[64,8,2048]{2,1,0:T(8,128)(2,1)} %all-to-all-done), kind=kOutput, calls=%fused_computation.52 | convolution fusion | flops 1612972032 | bytes 9175040 | tf_op jit(solution)/shard_map/dot_general | solution.py:17
  88.2 3.2 %fusion.14 = bf16[512,2048]{1,0:T(8,128)(2,1)} fusion(bf16[512,768]{1,0:T(8,128)(2,1)S(1)} %get-tuple-element.15, bf16[1,768,2048]{2,1,0:T(8,128)(2,1)S(1)} %copy-done), kind=kOutput, calls=%fused_computation.21 | convolution fusion | flops 1611661312 | bytes 6029312 | tf_op jit(solution)/shard_map/dot_general | solution.py:88
  91.3 38.3 %all-to-all-done.2 = bf16[64,8,2048]{2,1,0:T(8,128)(2,1)} async-done(((bf16[64,8,2048]{2,1,0:T(8,128)(2,1)}), bf16[64,8,2048]{2,1,0:T(8,128)(2,1)}, u32[]{:S(2)}, u32[]{:S(2)}) %all-to-all-start.2) | async-done | bytes 2097184 | tf_op jit(solution)/shard_map/all_to_all | solution.py:44
  129.6 6.0 %all-to-all-start.1 = ((bf16[64,8,2048]{2,1,0:T(8,128)(2,1)}), bf16[64,8,2048]{2,1,0:T(8,128)(2,1)}, u32[]{:S(2)}, u32[]{:S(2)}) async-start(bf16[64,8,2048]{2,1,0:T(8,128)(2,1)} %bitcast.128), calls=%async_computation.1 | async-start | bytes 4194304 | tf_op jit(solution)/shard_map/all_to_all | solution.py:44
  135.7 3.8 %convolution_convert_fusion.1 = bf16[768,2048]{1,0:T(8,128)(2,1)S(1)} fusion(bf16[512,768]{1,0:T(8,128)(2,1)} %copy-done.14, bf16[64,8,2048]{2,1,0:T(8,128)(2,1)} %all-to-all-done.2), kind=kOutput, calls=%fused_computation.6 | convolution fusion | flops 1612185600 | bytes 6029312 | tf_op jit(solution)/shard_map/dot_general | solution.py:38
  139.5 4.7 %multiply_convert_fusion.2 = (bf16[512,768]{1,0:T(8,128)(2,1)}, bf16[512,768]{1,0:T(8,128)(2,1)S(1)}) fusion(f32[512,768]{1,0:T(8,128)S(1)} %copy-done.16, f32[512,768]{1,0:T(8,128)S(1)} %copy-done.17, bf16[1,768,2048]{2,1,0:T(8,128)(2,1)S(1)} %copy-done, bf16[64,8,2048]{2,1,0:T(8,128)(2,1)} %all-to-all-done.2), kind=kOutput, calls=%fused_computation.48 | convolution fusion | flops 1615724544 | bytes 9961472 | tf_op jit(solution)/shard_map/dot_general | solution.py:24
  144.2 5.3 %convolution_convert_fusion.2 = bf16[2048,768]{1,0:T(8,128)(2,1)} fusion(bf16[512,768]{1,0:T(8,128)(2,1)S(1)} %get-tuple-element.20, bf16[64,8,2048]{2,1,0:T(8,128)(2,1)} %all-to-all-done), kind=kOutput, calls=%fused_computation.7 | convolution fusion | flops 1612185600 | bytes 6029312 | tf_op jit(solution)/shard_map/dot_general | solution.py:38
  149.5 1.6 fusion.47
  151.1 1.2 reshape.149
  152.4 3.2 %reshape.152 = bf16[4,256,768]{2,1,0:T(8,128)(2,1)S(1)} reshape(bf16[768,1024]{1,0:T(8,128)(2,1)} %get-tuple-element.21) | data formatting | bytes 3145728 | tf_op jit(solution)/shard_map/reshape | solution.py:105
  155.6 4.4 %pad_maximum_fusion = bf16[4,768,768]{2,1,0:T(8,128)(2,1)} fusion(bf16[4,256,768]{2,1,0:T(8,128)(2,1)S(1)} %reshape.149, bf16[4,512,768]{2,1,0:T(8,128)(2,1)} %bitcast.126), kind=kLoop, calls=%fused_computation | loop fusion | flops 9437184 | bytes 9437184 | tf_op jit(solution)/shard_map/concatenate | solution.py:110
  159.9 3.4 %convolution_convert_fusion = bf16[2048,768]{1,0:T(8,128)(2,1)S(1)} fusion(bf16[512,768]{1,0:T(8,128)(2,1)S(1)} %copy-done.13, bf16[64,8,2048]{2,1,0:T(8,128)(2,1)} %all-to-all-done), kind=kOutput, calls=%fused_computation.5 | convolution fusion | flops 1612185600 | bytes 6029312 | tf_op jit(solution)/shard_map/dot_general | solution.py:38
  163.4 0.3 pad_maximum_fusion.1
  163.7 1.6 copy-done.9
  165.3 1.8 fusion.6
  167.1 1.8 copy-done.10
  168.9 0.2 copy-done.12
  169.1 3.3 %add_convert_fusion = bf16[512,2048]{1,0:T(8,128)(2,1)} fusion(f32[512,2048]{1,0:T(8,128)S(1)} %fusion.6, bf16[512,768]{1,0:T(8,128)(2,1)S(1)} %copy-done.12, bf16[1,2048,768]{2,1,0:T(8,128)(2,1)S(1)} %copy-done.10), kind=kOutput, calls=%fused_computation.4 | convolution fusion | flops 1612709888 | bytes 10223616 | tf_op jit(solution)/shard_map/dot_general | solution.py:30
  172.4 2.8 %collective-permute-start.3 = (bf16[768,768]{1,0:T(8,128)(2,1)S(1)}, bf16[768,768]{1,0:T(8,128)(2,1)}, u32[]{:S(2)}, u32[]{:S(2)}) collective-permute-start(bf16[768,768]{1,0:T(8,128)(2,1)S(1)} %dynamic-slice_bitcast_fusion), channel_id=1, source_target_pairs={{0,3},{1,0},{2,1},{3,2},{4,7},{5,4},{6,5},{7,6},{8,11},{9,8},{10,9... | collective-permute-start | bytes 3538952 | tf_op jit(solution)/shard_map/ppermute | solution.py:58
  175.2 1.3 dynamic-slice_bitcast_fusion.1
  176.7 23.1 %collective-permute-done.3 = bf16[768,768]{1,0:T(8,128)(2,1)} collective-permute-done((bf16[768,768]{1,0:T(8,128)(2,1)S(1)}, bf16[768,768]{1,0:T(8,128)(2,1)}, u32[]{:S(2)}, u32[]{:S(2)}) %collective-permute-start.3) | collective-permute-done | bytes 1179680 | tf_op jit(solution)/shard_map/ppermute | solution.py:58
  199.9 1.9 fusion.23
  201.8 3.6 %collective-permute-start.4 = (bf16[768,768]{1,0:T(8,128)(2,1)S(1)}, bf16[768,768]{1,0:T(8,128)(2,1)}, u32[]{:S(2)}, u32[]{:S(2)}) collective-permute-start(bf16[768,768]{1,0:T(8,128)(2,1)S(1)} %fusion.23), channel_id=1, source_target_pairs={{0,3},{1,0},{2,1},{3,2},{4,7},{5,4},{6,5},{7,6},{8,11},{9,8},{10,9... | collective-permute-start | bytes 3538952 | tf_op jit(solution)/shard_map/ppermute | solution.py:58
  205.4 1.9 fusion.26
  207.4 12.0 %all-to-all-start.3 = ((bf16[64,8,2048]{2,1,0:T(8,128)(2,1)}), bf16[64,8,2048]{2,1,0:T(8,128)(2,1)}, u32[]{:S(2)}, u32[]{:S(2)}) async-start(bf16[64,8,2048]{2,1,0:T(8,128)(2,1)} %bitcast.18), calls=%async_computation.3 | async-start | bytes 4194304 | tf_op jit(solution)/shard_map/all_to_all | solution.py:44
  219.4 9.6 %collective-permute-done.4 = bf16[768,768]{1,0:T(8,128)(2,1)} collective-permute-done((bf16[768,768]{1,0:T(8,128)(2,1)S(1)}, bf16[768,768]{1,0:T(8,128)(2,1)}, u32[]{:S(2)}, u32[]{:S(2)}) %collective-permute-start.4) | collective-permute-done | bytes 1179680 | tf_op jit(solution)/shard_map/ppermute | solution.py:58
  229.1 1.9 fusion.22
  231.0 3.6 %collective-permute-start.5 = (bf16[768,768]{1,0:T(8,128)(2,1)S(1)}, bf16[768,768]{1,0:T(8,128)(2,1)}, u32[]{:S(2)}, u32[]{:S(2)}) collective-permute-start(bf16[768,768]{1,0:T(8,128)(2,1)S(1)} %fusion.22), channel_id=1, source_target_pairs={{0,3},{1,0},{2,1},{3,2},{4,7},{5,4},{6,5},{7,6},{8,11},{9,8},{10,9... | collective-permute-start | bytes 3538952 | tf_op jit(solution)/shard_map/ppermute | solution.py:58
  234.6 1.9 fusion.25
  236.5 0.3 collective-permute-start.2
  236.9 0.7 copy.35
  237.6 19.7 %collective-permute-done.5 = bf16[768,768]{1,0:T(8,128)(2,1)} collective-permute-done((bf16[768,768]{1,0:T(8,128)(2,1)S(1)}, bf16[768,768]{1,0:T(8,128)(2,1)}, u32[]{:S(2)}, u32[]{:S(2)}) %collective-permute-start.5) | collective-permute-done | bytes 1179680 | tf_op jit(solution)/shard_map/ppermute | solution.py:58
  257.3 1.9 fusion.21
  259.3 0.3 reshape.159
  259.6 3.2 %collective-permute-done.2 = bf16[768,768]{1,0:T(8,128)(2,1)} collective-permute-done((bf16[768,768]{1,0:T(8,128)(2,1)S(1)}, bf16[768,768]{1,0:T(8,128)(2,1)}, u32[]{:S(2)}, u32[]{:S(2)}) %collective-permute-start.2) | collective-permute-done | bytes 1179680 | tf_op jit(solution)/shard_map/ppermute | solution.py:58
  262.8 1.9 fusion.24
  264.8 0.3 reshape.158
  265.1 0.9 maximum_bitcast_fusion
  266.0 0.9 slice_bitcast_fusion.1
  267.0 0.9 slice_bitcast_fusion
  267.9 2.6 fusion.27
  270.6 1.3 fusion
  271.9 0.9 copy.42
  272.8 2.8 %convolution_convert_fusion.5 = bf16[64,2048]{1,0:T(8,128)(2,1)} fusion(bf16[64,512]{1,0:T(8,128)(2,1)S(1)} %copy-done.4, bf16[64,8,2048]{2,1,0:T(8,128)(2,1)} %all-to-all-done.3), kind=kOutput, calls=%fused_computation.38 | convolution fusion | flops 134348800 | bytes 2424832 | tf_op jit(solution)/shard_map/dot_general | solution.py:123
  (45 shorter events, 0.5 us)
Async XLA Ops:
  0.6 87.6 %copy-start = (bf16[1,768,2048]{2,1,0:T(8,128)(2,1)S(1)}, bf16[1,768,2048]{2,1,0:T(8,128)(2,1)}, u32[]{:S(2)}) copy-start(bf16[1,768,2048]{2,1,0:T(8,128)(2,1)} %param.13) | copy-start | bytes 9437188
  4.2 0.6 copy-start.3
  8.0 13.3 %copy-start.5 = (bf16[64,2048]{1,0:T(8,128)(2,1)S(1)}, bf16[64,2048]{1,0:T(8,128)(2,1)}, u32[]{:S(2)}) copy-start(bf16[64,2048]{1,0:T(8,128)(2,1)} %param.10) | copy-start | bytes 786436
  8.0 64.5 %all-to-all-start = ((bf16[64,8,2048]{2,1,0:T(8,128)(2,1)}), bf16[64,8,2048]{2,1,0:T(8,128)(2,1)}, u32[]{:S(2)}, u32[]{:S(2)}) async-start(bf16[64,8,2048]{2,1,0:T(8,128)(2,1)} %fusion.19), calls=%async_computation | async-start | bytes 4194304 | tf_op jit(solution)/shard_map/all_to_all | solution.py:44
  23.7 4.7 %copy-start.7 = (f32[64,6]{0,1:T(8,128)S(1)}, f32[64,6]{0,1:T(8,128)}, u32[]{:S(2)}) copy-start(f32[64,6]{0,1:T(8,128)} %param.9) | copy-start | bytes 4612
  72.4 57.2 %all-to-all-start.2 = ((bf16[64,8,2048]{2,1,0:T(8,128)(2,1)}), bf16[64,8,2048]{2,1,0:T(8,128)(2,1)}, u32[]{:S(2)}, u32[]{:S(2)}) async-start(bf16[64,8,2048]{2,1,0:T(8,128)(2,1)} %fusion.20), calls=%async_computation.2 | async-start | bytes 4194304 | tf_op jit(solution)/shard_map/all_to_all | solution.py:44
  78.5 4.5 %copy-start.8 = (bf16[1,2048,768]{2,1,0:T(8,128)(2,1)S(1)}, bf16[1,2048,768]{2,1,0:T(8,128)(2,1)}, u32[]{:S(2)}) copy-start(bf16[1,2048,768]{2,1,0:T(8,128)(2,1)} %param.12) | copy-start | bytes 9437188
  82.9 5.2 %copy-start.15 = (f32[512,768]{1,0:T(8,128)}, f32[512,768]{1,0:T(8,128)S(1)}, u32[]{:S(2)}) copy-start(f32[512,768]{1,0:T(8,128)S(1)} %fusion.12) | copy-start | bytes 4718596
  88.2 3.2 %copy-start.14 = (bf16[512,768]{1,0:T(8,128)(2,1)}, bf16[512,768]{1,0:T(8,128)(2,1)S(1)}, u32[]{:S(2)}) copy-start(bf16[512,768]{1,0:T(8,128)(2,1)S(1)} %get-tuple-element.15) | copy-start | bytes 2359300
  129.6 77.8 %all-to-all-start.1 = ((bf16[64,8,2048]{2,1,0:T(8,128)(2,1)}), bf16[64,8,2048]{2,1,0:T(8,128)(2,1)}, u32[]{:S(2)}, u32[]{:S(2)}) async-start(bf16[64,8,2048]{2,1,0:T(8,128)(2,1)} %bitcast.128), calls=%async_computation.1 | async-start | bytes 4194304 | tf_op jit(solution)/shard_map/all_to_all | solution.py:44
  135.6 3.8 %copy-start.16 = (f32[512,768]{1,0:T(8,128)S(1)}, f32[512,768]{1,0:T(8,128)}, u32[]{:S(2)}) copy-start(f32[512,768]{1,0:T(8,128)} %copy-done.15) | copy-start | bytes 4718596
  135.6 3.8 %copy-start.17 = (f32[512,768]{1,0:T(8,128)S(1)}, f32[512,768]{1,0:T(8,128)}, u32[]{:S(2)}) copy-start(f32[512,768]{1,0:T(8,128)} %get-tuple-element.13) | copy-start | bytes 4718596
  144.2 5.3 %copy-start.11 = (bf16[512,768]{1,0:T(8,128)(2,1)}, bf16[512,768]{1,0:T(8,128)(2,1)S(1)}, u32[]{:S(2)}) copy-start(bf16[512,768]{1,0:T(8,128)(2,1)S(1)} %get-tuple-element.20) | copy-start | bytes 2359300
  155.5 4.4 %copy-start.13 = (bf16[512,768]{1,0:T(8,128)(2,1)S(1)}, bf16[512,768]{1,0:T(8,128)(2,1)}, u32[]{:S(2)}) copy-start(bf16[512,768]{1,0:T(8,128)(2,1)} %get-tuple-element.19) | copy-start | bytes 2359300
  163.4 1.9 copy-start.9
  165.3 7.1 %copy-start.2 = (bf16[4,768,768]{2,1,0:T(8,128)(2,1)}, bf16[4,768,768]{2,1,0:T(8,128)(2,1)S(1)}, u32[]{:S(2)}) copy-start(bf16[4,768,768]{2,1,0:T(8,128)(2,1)S(1)} %pad_maximum_fusion.1) | copy-start | bytes 14155780
  165.3 3.6 %copy-start.10 = (bf16[1,2048,768]{2,1,0:T(8,128)(2,1)S(1)}, bf16[1,2048,768]{2,1,0:T(8,128)(2,1)}, u32[]{:S(2)}) copy-start(bf16[1,2048,768]{2,1,0:T(8,128)(2,1)} %param.11) | copy-start | bytes 9437188
  165.3 3.8 %copy-start.12 = (bf16[512,768]{1,0:T(8,128)(2,1)S(1)}, bf16[512,768]{1,0:T(8,128)(2,1)}, u32[]{:S(2)}) copy-start(bf16[512,768]{1,0:T(8,128)(2,1)} %copy-done.11) | copy-start | bytes 2359300
  172.4 27.4 %collective-permute-start.3 = (bf16[768,768]{1,0:T(8,128)(2,1)S(1)}, bf16[768,768]{1,0:T(8,128)(2,1)}, u32[]{:S(2)}, u32[]{:S(2)}) collective-permute-start(bf16[768,768]{1,0:T(8,128)(2,1)S(1)} %dynamic-slice_bitcast_fusion), channel_id=1, source_target_pairs={{0,3},{1,0},{2,1},{3,2},{4,7},{5,4},{6,5},{7,6},{8,11},{9,8},{10,9... | collective-permute-start | bytes 3538952 | tf_op jit(solution)/shard_map/ppermute | solution.py:58
  176.6 28.8 %collective-permute-start = (bf16[768,768]{1,0:T(8,128)(2,1)S(1)}, bf16[768,768]{1,0:T(8,128)(2,1)}, u32[]{:S(2)}, u32[]{:S(2)}) collective-permute-start(bf16[768,768]{1,0:T(8,128)(2,1)S(1)} %dynamic-slice_bitcast_fusion.1), channel_id=1, source_target_pairs={{0,1},{1,2},{2,3},{3,0},{4,5},{5,6},{6,7},{7,4},{8,9},{9,10},{10,1... | collective-permute-start | bytes 3538952 | tf_op jit(solution)/shard_map/ppermute | solution.py:58
  201.8 27.3 %collective-permute-start.4 = (bf16[768,768]{1,0:T(8,128)(2,1)S(1)}, bf16[768,768]{1,0:T(8,128)(2,1)}, u32[]{:S(2)}, u32[]{:S(2)}) collective-permute-start(bf16[768,768]{1,0:T(8,128)(2,1)S(1)} %fusion.23), channel_id=1, source_target_pairs={{0,3},{1,0},{2,1},{3,2},{4,7},{5,4},{6,5},{7,6},{8,11},{9,8},{10,9... | collective-permute-start | bytes 3538952 | tf_op jit(solution)/shard_map/ppermute | solution.py:58
  207.3 27.3 %collective-permute-start.1 = (bf16[768,768]{1,0:T(8,128)(2,1)S(1)}, bf16[768,768]{1,0:T(8,128)(2,1)}, u32[]{:S(2)}, u32[]{:S(2)}) collective-permute-start(bf16[768,768]{1,0:T(8,128)(2,1)S(1)} %fusion.26), channel_id=1, source_target_pairs={{0,1},{1,2},{2,3},{3,0},{4,5},{5,6},{6,7},{7,4},{8,9},{9,10},{10,1... | collective-permute-start | bytes 3538952 | tf_op jit(solution)/shard_map/ppermute | solution.py:58
  207.4 65.4 %all-to-all-start.3 = ((bf16[64,8,2048]{2,1,0:T(8,128)(2,1)}), bf16[64,8,2048]{2,1,0:T(8,128)(2,1)}, u32[]{:S(2)}, u32[]{:S(2)}) async-start(bf16[64,8,2048]{2,1,0:T(8,128)(2,1)} %bitcast.18), calls=%async_computation.3 | async-start | bytes 4194304 | tf_op jit(solution)/shard_map/all_to_all | solution.py:44
  231.0 26.4 %collective-permute-start.5 = (bf16[768,768]{1,0:T(8,128)(2,1)S(1)}, bf16[768,768]{1,0:T(8,128)(2,1)}, u32[]{:S(2)}, u32[]{:S(2)}) collective-permute-start(bf16[768,768]{1,0:T(8,128)(2,1)S(1)} %fusion.22), channel_id=1, source_target_pairs={{0,3},{1,0},{2,1},{3,2},{4,7},{5,4},{6,5},{7,6},{8,11},{9,8},{10,9... | collective-permute-start | bytes 3538952 | tf_op jit(solution)/shard_map/ppermute | solution.py:58
  236.5 26.3 %collective-permute-start.2 = (bf16[768,768]{1,0:T(8,128)(2,1)S(1)}, bf16[768,768]{1,0:T(8,128)(2,1)}, u32[]{:S(2)}, u32[]{:S(2)}) collective-permute-start(bf16[768,768]{1,0:T(8,128)(2,1)S(1)} %fusion.25), channel_id=1, source_target_pairs={{0,1},{1,2},{2,3},{3,0},{4,5},{5,6},{6,7},{7,4},{8,9},{9,10},{10,1... | collective-permute-start | bytes 3538952 | tf_op jit(solution)/shard_map/ppermute | solution.py:58
  267.9 2.6 copy-start.6
  270.5 2.2 copy-start.4
  270.5 5.0 %copy-start.1 = (bf16[1,768,2048]{2,1,0:T(8,128)(2,1)S(1)}, bf16[1,768,2048]{2,1,0:T(8,128)(2,1)}, u32[]{:S(2)}) copy-start(bf16[1,768,2048]{2,1,0:T(8,128)(2,1)} %param.13) | copy-start | bytes 9437188

commit v6 on v2

--- a/solution.py
+++ b/solution.py
@@ -86,21 +86,18 @@
     grad_tokens = jnp.dot(owner, returned_grad, preferred_element_type=jnp.float32).astype(
         jnp.bfloat16
     )
-    gate_up_grad = jnp.concatenate([d_gate, d_up], axis=1)
-    gate_up_sum = lax.psum_scatter(
-        outer_sum(slot_rows, gate_up_grad).astype(jnp.bfloat16),
-        "replica",
-        scatter_dimension=0,
-        tiled=True,
-    ).astype(jnp.float32)
+    grad_gate = lax.psum_scatter(
+        outer_sum(slot_rows, d_gate).astype(jnp.bfloat16), "replica", scatter_dimension=0, tiled=True
+    )[None]
+    grad_up = lax.psum_scatter(
+        outer_sum(slot_rows, d_up).astype(jnp.bfloat16), "replica", scatter_dimension=0, tiled=True
+    )[None]
     down_sum = lax.psum_scatter(
         outer_sum(activation, grads_in).astype(jnp.bfloat16),
         "replica",
         scatter_dimension=0,
         tiled=True,
     )
-    grad_gate = gate_up_sum[:, :hidden].astype(jnp.bfloat16)[None]
-    grad_up = gate_up_sum[:, hidden:].astype(jnp.bfloat16)[None]
     grad_down = down_sum[None]
     return (combined, grad_tokens, grad_gate, grad_up, grad_down)
 

time: 276 us -> 277 us (level)
  matrix products: 51.8 us -> 56.1 us
  local copies, waits for them, and re-layouts: 13.8 us -> 11 us
    dot_general x2 -> x3, matrix products: 12.5 us -> 15.8 us  [outer_sum(): lax.dot_general(left, right, (((0,), (0,)), ((), ())), preferred_element_...]
  transfers between devices with their start and end apart: 6 -> 7, of which waited for: 4 -> 4; matrix products, arithmetic and copies ran while one was open for 17% -> 20% of each run, Pallas kernels for 0% -> 0%
where the time goes in v6:
time: 277 us; the launch traced here: 276 us
  waiting for transfers between devices  162 us (58%)
  matrix products  56.1 us (20%)
  starting transfers between devices  31.6 us (11%)
  between operations  13.9 us (5%)
  local copies, waits for them, and re-layouts  11 us (4%)
    all_to_all x4, waiting for transfers between devices, exchange(): lax.all_to_all(blocks, 'expert', split_axis=0, concat_axis=0, tiled=True)  162 us
    all_to_all x4, starting transfers between devices, exchange(): lax.all_to_all(blocks, 'expert', split_axis=0, concat_axis=0, tiled=True)  31.3 us
    dot_general x3, matrix products, outer_sum(): lax.dot_general(left, right, (((0,), (0,)), ((), ())), preferred_element_...  15.8 us
    mul x3, local copies, waits for them, and re-layouts, per_device(): gate_probs[:, :, None] * out_cot[:, None, :].astype(jnp.float32)  7.34 us
    dot_general x1, matrix products, backward_rows(): lax.dot_general(grad_rows, down_weight, contract, preferred_element_type=...  5.62 us
  transfers between devices with their start and end apart: 7, of which 4 were waited for; matrix products, arithmetic and copies ran while one was open for 20% of the time, Pallas kernels for 0%

profile of v6, /device:TPU:1, one launch (start us, length us, event | category | flops | bytes accessed | tf_op | source)
XLA Modules:
  0.0 276.4 jit_solution(2960602985700565612)
XLA Ops:
  7.2 0.0 copy-start
  7.2 0.9 copy.29
  8.1 0.1 eq.67
  8.2 0.1 eq.71
  8.4 0.9 reduce-window.6
  9.3 0.2 slice_reduce_fusion
  9.6 0.1 fusion.42
  9.7 0.1 reduce_sum.24
  9.8 0.1 copy.32
  9.9 0.7 multiply_add_fusion
  10.6 0.1 fusion.37
  10.8 3.1 %fusion.19 = bf16[64,8,2048]{2,1,0:T(8,128)(2,1)} fusion(bf16[64,512]{1,0:T(8,128)(2,1)S(1)} %fusion.37, bf16[64,2048]{1,0:T(8,128)(2,1)} %param.7), kind=kOutput, calls=%fused_computation.22 | convolution fusion | flops 135266304 | bytes 2424832 | tf_op jit(solution)/shard_map/dot_general | solution.py:63
  13.8 0.0 copy-start.2
  13.8 0.0 copy-start.1
  13.8 13.3 %all-to-all-start = ((bf16[64,8,2048]{2,1,0:T(8,128)(2,1)}), bf16[64,8,2048]{2,1,0:T(8,128)(2,1)}, u32[]{:S(2)}, u32[]{:S(2)}) async-start(bf16[64,8,2048]{2,1,0:T(8,128)(2,1)} %fusion.19), calls=%async_computation | async-start | bytes 4194304 | tf_op jit(solution)/shard_map/all_to_all | solution.py:44
  27.1 0.0 copy-done.2
  27.2 0.1 copy.33
  27.3 0.1 mul.68
  27.4 0.0 copy-done.1
  27.4 2.5 mul.70
  29.9 4.7 %mul.71 = f32[384,2048]{1,0:T(8,128)} reshape(f32[64,6,2048]{2,1,0:T(8,128)} %mul.70) | data formatting | bytes 6291456 | tf_op jit(solution)/shard_map/mul | solution.py:65
  34.6 4.6 %fusion.20 = bf16[64,8,2048]{2,1,0:T(8,128)(2,1)} fusion(f32[384,2048]{1,0:T(8,128)} %mul.71, f32[384]{0:T(512)S(1)} %mul.68, s32[384]{0:T(512)S(1)} %multiply_add_fusion.1), kind=kOutput, calls=%fused_computation.23 | convolution fusion | flops 808124416 | bytes 5245952 | tf_op jit(solution)/shard_map/dot_general | solution.py:66
  39.2 39.1 %all-to-all-done = bf16[64,8,2048]{2,1,0:T(8,128)(2,1)} async-done(((bf16[64,8,2048]{2,1,0:T(8,128)(2,1)}), bf16[64,8,2048]{2,1,0:T(8,128)(2,1)}, u32[]{:S(2)}, u32[]{:S(2)}) %all-to-all-start) | async-done | bytes 2097184 | tf_op jit(solution)/shard_map/all_to_all | solution.py:44
  78.3 6.0 %all-to-all-start.2 = ((bf16[64,8,2048]{2,1,0:T(8,128)(2,1)}), bf16[64,8,2048]{2,1,0:T(8,128)(2,1)}, u32[]{:S(2)}, u32[]{:S(2)}) async-start(bf16[64,8,2048]{2,1,0:T(8,128)(2,1)} %fusion.20), calls=%async_computation.2 | async-start | bytes 4194304 | tf_op jit(solution)/shard_map/all_to_all | solution.py:44
  84.3 0.0 reduce-scatter.8.cloned.1.call-start
  84.4 0.0 copy-start.3
  84.4 4.5 %fusion.12 = f32[512,768]{1,0:T(8,128)S(1)} fusion(bf16[1,2048,768]{2,1,0:T(8,128)(2,1)} %param.11, bf16[64,8,2048]{2,1,0:T(8,128)(2,1)} %all-to-all-done), kind=kOutput, calls=%fused_computation.16 | convolution fusion | flops 1610612736 | bytes 6815744 | tf_op jit(solution)/shard_map/dot_general | solution.py:16
  88.8 0.0 copy-done.3
  88.9 0.0 copy-start.8
  88.9 5.2 %multiply_convert_fusion.4 = (bf16[512,768]{1,0:T(8,128)(2,1)S(1)}, f32[512,768]{1,0:T(8,128)}) fusion(f32[512,768]{1,0:T(8,128)S(1)} %fusion.12, bf16[1,2048,768]{2,1,0:T(8,128)(2,1)S(1)} %copy-done.3, bf16[64,8,2048]{2,1,0:T(8,128)(2,1)} %all-to-all-done), kind=kOutput, calls=%fused_computation.39 | convolution fusion | flops 1612972032 | bytes 9175040 | tf_op jit(solution)/shard_map/dot_general | solution.py:17
  94.1 0.0 copy-done.8
  94.1 0.0 copy-start.7
  94.1 0.0 copy-done
  94.1 3.2 %fusion.14 = bf16[512,2048]{1,0:T(8,128)(2,1)} fusion(bf16[512,768]{1,0:T(8,128)(2,1)S(1)} %get-tuple-element.12, bf16[1,768,2048]{2,1,0:T(8,128)(2,1)S(1)} %copy-done), kind=kOutput, calls=%fused_computation.19 | convolution fusion | flops 1611661312 | bytes 6029312 | tf_op jit(solution)/shard_map/dot_general | solution.py:72
  97.4 0.0 copy-done.7
  97.4 38.1 %all-to-all-done.2 = bf16[64,8,2048]{2,1,0:T(8,128)(2,1)} async-done(((bf16[64,8,2048]{2,1,0:T(8,128)(2,1)}), bf16[64,8,2048]{2,1,0:T(8,128)(2,1)}, u32[]{:S(2)}, u32[]{:S(2)}) %all-to-all-start.2) | async-done | bytes 2097184 | tf_op jit(solution)/shard_map/all_to_all | solution.py:44
  135.5 5.3 %convolution_convert_fusion = bf16[768,2048]{1,0:T(8,128)(2,1)} fusion(bf16[512,768]{1,0:T(8,128)(2,1)} %copy-done.7, bf16[64,8,2048]{2,1,0:T(8,128)(2,1)} %all-to-all-done.2), kind=kOutput, calls=%fused_computation.3 | convolution fusion | flops 1612185600 | bytes 6029312 | tf_op jit(solution)/shard_map/dot_general | solution.py:38
  140.8 0.0 reduce-scatter.8.cloned.1.call-update
  140.8 0.2 reduce-scatter.4.cloned.1.call-start
  141.1 5.6 %multiply_convert_fusion.3 = (bf16[512,768]{1,0:T(8,128)(2,1)S(1)}, bf16[512,768]{1,0:T(8,128)(2,1)}) fusion(f32[512,768]{1,0:T(8,128)} %copy-done.8, f32[512,768]{1,0:T(8,128)} %get-tuple-element.10, bf16[1,768,2048]{2,1,0:T(8,128)(2,1)S(1)} %copy-done, bf16[64,8,2048]{2,1,0:T(8,128)(2,1)} %all-to-all-done.2), kind=kOutput, calls=%fused_computation.36 | convolution fusion | flops 1615724544 | bytes 9961472 | tf_op jit(solution)/shard_map/dot_general | solution.py:24
  146.7 0.0 copy-start.5
  146.7 0.9 copy-done.5
  147.6 5.2 %convolution_convert_fusion.2 = bf16[2048,768]{1,0:T(8,128)(2,1)} fusion(bf16[512,768]{1,0:T(8,128)(2,1)S(1)} %get-tuple-element.13, bf16[64,8,2048]{2,1,0:T(8,128)(2,1)} %all-to-all-done), kind=kOutput, calls=%fused_computation.5 | convolution fusion | flops 1612185600 | bytes 6029312 | tf_op jit(solution)/shard_map/dot_general | solution.py:38
  152.7 0.0 reduce-scatter.4.cloned.1.call-update
  152.8 6.0 %all-to-all-start.1 = ((bf16[64,8,2048]{2,1,0:T(8,128)(2,1)}), bf16[64,8,2048]{2,1,0:T(8,128)(2,1)}, u32[]{:S(2)}, u32[]{:S(2)}) async-start(bf16[64,8,2048]{2,1,0:T(8,128)(2,1)} %bitcast.98), calls=%async_computation.1 | async-start | bytes 4194304 | tf_op jit(solution)/shard_map/all_to_all | solution.py:44
  158.7 0.0 reduce-scatter.6.cloned.1.call-start
  158.8 5.4 %convolution_convert_fusion.1 = bf16[2048,768]{1,0:T(8,128)(2,1)} fusion(bf16[512,768]{1,0:T(8,128)(2,1)} %get-tuple-element.14, bf16[64,8,2048]{2,1,0:T(8,128)(2,1)} %all-to-all-done), kind=kOutput, calls=%fused_computation.4 | convolution fusion | flops 1612185600 | bytes 6029312 | tf_op jit(solution)/shard_map/dot_general | solution.py:38
  164.1 0.0 reduce-scatter.6.cloned.1.call-update
  164.2 0.0 copy-start.4
  164.2 0.0 copy-start.6
  164.2 4.1 %fusion.6 = f32[512,2048]{1,0:T(8,128)S(1)} fusion(bf16[512,768]{1,0:T(8,128)(2,1)} %get-tuple-element.14, bf16[1,2048,768]{2,1,0:T(8,128)(2,1)} %param.12), kind=kOutput, calls=%fused_computation.10 | convolution fusion | flops 1610612736 | bytes 8126464 | tf_op jit(solution)/shard_map/dot_general | solution.py:31
  168.3 0.0 copy-done.4
  168.3 0.0 copy-done.6
  168.4 3.1 %fusion.21 = bf16[64,8,2048]{2,1,0:T(8,128)(2,1)} fusion(f32[512,2048]{1,0:T(8,128)S(1)} %fusion.6, bf16[512,768]{1,0:T(8,128)(2,1)S(1)} %copy-done.6, bf16[1,2048,768]{2,1,0:T(8,128)(2,1)S(1)} %copy-done.4), kind=kOutput, calls=%fused_computation.24 | convolution fusion | flops 1612709888 | bytes 10223616 | tf_op jit(solution)/shard_map/dot_general | solution.py:30
  171.5 38.4 %all-to-all-done.1 = bf16[64,8,2048]{2,1,0:T(8,128)(2,1)} async-done(((bf16[64,8,2048]{2,1,0:T(8,128)(2,1)}), bf16[64,8,2048]{2,1,0:T(8,128)(2,1)}, u32[]{:S(2)}, u32[]{:S(2)}) %all-to-all-start.1) | async-done | bytes 2097184 | tf_op jit(solution)/shard_map/all_to_all | solution.py:44
  209.9 6.0 %all-to-all-start.3 = ((bf16[64,8,2048]{2,1,0:T(8,128)(2,1)}), bf16[64,8,2048]{2,1,0:T(8,128)(2,1)}, u32[]{:S(2)}, u32[]{:S(2)}) async-start(bf16[64,8,2048]{2,1,0:T(8,128)(2,1)} %fusion.21), calls=%async_computation.3 | async-start | bytes 4194304 | tf_op jit(solution)/shard_map/all_to_all | solution.py:44
  215.9 0.1 copy.35
  216.0 2.6 fusion.24
  218.7 1.3 fusion
  220.0 0.9 copy.42
  220.9 46.2 %all-to-all-done.3 = bf16[64,8,2048]{2,1,0:T(8,128)(2,1)} async-done(((bf16[64,8,2048]{2,1,0:T(8,128)(2,1)}), bf16[64,8,2048]{2,1,0:T(8,128)(2,1)}, u32[]{:S(2)}, u32[]{:S(2)}) %all-to-all-start.3) | async-done | bytes 2097184 | tf_op jit(solution)/shard_map/all_to_all | solution.py:44
  267.1 2.8 %convolution_convert_fusion.5 = bf16[64,2048]{1,0:T(8,128)(2,1)} fusion(bf16[64,512]{1,0:T(8,128)(2,1)S(1)} %fusion.37, bf16[64,8,2048]{2,1,0:T(8,128)(2,1)} %all-to-all-done.3), kind=kOutput, calls=%fused_computation.25 | convolution fusion | flops 134348800 | bytes 2424832 | tf_op jit(solution)/shard_map/dot_general | solution.py:86
  269.8 0.0 reduce-scatter.8.cloned.1.call-done
  269.8 0.0 reduce-scatter.4.cloned.1.call-done
  (4 shorter events, 0.1 us)
Async XLA Ops:
  7.2 86.9 %copy-start = (bf16[1,768,2048]{2,1,0:T(8,128)(2,1)S(1)}, bf16[1,768,2048]{2,1,0:T(8,128)(2,1)}, u32[]{:S(2)}) copy-start(bf16[1,768,2048]{2,1,0:T(8,128)(2,1)} %param.13) | copy-start | bytes 9437188
  13.8 13.3 %copy-start.2 = (f32[64,6]{0,1:T(8,128)S(1)}, f32[64,6]{0,1:T(8,128)}, u32[]{:S(2)}) copy-start(f32[64,6]{0,1:T(8,128)} %param.9) | copy-start | bytes 4612
  13.8 13.6 %copy-start.1 = (bf16[64,2048]{1,0:T(8,128)(2,1)S(1)}, bf16[64,2048]{1,0:T(8,128)(2,1)}, u32[]{:S(2)}) copy-start(bf16[64,2048]{1,0:T(8,128)(2,1)} %param.10) | copy-start | bytes 786436
  13.8 64.5 %all-to-all-start = ((bf16[64,8,2048]{2,1,0:T(8,128)(2,1)}), bf16[64,8,2048]{2,1,0:T(8,128)(2,1)}, u32[]{:S(2)}, u32[]{:S(2)}) async-start(bf16[64,8,2048]{2,1,0:T(8,128)(2,1)} %fusion.19), calls=%async_computation | async-start | bytes 4194304 | tf_op jit(solution)/shard_map/all_to_all | solution.py:44
  78.3 57.2 %all-to-all-start.2 = ((bf16[64,8,2048]{2,1,0:T(8,128)(2,1)}), bf16[64,8,2048]{2,1,0:T(8,128)(2,1)}, u32[]{:S(2)}, u32[]{:S(2)}) async-start(bf16[64,8,2048]{2,1,0:T(8,128)(2,1)} %fusion.20), calls=%async_computation.2 | async-start | bytes 4194304 | tf_op jit(solution)/shard_map/all_to_all | solution.py:44
  84.3 185.5 %reduce-scatter.8.cloned.1.call-start = ((), (), s32[]{:S(2)}) async-start(), calls=%async_computation.9 | async-start | bytes 3932160 | tf_op jit(solution)/shard_map/reduce_scatter | solution.py:95
  84.4 4.5 %copy-start.3 = (bf16[1,2048,768]{2,1,0:T(8,128)(2,1)S(1)}, bf16[1,2048,768]{2,1,0:T(8,128)(2,1)}, u32[]{:S(2)}) copy-start(bf16[1,2048,768]{2,1,0:T(8,128)(2,1)} %param.12) | copy-start | bytes 9437188
  88.9 5.2 %copy-start.8 = (f32[512,768]{1,0:T(8,128)}, f32[512,768]{1,0:T(8,128)S(1)}, u32[]{:S(2)}) copy-start(f32[512,768]{1,0:T(8,128)S(1)} %fusion.12) | copy-start | bytes 4718596
  94.1 3.3 %copy-start.7 = (bf16[512,768]{1,0:T(8,128)(2,1)}, bf16[512,768]{1,0:T(8,128)(2,1)S(1)}, u32[]{:S(2)}) copy-start(bf16[512,768]{1,0:T(8,128)(2,1)S(1)} %get-tuple-element.12) | copy-start | bytes 2359300
  140.8 129.0 %reduce-scatter.4.cloned.1.call-start = ((), (), s32[]{:S(2)}) async-start(), calls=%async_computation.7 | async-start | bytes 3932160 | tf_op jit(solution)/shard_map/reduce_scatter | solution.py:89
  146.7 0.9 copy-start.5
  152.8 57.1 %all-to-all-start.1 = ((bf16[64,8,2048]{2,1,0:T(8,128)(2,1)}), bf16[64,8,2048]{2,1,0:T(8,128)(2,1)}, u32[]{:S(2)}, u32[]{:S(2)}) async-start(bf16[64,8,2048]{2,1,0:T(8,128)(2,1)} %bitcast.98), calls=%async_computation.1 | async-start | bytes 4194304 | tf_op jit(solution)/shard_map/all_to_all | solution.py:44
  158.7 111.1 %reduce-scatter.6.cloned.1.call-start = ((), (), s32[]{:S(2)}) async-start(), calls=%async_computation.8 | async-start | bytes 3932160 | tf_op jit(solution)/shard_map/reduce_scatter | solution.py:92
  164.2 4.2 %copy-start.4 = (bf16[1,2048,768]{2,1,0:T(8,128)(2,1)S(1)}, bf16[1,2048,768]{2,1,0:T(8,128)(2,1)}, u32[]{:S(2)}) copy-start(bf16[1,2048,768]{2,1,0:T(8,128)(2,1)} %param.11) | copy-start | bytes 9437188
  164.2 4.2 %copy-start.6 = (bf16[512,768]{1,0:T(8,128)(2,1)S(1)}, bf16[512,768]{1,0:T(8,128)(2,1)}, u32[]{:S(2)}) copy-start(bf16[512,768]{1,0:T(8,128)(2,1)} %copy-done.5) | copy-start | bytes 2359300
  209.9 57.2 %all-to-all-start.3 = ((bf16[64,8,2048]{2,1,0:T(8,128)(2,1)}), bf16[64,8,2048]{2,1,0:T(8,128)(2,1)}, u32[]{:S(2)}, u32[]{:S(2)}) async-start(bf16[64,8,2048]{2,1,0:T(8,128)(2,1)} %fusion.21), calls=%async_computation.3 | async-start | bytes 4194304 | tf_op jit(solution)/shard_map/all_to_all | solution.py:44
Sparse Core Ops, SparseCore 0:
  140.9 37.5 reduce-scatter.7
  181.6 40.5 reduce-scatter.3
  225.4 40.5 reduce-scatter.5

commit v7 on v3

--- a/solution.py
+++ b/solution.py
@@ -97,15 +97,16 @@
     )
     returned_grad = exchange(back_rows.reshape(experts, capacity, features)).reshape(-1, features)
 
-    picked = jnp.einsum("tkp,pd->tkd", pick3, returned, preferred_element_type=jnp.float32)
-    combined = jnp.einsum("tk,tkd->td", gate_probs, picked).astype(jnp.bfloat16)
-    grad_tokens = jnp.dot(owner, returned_grad, preferred_element_type=jnp.float32).astype(
-        jnp.bfloat16
+    grad_gate = lax.psum_scatter(
+        outer_sum(slot_rows, d_gate).astype(jnp.bfloat16), "replica", scatter_dimension=0, tiled=True
+    )[None]
+    grad_up = lax.psum_scatter(
+        outer_sum(slot_rows, d_up).astype(jnp.bfloat16), "replica", scatter_dimension=0, tiled=True
+    )[None]
+    part_down, returned = lax.optimization_barrier(
+        (outer_sum(activation, grads_in).astype(jnp.bfloat16), returned)
     )
     half = features // 2
-    grad_gate = ring_reduce_scatter(outer_sum(slot_rows, d_gate).astype(jnp.bfloat16), 1)[None]
-    grad_up = ring_reduce_scatter(outer_sum(slot_rows, d_up).astype(jnp.bfloat16), -1)[None]
-    part_down = outer_sum(activation, grads_in).astype(jnp.bfloat16)
     grad_down = jnp.concatenate(
         [
             ring_reduce_scatter(part_down[:, :half], 1),
@@ -113,6 +114,11 @@
         ],
         axis=1,
     )[None]
+    picked = jnp.einsum("tkp,pd->tkd", pick3, returned, preferred_element_type=jnp.float32)
+    combined = jnp.einsum("tk,tkd->td", gate_probs, picked).astype(jnp.bfloat16)
+    grad_tokens = jnp.dot(owner, returned_grad, preferred_element_type=jnp.float32).astype(
+        jnp.bfloat16
+    )
     return (combined, grad_tokens, grad_gate, grad_up, grad_down)
 
 

time: 279 us -> 277 us (level)
  between operations: 1.03 us -> 14.5 us
  other arithmetic: 20.1 us -> 7.43 us
  starting transfers between devices: 49.9 us -> 39 us
  waiting for transfers between devices: 142 us -> 150 us
  matrix products: 47.6 us -> 52.3 us
  local copies, waits for them, and re-layouts: 15.6 us -> 12.7 us
    all_to_all x4, waiting for transfers between devices: 105 us -> 129 us  [exchange(): lax.all_to_all(blocks, 'expert', split_axis=0, concat_axis=0, tiled=True)]
    ppermute x12 -> x6, waiting for transfers between devices: 37.3 us -> 20.8 us  [ring_reduce_scatter(): acc = lax.ppermute(acc, 'replica', perm)]
    ppermute x12 -> x6, starting transfers between devices: 18.6 us -> 7.24 us  [ring_reduce_scatter(): acc = lax.ppermute(acc, 'replica', perm)]
    convert_element_type x10 -> x6, other arithmetic: 14 us -> 4.55 us  [ring_reduce_scatter(): (acc.astype(jnp.float32) + own(step).astype(jnp.float32)).astype(jnp.bflo...]
    squeeze x4 -> x2, local copies, waits for them, and re-layouts: 3.49 us -> 0.06 us  [own(): lax.dynamic_index_in_dim(table, (me - direction * (step + 1)) % n, 0, False)]
    broadcast_in_dim x2 -> x0, other arithmetic: 3.26 us -> none  [the longest x1 2.19 us: per_device(): ring_reduce_scatter(outer_sum(slot_rows, d_gate).astype(jnp.bfloat16), 1)]
    dot_general x3, matrix products: 10.8 us -> 13.6 us  [outer_sum(): lax.dot_general(left, right, (((0,), (0,)), ((), ())), preferred_element_...]
  transfers between devices with their start and end apart: 16 -> 12, of which waited for: 10 -> 6; matrix products, arithmetic and copies ran while one was open for 26% -> 19% of each run, Pallas kernels for 0% -> 0%
where the time goes in v7:
time: 277 us; the launch traced here: 276 us
  waiting for transfers between devices  150 us (54%)
  matrix products  52.3 us (19%)
  starting transfers between devices  39 us (14%)
  between operations  14.5 us (5%)
  local copies, waits for them, and re-layouts  12.7 us (5%)
  other arithmetic  7.43 us (3%)
    all_to_all x4, waiting for transfers between devices, exchange(): lax.all_to_all(blocks, 'expert', split_axis=0, concat_axis=0, tiled=True)  129 us
    all_to_all x4, starting transfers between devices, exchange(): lax.all_to_all(blocks, 'expert', split_axis=0, concat_axis=0, tiled=True)  31.3 us
    ppermute x6, waiting for transfers between devices, ring_reduce_scatter(): acc = lax.ppermute(acc, 'replica', perm)  20.8 us
    dot_general x3, matrix products, outer_sum(): lax.dot_general(left, right, (((0,), (0,)), ((), ())), preferred_element_...  13.6 us
    mul x3, local copies, waits for them, and re-layouts, per_device(): gate_probs[:, :, None] * out_cot[:, None, :].astype(jnp.float32)  7.37 us
    ppermute x6, starting transfers between devices, ring_reduce_scatter(): acc = lax.ppermute(acc, 'replica', perm)  7.24 us
    dot_general x1, matrix products, backward_rows(): lax.dot_general(grad_rows, down_weight, contract, preferred_element_type=...  5.6 us
  transfers between devices with their start and end apart: 12, of which 6 were waited for; matrix products, arithmetic and copies ran while one was open for 19% of the time, Pallas kernels for 0%

profile of v7, /device:TPU:1, one launch (start us, length us, event | category | flops | bytes accessed | tf_op | source)
XLA Modules:
  0.0 276.0 jit_solution(6207444879748275316)
XLA Ops:
  7.2 0.0 copy-start
  7.2 0.9 copy.26
  8.1 0.1 eq.55
  8.2 0.1 eq.59
  8.4 0.9 reduce-window.6
  9.3 0.2 slice_reduce_fusion
  9.6 0.1 fusion.46
  9.7 0.1 reduce_sum.24
  9.8 0.1 copy.29
  9.9 0.7 multiply_add_fusion
  10.6 0.1 fusion.41
  10.8 3.0 %fusion.19 = bf16[64,8,2048]{2,1,0:T(8,128)(2,1)} fusion(bf16[64,512]{1,0:T(8,128)(2,1)S(1)} %fusion.41, bf16[64,2048]{1,0:T(8,128)(2,1)} %param.7), kind=kOutput, calls=%fused_computation.22 | convolution fusion | flops 135266304 | bytes 2424832 | tf_op jit(solution)/shard_map/dot_general | solution.py:79
  13.8 13.3 %all-to-all-start = ((bf16[64,8,2048]{2,1,0:T(8,128)(2,1)}), bf16[64,8,2048]{2,1,0:T(8,128)(2,1)}, u32[]{:S(2)}, u32[]{:S(2)}) async-start(bf16[64,8,2048]{2,1,0:T(8,128)(2,1)} %fusion.19), calls=%async_computation | async-start | bytes 4194304 | tf_op jit(solution)/shard_map/all_to_all | solution.py:44
  27.1 2.5 mul.70
  29.6 4.8 %mul.71 = f32[384,2048]{1,0:T(8,128)} reshape(f32[64,6,2048]{2,1,0:T(8,128)} %mul.70) | data formatting | bytes 6291456 | tf_op jit(solution)/shard_map/mul | solution.py:81
  34.3 0.1 copy.30
  34.4 0.1 mul.68
  34.6 4.6 %fusion.20 = bf16[64,8,2048]{2,1,0:T(8,128)(2,1)} fusion(f32[384,2048]{1,0:T(8,128)} %mul.71, f32[384]{0:T(512)S(1)} %mul.68, s32[384]{0:T(512)S(1)} %multiply_add_fusion.1), kind=kOutput, calls=%fused_computation.23 | convolution fusion | flops 808124416 | bytes 5245952 | tf_op jit(solution)/shard_map/dot_general | solution.py:82
  39.2 39.1 %all-to-all-done = bf16[64,8,2048]{2,1,0:T(8,128)(2,1)} async-done(((bf16[64,8,2048]{2,1,0:T(8,128)(2,1)}), bf16[64,8,2048]{2,1,0:T(8,128)(2,1)}, u32[]{:S(2)}, u32[]{:S(2)}) %all-to-all-start) | async-done | bytes 2097184 | tf_op jit(solution)/shard_map/all_to_all | solution.py:44
  78.2 6.0 %all-to-all-start.1 = ((bf16[64,8,2048]{2,1,0:T(8,128)(2,1)}), bf16[64,8,2048]{2,1,0:T(8,128)(2,1)}, u32[]{:S(2)}, u32[]{:S(2)}) async-start(bf16[64,8,2048]{2,1,0:T(8,128)(2,1)} %fusion.20), calls=%async_computation.1 | async-start | bytes 4194304 | tf_op jit(solution)/shard_map/all_to_all | solution.py:44
  84.3 0.2 reduce-scatter.3.cloned.1.call-start
  84.5 0.0 copy-start.8
  84.5 4.5 %fusion.12 = f32[512,768]{1,0:T(8,128)S(1)} fusion(bf16[1,2048,768]{2,1,0:T(8,128)(2,1)} %param.11, bf16[64,8,2048]{2,1,0:T(8,128)(2,1)} %all-to-all-done), kind=kOutput, calls=%fused_computation.16 | convolution fusion | flops 1610612736 | bytes 6815744 | tf_op jit(solution)/shard_map/dot_general | solution.py:16
  89.0 5.2 %multiply_convert_fusion.4 = (bf16[512,768]{1,0:T(8,128)(2,1)S(1)}, f32[512,768]{1,0:T(8,128)}) fusion(f32[512,768]{1,0:T(8,128)S(1)} %fusion.12, bf16[1,2048,768]{2,1,0:T(8,128)(2,1)S(1)} %copy-done.8, bf16[64,8,2048]{2,1,0:T(8,128)(2,1)} %all-to-all-done), kind=kOutput, calls=%fused_computation.39 | convolution fusion | flops 1612972032 | bytes 9175040 | tf_op jit(solution)/shard_map/dot_general | solution.py:17
  94.2 3.3 %fusion.14 = bf16[512,2048]{1,0:T(8,128)(2,1)} fusion(bf16[512,768]{1,0:T(8,128)(2,1)S(1)} %get-tuple-element.11, bf16[1,768,2048]{2,1,0:T(8,128)(2,1)S(1)} %copy-done), kind=kOutput, calls=%fused_computation.19 | convolution fusion | flops 1611661312 | bytes 6029312 | tf_op jit(solution)/shard_map/dot_general | solution.py:88
  97.4 38.0 %all-to-all-done.1 = bf16[64,8,2048]{2,1,0:T(8,128)(2,1)} async-done(((bf16[64,8,2048]{2,1,0:T(8,128)(2,1)}), bf16[64,8,2048]{2,1,0:T(8,128)(2,1)}, u32[]{:S(2)}, u32[]{:S(2)}) %all-to-all-start.1) | async-done | bytes 2097184 | tf_op jit(solution)/shard_map/all_to_all | solution.py:44
  135.4 5.6 %multiply_convert_fusion.3 = (bf16[512,768]{1,0:T(8,128)(2,1)S(1)}, bf16[512,768]{1,0:T(8,128)(2,1)}) fusion(f32[512,768]{1,0:T(8,128)} %copy-done.15, f32[512,768]{1,0:T(8,128)} %get-tuple-element.14, bf16[1,768,2048]{2,1,0:T(8,128)(2,1)S(1)} %copy-done, bf16[64,8,2048]{2,1,0:T(8,128)(2,1)} %all-to-all-done.1), kind=kOutput, calls=%fused_computation.36 | convolution fusion | flops 1615724544 | bytes 9961472 | tf_op jit(solution)/shard_map/dot_general | solution.py:24
  141.0 0.9 copy-done.10
  141.9 5.1 %convolution_convert_fusion.1 = bf16[2048,768]{1,0:T(8,128)(2,1)} fusion(bf16[512,768]{1,0:T(8,128)(2,1)S(1)} %get-tuple-element.19, bf16[64,8,2048]{2,1,0:T(8,128)(2,1)} %all-to-all-done), kind=kOutput, calls=%fused_computation.4 | convolution fusion | flops 1612185600 | bytes 6029312 | tf_op jit(solution)/shard_map/dot_general | solution.py:38
  147.0 0.0 reduce-scatter.3.cloned.1.call-update
  147.0 0.0 copy-start.12
  147.0 6.0 %all-to-all-start.2 = ((bf16[64,8,2048]{2,1,0:T(8,128)(2,1)}), bf16[64,8,2048]{2,1,0:T(8,128)(2,1)S(1)}, u32[]{:S(2)}, u32[]{:S(2)}) async-start(bf16[64,8,2048]{2,1,0:T(8,128)(2,1)} %bitcast.128), calls=%async_computation.2 | async-start | bytes 4194304 | tf_op jit(solution)/shard_map/all_to_all | solution.py:44
  153.0 0.3 reduce-scatter.5.cloned.1.call-start
  153.3 5.1 %convolution_convert_fusion = bf16[2048,768]{1,0:T(8,128)(2,1)} fusion(bf16[512,768]{1,0:T(8,128)(2,1)S(1)} %copy-done.12, bf16[64,8,2048]{2,1,0:T(8,128)(2,1)} %all-to-all-done), kind=kOutput, calls=%fused_computation.3 | convolution fusion | flops 1612185600 | bytes 6029312 | tf_op jit(solution)/shard_map/dot_general | solution.py:38
  158.4 0.0 reduce-scatter.5.cloned.1.call-update
  158.4 0.0 copy-start.9
  158.4 4.1 %fusion.6 = f32[512,2048]{1,0:T(8,128)S(1)} fusion(bf16[512,768]{1,0:T(8,128)(2,1)} %get-tuple-element.20, bf16[1,2048,768]{2,1,0:T(8,128)(2,1)} %param.12), kind=kOutput, calls=%fused_computation.10 | convolution fusion | flops 1610612736 | bytes 8126464 | tf_op jit(solution)/shard_map/dot_general | solution.py:31
  162.6 3.2 %fusion.21 = bf16[64,8,2048]{2,1,0:T(8,128)(2,1)} fusion(f32[512,2048]{1,0:T(8,128)S(1)} %fusion.6, bf16[512,768]{1,0:T(8,128)(2,1)S(1)} %copy-done.11, bf16[1,2048,768]{2,1,0:T(8,128)(2,1)S(1)} %copy-done.9), kind=kOutput, calls=%fused_computation.24 | convolution fusion | flops 1612709888 | bytes 10223616 | tf_op jit(solution)/shard_map/dot_general | solution.py:30
  165.8 38.5 %all-to-all-done.2 = bf16[64,8,2048]{2,1,0:T(8,128)(2,1)S(1)} async-done(((bf16[64,8,2048]{2,1,0:T(8,128)(2,1)}), bf16[64,8,2048]{2,1,0:T(8,128)(2,1)S(1)}, u32[]{:S(2)}, u32[]{:S(2)}) %all-to-all-start.2) | async-done | bytes 2097184 | tf_op jit(solution)/shard_map/all_to_all | solution.py:44
  204.3 1.3 copy-done.4
  205.6 6.0 %all-to-all-start.3 = ((bf16[64,8,2048]{2,1,0:T(8,128)(2,1)}), bf16[64,8,2048]{2,1,0:T(8,128)(2,1)}, u32[]{:S(2)}, u32[]{:S(2)}) async-start(bf16[64,8,2048]{2,1,0:T(8,128)(2,1)} %fusion.21), calls=%async_computation.3 | async-start | bytes 4194304 | tf_op jit(solution)/shard_map/all_to_all | solution.py:44
  211.7 0.1 copy.32
  211.9 3.4 %convolution_convert_fusion.2 = bf16[768,2048]{1,0:T(8,128)(2,1)S(1)} fusion(bf16[512,768]{1,0:T(8,128)(2,1)S(1)} %copy-done.14, bf16[64,8,2048]{2,1,0:T(8,128)(2,1)} %all-to-all-done.1), kind=kOutput, calls=%fused_computation.5 | convolution fusion | flops 1612185600 | bytes 6029312 | tf_op jit(solution)/shard_map/dot_general | solution.py:38
  215.3 0.3 fusion.48
  215.7 2.8 %collective-permute-start.3 = (bf16[192,1024]{1,0:T(8,128)(2,1)S(1)}, bf16[192,1024]{1,0:T(8,128)(2,1)S(1)}, u32[]{:S(2)}, u32[]{:S(2)}) collective-permute-start(bf16[192,1024]{1,0:T(8,128)(2,1)S(1)} %dynamic-slice_bitcast_fusion), channel_id=1, source_target_pairs={{0,3},{1,0},{2,1},{3,2},{4,7},{5,4},{6,5},{7,6},{8,11},{9,8},{10,9... | collective-permute-start | bytes 1179656 | tf_op jit(solution)/shard_map/ppermute | solution.py:58
  218.6 0.1 collective-permute-start
  218.7 1.0 fusion.25
  219.7 14.7 %collective-permute-done.3 = bf16[192,1024]{1,0:T(8,128)(2,1)S(1)} collective-permute-done((bf16[192,1024]{1,0:T(8,128)(2,1)S(1)}, bf16[192,1024]{1,0:T(8,128)(2,1)S(1)}, u32[]{:S(2)}, u32[]{:S(2)}) %collective-permute-start.3) | collective-permute-done | bytes 393248 | tf_op jit(solution)/shard_map/ppermute | solution.py:58
  234.4 0.1 fusion.36
  234.6 1.3 collective-permute-start.4
  235.9 0.0 collective-permute-done
  235.9 0.1 fusion.39
  236.0 0.6 collective-permute-start.1
  236.6 1.3 fusion
  237.9 0.9 copy.39
  238.8 6.1 %collective-permute-done.4 = bf16[192,1024]{1,0:T(8,128)(2,1)S(1)} collective-permute-done((bf16[192,1024]{1,0:T(8,128)(2,1)S(1)}, bf16[192,1024]{1,0:T(8,128)(2,1)S(1)}, u32[]{:S(2)}, u32[]{:S(2)}) %collective-permute-start.4) | collective-permute-done | bytes 393248 | tf_op jit(solution)/shard_map/ppermute | solution.py:58
  244.9 0.9 fusion.35
  245.7 2.4 collective-permute-start.5
  248.2 0.9 fusion.38
  249.1 13.6 %all-to-all-done.3 = bf16[64,8,2048]{2,1,0:T(8,128)(2,1)} async-done(((bf16[64,8,2048]{2,1,0:T(8,128)(2,1)}), bf16[64,8,2048]{2,1,0:T(8,128)(2,1)}, u32[]{:S(2)}, u32[]{:S(2)}) %all-to-all-start.3) | async-done | bytes 2097184 | tf_op jit(solution)/shard_map/all_to_all | solution.py:44
  262.7 2.9 %convolution_convert_fusion.5 = bf16[64,2048]{1,0:T(8,128)(2,1)} fusion(bf16[64,512]{1,0:T(8,128)(2,1)S(1)} %fusion.41, bf16[64,8,2048]{2,1,0:T(8,128)(2,1)} %all-to-all-done.3), kind=kOutput, calls=%fused_computation.25 | convolution fusion | flops 134348800 | bytes 2424832 | tf_op jit(solution)/shard_map/dot_general | solution.py:119
  265.7 1.2 fusion.34
  266.9 1.2 fusion.37
  268.2 0.9 maximum_bitcast_fusion
  (37 shorter events, 0.2 us)
Async XLA Ops:
  7.2 87.0 %copy-start = (bf16[1,768,2048]{2,1,0:T(8,128)(2,1)S(1)}, bf16[1,768,2048]{2,1,0:T(8,128)(2,1)}, u32[]{:S(2)}) copy-start(bf16[1,768,2048]{2,1,0:T(8,128)(2,1)} %param.13) | copy-start | bytes 9437188
  13.8 13.3 %copy-start.6 = (bf16[64,2048]{1,0:T(8,128)(2,1)S(1)}, bf16[64,2048]{1,0:T(8,128)(2,1)}, u32[]{:S(2)}) copy-start(bf16[64,2048]{1,0:T(8,128)(2,1)} %param.10) | copy-start | bytes 786436
  13.8 64.5 %all-to-all-start = ((bf16[64,8,2048]{2,1,0:T(8,128)(2,1)}), bf16[64,8,2048]{2,1,0:T(8,128)(2,1)}, u32[]{:S(2)}, u32[]{:S(2)}) async-start(bf16[64,8,2048]{2,1,0:T(8,128)(2,1)} %fusion.19), calls=%async_computation | async-start | bytes 4194304 | tf_op jit(solution)/shard_map/all_to_all | solution.py:44
  29.6 4.8 %copy-start.7 = (f32[64,6]{0,1:T(8,128)S(1)}, f32[64,6]{0,1:T(8,128)}, u32[]{:S(2)}) copy-start(f32[64,6]{0,1:T(8,128)} %param.9) | copy-start | bytes 4612
  78.2 57.2 %all-to-all-start.1 = ((bf16[64,8,2048]{2,1,0:T(8,128)(2,1)}), bf16[64,8,2048]{2,1,0:T(8,128)(2,1)}, u32[]{:S(2)}, u32[]{:S(2)}) async-start(bf16[64,8,2048]{2,1,0:T(8,128)(2,1)} %fusion.20), calls=%async_computation.1 | async-start | bytes 4194304 | tf_op jit(solution)/shard_map/all_to_all | solution.py:44
  84.3 184.9 %reduce-scatter.3.cloned.1.call-start = ((), (), s32[]{:S(2)}) async-start(), calls=%async_computation.6 | async-start | bytes 3932160 | tf_op jit(solution)/shard_map/reduce_scatter | solution.py:100
  84.5 4.5 %copy-start.8 = (bf16[1,2048,768]{2,1,0:T(8,128)(2,1)S(1)}, bf16[1,2048,768]{2,1,0:T(8,128)(2,1)}, u32[]{:S(2)}) copy-start(bf16[1,2048,768]{2,1,0:T(8,128)(2,1)} %param.12) | copy-start | bytes 9437188
  89.0 5.2 %copy-start.15 = (f32[512,768]{1,0:T(8,128)}, f32[512,768]{1,0:T(8,128)S(1)}, u32[]{:S(2)}) copy-start(f32[512,768]{1,0:T(8,128)S(1)} %fusion.12) | copy-start | bytes 4718596
  94.2 3.3 %copy-start.13 = (bf16[512,768]{1,0:T(8,128)(2,1)}, bf16[512,768]{1,0:T(8,128)(2,1)S(1)}, u32[]{:S(2)}) copy-start(bf16[512,768]{1,0:T(8,128)(2,1)S(1)} %get-tuple-element.11) | copy-start | bytes 2359300
  141.0 0.9 copy-start.10
  147.0 6.3 %copy-start.12 = (bf16[512,768]{1,0:T(8,128)(2,1)S(1)}, bf16[512,768]{1,0:T(8,128)(2,1)}, u32[]{:S(2)}) copy-start(bf16[512,768]{1,0:T(8,128)(2,1)} %get-tuple-element.20) | copy-start | bytes 2359300
  147.0 57.2 %all-to-all-start.2 = ((bf16[64,8,2048]{2,1,0:T(8,128)(2,1)}), bf16[64,8,2048]{2,1,0:T(8,128)(2,1)S(1)}, u32[]{:S(2)}, u32[]{:S(2)}) async-start(bf16[64,8,2048]{2,1,0:T(8,128)(2,1)} %bitcast.128), calls=%async_computation.2 | async-start | bytes 4194304 | tf_op jit(solution)/shard_map/all_to_all | solution.py:44
  153.0 116.1 %reduce-scatter.5.cloned.1.call-start = ((), (), s32[]{:S(2)}) async-start(), calls=%async_computation.7 | async-start | bytes 3932160 | tf_op jit(solution)/shard_map/reduce_scatter | solution.py:103
  158.4 4.1 %copy-start.9 = (bf16[1,2048,768]{2,1,0:T(8,128)(2,1)S(1)}, bf16[1,2048,768]{2,1,0:T(8,128)(2,1)}, u32[]{:S(2)}) copy-start(bf16[1,2048,768]{2,1,0:T(8,128)(2,1)} %param.11) | copy-start | bytes 9437188
  158.4 4.1 %copy-start.11 = (bf16[512,768]{1,0:T(8,128)(2,1)S(1)}, bf16[512,768]{1,0:T(8,128)(2,1)}, u32[]{:S(2)}) copy-start(bf16[512,768]{1,0:T(8,128)(2,1)} %copy-done.10) | copy-start | bytes 2359300
  165.8 46.1 %copy-start.14 = (bf16[512,768]{1,0:T(8,128)(2,1)S(1)}, bf16[512,768]{1,0:T(8,128)(2,1)}, u32[]{:S(2)}) copy-start(bf16[512,768]{1,0:T(8,128)(2,1)} %copy-done.13) | copy-start | bytes 2359300
  204.3 1.3 copy-start.4
  205.6 57.2 %all-to-all-start.3 = ((bf16[64,8,2048]{2,1,0:T(8,128)(2,1)}), bf16[64,8,2048]{2,1,0:T(8,128)(2,1)}, u32[]{:S(2)}, u32[]{:S(2)}) async-start(bf16[64,8,2048]{2,1,0:T(8,128)(2,1)} %fusion.21), calls=%async_computation.3 | async-start | bytes 4194304 | tf_op jit(solution)/shard_map/all_to_all | solution.py:44
  215.3 3.4 %copy-start.5 = (bf16[64,8,2048]{2,1,0:T(8,128)(2,1)S(1)}, bf16[64,8,2048]{2,1,0:T(8,128)(2,1)}, u32[]{:S(2)}) copy-start(bf16[64,8,2048]{2,1,0:T(8,128)(2,1)} %copy-done.4) | copy-start | bytes 6291460
  215.6 29.2 %copy-start.3 = (bf16[768,1024]{1,0:T(8,128)(2,1)}, bf16[768,1024]{1,0:T(8,128)(2,1)S(1)}, u32[]{:S(2)}) copy-start(bf16[768,1024]{1,0:T(8,128)(2,1)S(1)} %get-tuple-element.18) | copy-start | bytes 4718596
  215.6 32.5 %copy-start.2 = (bf16[768,1024]{1,0:T(8,128)(2,1)}, bf16[768,1024]{1,0:T(8,128)(2,1)S(1)}, u32[]{:S(2)}) copy-start(bf16[768,1024]{1,0:T(8,128)(2,1)S(1)} %get-tuple-element.17) | copy-start | bytes 4718596
  215.7 18.7 %collective-permute-start.3 = (bf16[192,1024]{1,0:T(8,128)(2,1)S(1)}, bf16[192,1024]{1,0:T(8,128)(2,1)S(1)}, u32[]{:S(2)}, u32[]{:S(2)}) collective-permute-start(bf16[192,1024]{1,0:T(8,128)(2,1)S(1)} %dynamic-slice_bitcast_fusion), channel_id=1, source_target_pairs={{0,3},{1,0},{2,1},{3,2},{4,7},{5,4},{6,5},{7,6},{8,11},{9,8},{10,9... | collective-permute-start | bytes 1179656 | tf_op jit(solution)/shard_map/ppermute | solution.py:58
  218.6 17.3 %collective-permute-start = (bf16[192,1024]{1,0:T(8,128)(2,1)S(1)}, bf16[192,1024]{1,0:T(8,128)(2,1)S(1)}, u32[]{:S(2)}, u32[]{:S(2)}) collective-permute-start(bf16[192,1024]{1,0:T(8,128)(2,1)S(1)} %dynamic-slice_bitcast_fusion.1), channel_id=1, source_target_pairs={{0,1},{1,2},{2,3},{3,0},{4,5},{5,6},{6,7},{7,4},{8,9},{9,10},{10,1... | collective-permute-start | bytes 1179656 | tf_op jit(solution)/shard_map/ppermute | solution.py:58
  234.6 10.3 %collective-permute-start.4 = (bf16[192,1024]{1,0:T(8,128)(2,1)S(1)}, bf16[192,1024]{1,0:T(8,128)(2,1)S(1)}, u32[]{:S(2)}, u32[]{:S(2)}) collective-permute-start(bf16[192,1024]{1,0:T(8,128)(2,1)S(1)} %fusion.36), channel_id=1, source_target_pairs={{0,3},{1,0},{2,1},{3,2},{4,7},{5,4},{6,5},{7,6},{8,11},{9,8},{10,9... | collective-permute-start | bytes 1179656 | tf_op jit(solution)/shard_map/ppermute | solution.py:58
  236.0 12.2 %collective-permute-start.1 = (bf16[192,1024]{1,0:T(8,128)(2,1)S(1)}, bf16[192,1024]{1,0:T(8,128)(2,1)S(1)}, u32[]{:S(2)}, u32[]{:S(2)}) collective-permute-start(bf16[192,1024]{1,0:T(8,128)(2,1)S(1)} %fusion.39), channel_id=1, source_target_pairs={{0,1},{1,2},{2,3},{3,0},{4,5},{5,6},{6,7},{7,4},{8,9},{9,10},{10,1... | collective-permute-start | bytes 1179656 | tf_op jit(solution)/shard_map/ppermute | solution.py:58
  245.7 19.9 %collective-permute-start.5 = (bf16[192,1024]{1,0:T(8,128)(2,1)}, bf16[192,1024]{1,0:T(8,128)(2,1)}, u32[]{:S(2)}, u32[]{:S(2)}) collective-permute-start(bf16[192,1024]{1,0:T(8,128)(2,1)} %fusion.35), channel_id=1, source_target_pairs={{0,3},{1,0},{2,1},{3,2},{4,7},{5,4},{6,5},{7,6},{8,11},{9,8},{10,9... | collective-permute-start | bytes 1179656 | tf_op jit(solution)/shard_map/ppermute | solution.py:58
  249.1 17.8 %collective-permute-start.2 = (bf16[192,1024]{1,0:T(8,128)(2,1)}, bf16[192,1024]{1,0:T(8,128)(2,1)}, u32[]{:S(2)}, u32[]{:S(2)}) collective-permute-start(bf16[192,1024]{1,0:T(8,128)(2,1)} %fusion.38), channel_id=1, source_target_pairs={{0,1},{1,2},{2,3},{3,0},{4,5},{5,6},{6,7},{7,4},{8,9},{9,10},{10,1... | collective-permute-start | bytes 1179656 | tf_op jit(solution)/shard_map/ppermute | solution.py:58
  262.7 6.4 %copy-start.1 = (bf16[1,768,2048]{2,1,0:T(8,128)(2,1)S(1)}, bf16[1,768,2048]{2,1,0:T(8,128)(2,1)}, u32[]{:S(2)}) copy-start(bf16[1,768,2048]{2,1,0:T(8,128)(2,1)} %param.13) | copy-start | bytes 9437188
Sparse Core Ops, SparseCore 0:
  147.1 37.5 reduce-scatter.2
  187.8 46.3 reduce-scatter.4

commit v8 on v7

--- a/solution.py
+++ b/solution.py
@@ -106,14 +106,7 @@
     part_down, returned = lax.optimization_barrier(
         (outer_sum(activation, grads_in).astype(jnp.bfloat16), returned)
     )
-    half = features // 2
-    grad_down = jnp.concatenate(
-        [
-            ring_reduce_scatter(part_down[:, :half], 1),
-            ring_reduce_scatter(part_down[:, half:], -1),
-        ],
-        axis=1,
-    )[None]
+    grad_down = ring_reduce_scatter(part_down, 1)[None]
     picked = jnp.einsum("tkp,pd->tkd", pick3, returned, preferred_element_type=jnp.float32)
     combined = jnp.einsum("tk,tkd->td", gate_probs, picked).astype(jnp.bfloat16)
     grad_tokens = jnp.dot(owner, returned_grad, preferred_element_type=jnp.float32).astype(

time: 277 us -> 300 us (1.083)
  waiting for transfers between devices: 150 us -> 173 us
  starting transfers between devices: 39 us -> 33.1 us
    ppermute x6 -> x3, waiting for transfers between devices: 20.8 us -> 57.5 us  [ring_reduce_scatter(): acc = lax.ppermute(acc, 'replica', perm)]
    all_to_all x4, waiting for transfers between devices: 129 us -> 115 us  [exchange(): lax.all_to_all(blocks, 'expert', split_axis=0, concat_axis=0, tiled=True)]
    ppermute x6 -> x3, starting transfers between devices: 7.24 us -> 1.28 us  [ring_reduce_scatter(): acc = lax.ppermute(acc, 'replica', perm)]
  transfers between devices with their start and end apart: 12 -> 9, of which waited for: 6 -> 6; matrix products, arithmetic and copies ran while one was open for 19% -> 19% of each run, Pallas kernels for 0% -> 0%
where the time goes in v8:
time: 300 us; the launch traced here: 298 us
  waiting for transfers between devices  173 us (58%)
  matrix products  54.1 us (18%)
  starting transfers between devices  33.1 us (11%)
  between operations  14.3 us (5%)
  local copies, waits for them, and re-layouts  13.6 us (5%)
  other arithmetic  9.49 us (3%)
    all_to_all x4, waiting for transfers between devices, exchange(): lax.all_to_all(blocks, 'expert', split_axis=0, concat_axis=0, tiled=True)  115 us
    ppermute x3, waiting for transfers between devices, ring_reduce_scatter(): acc = lax.ppermute(acc, 'replica', perm)  57.5 us
    all_to_all x4, starting transfers between devices, exchange(): lax.all_to_all(blocks, 'expert', split_axis=0, concat_axis=0, tiled=True)  31.3 us
    dot_general x3, matrix products, outer_sum(): lax.dot_general(left, right, (((0,), (0,)), ((), ())), preferred_element_...  14.1 us
    mul x3, local copies, waits for them, and re-layouts, per_device(): gate_probs[:, :, None] * out_cot[:, None, :].astype(jnp.float32)  7.34 us
  transfers between devices with their start and end apart: 9, of which 6 were waited for; matrix products, arithmetic and copies ran while one was open for 19% of the time, Pallas kernels for 0%

profile of v8, /device:TPU:1, one launch (start us, length us, event | category | flops | bytes accessed | tf_op | source)
XLA Modules:
  0.0 297.5 jit_solution(5044092217756237915)
XLA Ops:
  7.2 0.0 copy-start
  7.2 0.9 copy.26
  8.1 0.1 eq.55
  8.2 0.1 eq.51
  8.4 0.9 reduce-window.6
  9.3 0.2 slice_reduce_fusion
  9.6 0.1 fusion.44
  9.7 0.1 reduce_sum.24
  9.8 0.1 copy.29
  9.9 0.7 multiply_add_fusion
  10.6 0.1 fusion.39
  10.8 3.0 %fusion.19 = bf16[64,8,2048]{2,1,0:T(8,128)(2,1)} fusion(bf16[64,512]{1,0:T(8,128)(2,1)S(1)} %fusion.39, bf16[64,2048]{1,0:T(8,128)(2,1)} %param.7), kind=kOutput, calls=%fused_computation.22 | convolution fusion | flops 135266304 | bytes 2424832 | tf_op jit(solution)/shard_map/dot_general | solution.py:79
  13.8 13.3 %all-to-all-start = ((bf16[64,8,2048]{2,1,0:T(8,128)(2,1)}), bf16[64,8,2048]{2,1,0:T(8,128)(2,1)}, u32[]{:S(2)}, u32[]{:S(2)}) async-start(bf16[64,8,2048]{2,1,0:T(8,128)(2,1)} %fusion.19), calls=%async_computation | async-start | bytes 4194304 | tf_op jit(solution)/shard_map/all_to_all | solution.py:44
  27.1 0.0 copy-done.2
  27.1 2.5 mul.70
  29.5 4.8 %mul.71 = f32[384,2048]{1,0:T(8,128)} reshape(f32[64,6,2048]{2,1,0:T(8,128)} %mul.70) | data formatting | bytes 6291456 | tf_op jit(solution)/shard_map/mul | solution.py:81
  34.3 0.0 copy-done.3
  34.3 0.1 copy.30
  34.4 0.1 mul.68
  34.5 4.6 %fusion.20 = bf16[64,8,2048]{2,1,0:T(8,128)(2,1)} fusion(f32[384,2048]{1,0:T(8,128)} %mul.71, f32[384]{0:T(512)S(1)} %mul.68, s32[384]{0:T(512)S(1)} %multiply_add_fusion.1), kind=kOutput, calls=%fused_computation.23 | convolution fusion | flops 808124416 | bytes 5245952 | tf_op jit(solution)/shard_map/dot_general | solution.py:82
  39.2 39.1 %all-to-all-done = bf16[64,8,2048]{2,1,0:T(8,128)(2,1)} async-done(((bf16[64,8,2048]{2,1,0:T(8,128)(2,1)}), bf16[64,8,2048]{2,1,0:T(8,128)(2,1)}, u32[]{:S(2)}, u32[]{:S(2)}) %all-to-all-start) | async-done | bytes 2097184 | tf_op jit(solution)/shard_map/all_to_all | solution.py:44
  78.2 6.0 %all-to-all-start.1 = ((bf16[64,8,2048]{2,1,0:T(8,128)(2,1)}), bf16[64,8,2048]{2,1,0:T(8,128)(2,1)}, u32[]{:S(2)}, u32[]{:S(2)}) async-start(bf16[64,8,2048]{2,1,0:T(8,128)(2,1)} %fusion.20), calls=%async_computation.1 | async-start | bytes 4194304 | tf_op jit(solution)/shard_map/all_to_all | solution.py:44
  84.2 0.2 reduce-scatter.3.cloned.1.call-start
  84.5 0.0 copy-start.4
  84.5 4.5 %fusion.12 = f32[512,768]{1,0:T(8,128)S(1)} fusion(bf16[1,2048,768]{2,1,0:T(8,128)(2,1)} %param.11, bf16[64,8,2048]{2,1,0:T(8,128)(2,1)} %all-to-all-done), kind=kOutput, calls=%fused_computation.16 | convolution fusion | flops 1610612736 | bytes 6815744 | tf_op jit(solution)/shard_map/dot_general | solution.py:16
  89.0 0.0 copy-done.4
  89.0 0.0 copy-start.9
  89.0 5.2 %multiply_convert_fusion.4 = (bf16[512,768]{1,0:T(8,128)(2,1)S(1)}, f32[512,768]{1,0:T(8,128)}) fusion(f32[512,768]{1,0:T(8,128)S(1)} %fusion.12, bf16[1,2048,768]{2,1,0:T(8,128)(2,1)S(1)} %copy-done.4, bf16[64,8,2048]{2,1,0:T(8,128)(2,1)} %all-to-all-done), kind=kOutput, calls=%fused_computation.45 | convolution fusion | flops 1612972032 | bytes 9175040 | tf_op jit(solution)/shard_map/dot_general | solution.py:17
  94.2 0.0 copy-done.9
  94.2 0.0 copy-done
  94.2 3.1 %fusion.14 = bf16[512,2048]{1,0:T(8,128)(2,1)} fusion(bf16[512,768]{1,0:T(8,128)(2,1)S(1)} %get-tuple-element.11, bf16[1,768,2048]{2,1,0:T(8,128)(2,1)S(1)} %copy-done), kind=kOutput, calls=%fused_computation.19 | convolution fusion | flops 1611661312 | bytes 6029312 | tf_op jit(solution)/shard_map/dot_general | solution.py:88
  97.3 0.0 copy-done.8
  97.3 38.1 %all-to-all-done.1 = bf16[64,8,2048]{2,1,0:T(8,128)(2,1)} async-done(((bf16[64,8,2048]{2,1,0:T(8,128)(2,1)}), bf16[64,8,2048]{2,1,0:T(8,128)(2,1)}, u32[]{:S(2)}, u32[]{:S(2)}) %all-to-all-start.1) | async-done | bytes 2097184 | tf_op jit(solution)/shard_map/all_to_all | solution.py:44
  135.4 5.6 %multiply_convert_fusion.3 = (bf16[512,768]{1,0:T(8,128)(2,1)S(1)}, bf16[512,768]{1,0:T(8,128)(2,1)}) fusion(f32[512,768]{1,0:T(8,128)} %copy-done.9, f32[512,768]{1,0:T(8,128)} %get-tuple-element.14, bf16[1,768,2048]{2,1,0:T(8,128)(2,1)S(1)} %copy-done, bf16[64,8,2048]{2,1,0:T(8,128)(2,1)} %all-to-all-done.1), kind=kOutput, calls=%fused_computation.42 | convolution fusion | flops 1615724544 | bytes 9961472 | tf_op jit(solution)/shard_map/dot_general | solution.py:24
  141.0 0.9 copy-done.6
  141.9 5.1 %convolution_convert_fusion.1 = bf16[2048,768]{1,0:T(8,128)(2,1)} fusion(bf16[512,768]{1,0:T(8,128)(2,1)S(1)} %get-tuple-element.17, bf16[64,8,2048]{2,1,0:T(8,128)(2,1)} %all-to-all-done), kind=kOutput, calls=%fused_computation.4 | convolution fusion | flops 1612185600 | bytes 6029312 | tf_op jit(solution)/shard_map/dot_general | solution.py:38
  147.0 0.0 reduce-scatter.3.cloned.1.call-update
  147.0 6.0 %all-to-all-start.2 = ((bf16[64,8,2048]{2,1,0:T(8,128)(2,1)}), bf16[64,8,2048]{2,1,0:T(8,128)(2,1)}, u32[]{:S(2)}, u32[]{:S(2)}) async-start(bf16[64,8,2048]{2,1,0:T(8,128)(2,1)} %bitcast.111), calls=%async_computation.2 | async-start | bytes 4194304 | tf_op jit(solution)/shard_map/all_to_all | solution.py:44
  153.0 0.3 reduce-scatter.5.cloned.1.call-start
  153.3 5.3 %convolution_convert_fusion = bf16[2048,768]{1,0:T(8,128)(2,1)} fusion(bf16[512,768]{1,0:T(8,128)(2,1)} %get-tuple-element.18, bf16[64,8,2048]{2,1,0:T(8,128)(2,1)} %all-to-all-done), kind=kOutput, calls=%fused_computation.3 | convolution fusion | flops 1612185600 | bytes 6029312 | tf_op jit(solution)/shard_map/dot_general | solution.py:38
  158.6 0.0 reduce-scatter.5.cloned.1.call-update
  158.6 0.0 copy-start.5
  158.6 4.1 %fusion.6 = f32[512,2048]{1,0:T(8,128)S(1)} fusion(bf16[512,768]{1,0:T(8,128)(2,1)} %get-tuple-element.18, bf16[1,2048,768]{2,1,0:T(8,128)(2,1)} %param.12), kind=kOutput, calls=%fused_computation.10 | convolution fusion | flops 1610612736 | bytes 8126464 | tf_op jit(solution)/shard_map/dot_general | solution.py:31
  162.8 3.1 %fusion.21 = bf16[64,8,2048]{2,1,0:T(8,128)(2,1)} fusion(f32[512,2048]{1,0:T(8,128)S(1)} %fusion.6, bf16[512,768]{1,0:T(8,128)(2,1)S(1)} %copy-done.7, bf16[1,2048,768]{2,1,0:T(8,128)(2,1)S(1)} %copy-done.5), kind=kOutput, calls=%fused_computation.24 | convolution fusion | flops 1612709888 | bytes 10223616 | tf_op jit(solution)/shard_map/dot_general | solution.py:30
  165.9 38.3 %all-to-all-done.2 = bf16[64,8,2048]{2,1,0:T(8,128)(2,1)} async-done(((bf16[64,8,2048]{2,1,0:T(8,128)(2,1)}), bf16[64,8,2048]{2,1,0:T(8,128)(2,1)}, u32[]{:S(2)}, u32[]{:S(2)}) %all-to-all-start.2) | async-done | bytes 2097184 | tf_op jit(solution)/shard_map/all_to_all | solution.py:44
  204.2 6.0 %all-to-all-start.3 = ((bf16[64,8,2048]{2,1,0:T(8,128)(2,1)}), bf16[64,8,2048]{2,1,0:T(8,128)(2,1)}, u32[]{:S(2)}, u32[]{:S(2)}) async-start(bf16[64,8,2048]{2,1,0:T(8,128)(2,1)} %fusion.21), calls=%async_computation.3 | async-start | bytes 4194304 | tf_op jit(solution)/shard_map/all_to_all | solution.py:44
  210.2 3.7 %convolution_convert_fusion.2 = bf16[768,2048]{1,0:T(8,128)(2,1)S(1)} fusion(bf16[512,768]{1,0:T(8,128)(2,1)} %copy-done.8, bf16[64,8,2048]{2,1,0:T(8,128)(2,1)} %all-to-all-done.1), kind=kOutput, calls=%fused_computation.5 | convolution fusion | flops 1612185600 | bytes 6029312 | tf_op jit(solution)/shard_map/dot_general | solution.py:38
  213.9 1.7 copy-done.1
  215.6 0.9 dynamic-slice_bitcast_fusion
  216.6 1.3 collective-permute-start
  217.8 26.2 %collective-permute-done = bf16[192,2048]{1,0:T(8,128)(2,1)} collective-permute-done((bf16[192,2048]{1,0:T(8,128)(2,1)}, bf16[192,2048]{1,0:T(8,128)(2,1)}, u32[]{:S(2)}, u32[]{:S(2)}) %collective-permute-start) | collective-permute-done | bytes 786464 | tf_op jit(solution)/shard_map/ppermute | solution.py:58
  244.1 2.5 fusion.35
  246.6 0.0 collective-permute-start.1
  246.6 0.1 copy.32
  246.7 19.8 %collective-permute-done.1 = bf16[192,2048]{1,0:T(8,128)(2,1)} collective-permute-done((bf16[192,2048]{1,0:T(8,128)(2,1)}, bf16[192,2048]{1,0:T(8,128)(2,1)}, u32[]{:S(2)}, u32[]{:S(2)}) %collective-permute-start.1) | collective-permute-done | bytes 786464 | tf_op jit(solution)/shard_map/ppermute | solution.py:58
  266.6 2.5 fusion.34
  269.1 0.0 collective-permute-start.2
  269.1 2.6 fusion.25
  271.7 1.3 fusion
  273.1 0.9 copy.39
  273.9 0.0 all-to-all-done.3
  273.9 2.8 convolution_convert_fusion.5
  276.7 11.4 %collective-permute-done.2 = bf16[192,2048]{1,0:T(8,128)(2,1)} collective-permute-done((bf16[192,2048]{1,0:T(8,128)(2,1)}, bf16[192,2048]{1,0:T(8,128)(2,1)}, u32[]{:S(2)}, u32[]{:S(2)}) %collective-permute-start.2) | collective-permute-done | bytes 786464 | tf_op jit(solution)/shard_map/ppermute | solution.py:58
  288.2 2.5 fusion.37
  (13 shorter events, 0.1 us)
Async XLA Ops:
  7.2 87.0 %copy-start = (bf16[1,768,2048]{2,1,0:T(8,128)(2,1)S(1)}, bf16[1,768,2048]{2,1,0:T(8,128)(2,1)}, u32[]{:S(2)}) copy-start(bf16[1,768,2048]{2,1,0:T(8,128)(2,1)} %param.13) | copy-start | bytes 9437188
  13.8 13.3 %copy-start.2 = (bf16[64,2048]{1,0:T(8,128)(2,1)S(1)}, bf16[64,2048]{1,0:T(8,128)(2,1)}, u32[]{:S(2)}) copy-start(bf16[64,2048]{1,0:T(8,128)(2,1)} %param.10) | copy-start | bytes 786436
  13.8 64.5 %all-to-all-start = ((bf16[64,8,2048]{2,1,0:T(8,128)(2,1)}), bf16[64,8,2048]{2,1,0:T(8,128)(2,1)}, u32[]{:S(2)}, u32[]{:S(2)}) async-start(bf16[64,8,2048]{2,1,0:T(8,128)(2,1)} %fusion.19), calls=%async_computation | async-start | bytes 4194304 | tf_op jit(solution)/shard_map/all_to_all | solution.py:44
  29.5 4.8 %copy-start.3 = (f32[64,6]{0,1:T(8,128)S(1)}, f32[64,6]{0,1:T(8,128)}, u32[]{:S(2)}) copy-start(f32[64,6]{0,1:T(8,128)} %param.9) | copy-start | bytes 4612
  78.2 57.2 %all-to-all-start.1 = ((bf16[64,8,2048]{2,1,0:T(8,128)(2,1)}), bf16[64,8,2048]{2,1,0:T(8,128)(2,1)}, u32[]{:S(2)}, u32[]{:S(2)}) async-start(bf16[64,8,2048]{2,1,0:T(8,128)(2,1)} %fusion.20), calls=%async_computation.1 | async-start | bytes 4194304 | tf_op jit(solution)/shard_map/all_to_all | solution.py:44
  84.2 206.4 %reduce-scatter.3.cloned.1.call-start = ((), (), s32[]{:S(2)}) async-start(), calls=%async_computation.6 | async-start | bytes 3932160 | tf_op jit(solution)/shard_map/reduce_scatter | solution.py:100
  84.5 4.5 %copy-start.4 = (bf16[1,2048,768]{2,1,0:T(8,128)(2,1)S(1)}, bf16[1,2048,768]{2,1,0:T(8,128)(2,1)}, u32[]{:S(2)}) copy-start(bf16[1,2048,768]{2,1,0:T(8,128)(2,1)} %param.12) | copy-start | bytes 9437188
  89.0 5.2 %copy-start.9 = (f32[512,768]{1,0:T(8,128)}, f32[512,768]{1,0:T(8,128)S(1)}, u32[]{:S(2)}) copy-start(f32[512,768]{1,0:T(8,128)S(1)} %fusion.12) | copy-start | bytes 4718596
  94.2 3.1 %copy-start.8 = (bf16[512,768]{1,0:T(8,128)(2,1)}, bf16[512,768]{1,0:T(8,128)(2,1)S(1)}, u32[]{:S(2)}) copy-start(bf16[512,768]{1,0:T(8,128)(2,1)S(1)} %get-tuple-element.11) | copy-start | bytes 2359300
  141.0 0.9 copy-start.6
  147.0 57.2 %all-to-all-start.2 = ((bf16[64,8,2048]{2,1,0:T(8,128)(2,1)}), bf16[64,8,2048]{2,1,0:T(8,128)(2,1)}, u32[]{:S(2)}, u32[]{:S(2)}) async-start(bf16[64,8,2048]{2,1,0:T(8,128)(2,1)} %bitcast.111), calls=%async_computation.2 | async-start | bytes 4194304 | tf_op jit(solution)/shard_map/all_to_all | solution.py:44
  153.0 137.7 %reduce-scatter.5.cloned.1.call-start = ((), (), s32[]{:S(2)}) async-start(), calls=%async_computation.7 | async-start | bytes 3932160 | tf_op jit(solution)/shard_map/reduce_scatter | solution.py:103
  158.6 4.1 %copy-start.5 = (bf16[1,2048,768]{2,1,0:T(8,128)(2,1)S(1)}, bf16[1,2048,768]{2,1,0:T(8,128)(2,1)}, u32[]{:S(2)}) copy-start(bf16[1,2048,768]{2,1,0:T(8,128)(2,1)} %param.11) | copy-start | bytes 9437188
  158.6 4.1 %copy-start.7 = (bf16[512,768]{1,0:T(8,128)(2,1)S(1)}, bf16[512,768]{1,0:T(8,128)(2,1)}, u32[]{:S(2)}) copy-start(bf16[512,768]{1,0:T(8,128)(2,1)} %copy-done.6) | copy-start | bytes 2359300
  204.2 69.8 %all-to-all-start.3 = ((bf16[64,8,2048]{2,1,0:T(8,128)(2,1)}), bf16[64,8,2048]{2,1,0:T(8,128)(2,1)}, u32[]{:S(2)}, u32[]{:S(2)}) async-start(bf16[64,8,2048]{2,1,0:T(8,128)(2,1)} %fusion.21), calls=%async_computation.3 | async-start | bytes 4194304 | tf_op jit(solution)/shard_map/all_to_all | solution.py:44
  213.9 1.7 copy-start.1
  216.6 27.5 %collective-permute-start = (bf16[192,2048]{1,0:T(8,128)(2,1)}, bf16[192,2048]{1,0:T(8,128)(2,1)}, u32[]{:S(2)}, u32[]{:S(2)}) collective-permute-start(bf16[192,2048]{1,0:T(8,128)(2,1)} %dynamic-slice_bitcast_fusion), channel_id=1, source_target_pairs={{0,1},{1,2},{2,3},{3,0},{4,5},{5,6},{6,7},{7,4},{8,9},{9,10},{10,1... | collective-permute-start | bytes 2359304 | tf_op jit(solution)/shard_map/ppermute | solution.py:58
  246.6 20.0 %collective-permute-start.1 = (bf16[192,2048]{1,0:T(8,128)(2,1)}, bf16[192,2048]{1,0:T(8,128)(2,1)}, u32[]{:S(2)}, u32[]{:S(2)}) collective-permute-start(bf16[192,2048]{1,0:T(8,128)(2,1)} %fusion.35), channel_id=1, source_target_pairs={{0,1},{1,2},{2,3},{3,0},{4,5},{5,6},{6,7},{7,4},{8,9},{9,10},{10,1... | collective-permute-start | bytes 2359304 | tf_op jit(solution)/shard_map/ppermute | solution.py:58
  269.1 19.0 %collective-permute-start.2 = (bf16[192,2048]{1,0:T(8,128)(2,1)}, bf16[192,2048]{1,0:T(8,128)(2,1)}, u32[]{:S(2)}, u32[]{:S(2)}) collective-permute-start(bf16[192,2048]{1,0:T(8,128)(2,1)} %fusion.34), channel_id=1, source_target_pairs={{0,1},{1,2},{2,3},{3,0},{4,5},{5,6},{6,7},{7,4},{8,9},{9,10},{10,1... | collective-permute-start | bytes 2359304 | tf_op jit(solution)/shard_map/ppermute | solution.py:58
Sparse Core Ops, SparseCore 0:
  147.1 37.5 reduce-scatter.2
  187.8 46.5 reduce-scatter.4

commit v9 on v8

--- a/solution.py
+++ b/solution.py
@@ -44,20 +44,25 @@
     return lax.all_to_all(blocks, "expert", split_axis=0, concat_axis=0, tiled=True)
 
 
-def ring_reduce_scatter(part, direction):
+def chain_reduce_scatter(part):
     n = lax.axis_size("replica")
     me = lax.axis_index("replica")
     table = part.reshape((n, part.shape[0] // n) + part.shape[1:])
-    perm = [(i, (i + direction) % n) for i in range(n)]
 
-    def own(step):
-        return lax.dynamic_index_in_dim(table, (me - direction * (step + 1)) % n, 0, False)
+    def own(offset):
+        return lax.dynamic_index_in_dim(table, (me + offset) % n, 0, False).astype(jnp.float32)
 
-    acc = own(0)
-    for step in range(1, n):
-        acc = lax.ppermute(acc, "replica", perm)
-        acc = (acc.astype(jnp.float32) + own(step).astype(jnp.float32)).astype(jnp.bfloat16)
-    return acc
+    total = own(0)
+    for direction, length in ((1, (n - 1 + 1) // 2), (-1, (n - 1) // 2)):
+        if length == 0:
+            continue
+        perm = [(i, (i + direction) % n) for i in range(n)]
+        acc = own(direction * length)
+        for step in range(1, length):
+            acc = lax.ppermute(acc.astype(jnp.bfloat16), "replica", perm).astype(jnp.float32)
+            acc = acc + own(direction * (length - step))
+        total = total + lax.ppermute(acc.astype(jnp.bfloat16), "replica", perm).astype(jnp.float32)
+    return total.astype(jnp.bfloat16)
 
 
 def per_device(tokens, route_ids, gate_probs, out_cot, w_gate, w_up, w_down):
@@ -106,7 +111,7 @@
     part_down, returned = lax.optimization_barrier(
         (outer_sum(activation, grads_in).astype(jnp.bfloat16), returned)
     )
-    grad_down = ring_reduce_scatter(part_down, 1)[None]
+    grad_down = chain_reduce_scatter(part_down)[None]
     picked = jnp.einsum("tkp,pd->tkd", pick3, returned, preferred_element_type=jnp.float32)
     combined = jnp.einsum("tk,tkd->td", gate_probs, picked).astype(jnp.bfloat16)
     grad_tokens = jnp.dot(owner, returned_grad, preferred_element_type=jnp.float32).astype(

time: 300 us -> 277 us (0.923)
  waiting for transfers between devices: 173 us -> 152 us
    ppermute x3, waiting for transfers between devices: 57.5 us -> 26.7 us  [chain_reduce_scatter(): lax.ppermute(acc.astype(jnp.bfloat16), 'replica', perm).astype(jnp.float32)]
    all_to_all x4, waiting for transfers between devices: 115 us -> 125 us  [exchange(): lax.all_to_all(blocks, 'expert', split_axis=0, concat_axis=0, tiled=True)]
  transfers between devices with their start and end apart: 9 -> 9, of which waited for: 6 -> 6; matrix products, arithmetic and copies ran while one was open for 19% -> 20% of each run, Pallas kernels for 0% -> 0%
where the time goes in v9:
time: 277 us; the launch traced here: 276 us
  waiting for transfers between devices  152 us (55%)
  matrix products  54 us (19%)
  starting transfers between devices  34.6 us (12%)
  between operations  14.3 us (5%)
  local copies, waits for them, and re-layouts  13.9 us (5%)
  other arithmetic  7.33 us (3%)
    all_to_all x4, waiting for transfers between devices, exchange(): lax.all_to_all(blocks, 'expert', split_axis=0, concat_axis=0, tiled=True)  125 us
    all_to_all x4, starting transfers between devices, exchange(): lax.all_to_all(blocks, 'expert', split_axis=0, concat_axis=0, tiled=True)  31.3 us
    ppermute x3, waiting for transfers between devices, chain_reduce_scatter(): lax.ppermute(acc.astype(jnp.bfloat16), 'replica', perm).astype(jnp.float32)  26.7 us
    dot_general x3, matrix products, outer_sum(): lax.dot_general(left, right, (((0,), (0,)), ((), ())), preferred_element_...  14.1 us
    mul x3, local copies, waits for them, and re-layouts, per_device(): gate_probs[:, :, None] * out_cot[:, None, :].astype(jnp.float32)  7.35 us
    dot_general x1, matrix products, backward_rows(): lax.dot_general(grad_rows, down_weight, contract, preferred_element_type=...  5.6 us
  transfers between devices with their start and end apart: 9, of which 6 were waited for; matrix products, arithmetic and copies ran while one was open for 20% of the time, Pallas kernels for 0%

profile of v9, /device:TPU:1, one launch (start us, length us, event | category | flops | bytes accessed | tf_op | source)
XLA Modules:
  0.0 276.3 jit_solution(2629672242940749028)
XLA Ops:
  7.2 0.0 copy-start
  7.2 0.9 copy.26
  8.1 0.1 eq.55
  8.2 0.1 eq.51
  8.4 0.9 reduce-window.6
  9.3 0.2 slice_reduce_fusion
  9.6 0.1 fusion.44
  9.7 0.1 reduce_sum.24
  9.8 0.1 copy.29
  9.9 0.7 multiply_add_fusion
  10.6 0.1 fusion.39
  10.8 3.0 %fusion.19 = bf16[64,8,2048]{2,1,0:T(8,128)(2,1)} fusion(bf16[64,512]{1,0:T(8,128)(2,1)S(1)} %fusion.39, bf16[64,2048]{1,0:T(8,128)(2,1)} %param.7), kind=kOutput, calls=%fused_computation.22 | convolution fusion | flops 135266304 | bytes 2424832 | tf_op jit(solution)/shard_map/dot_general | solution.py:84
  13.8 13.3 %all-to-all-start = ((bf16[64,8,2048]{2,1,0:T(8,128)(2,1)}), bf16[64,8,2048]{2,1,0:T(8,128)(2,1)}, u32[]{:S(2)}, u32[]{:S(2)}) async-start(bf16[64,8,2048]{2,1,0:T(8,128)(2,1)} %fusion.19), calls=%async_computation | async-start | bytes 4194304 | tf_op jit(solution)/shard_map/all_to_all | solution.py:44
  27.1 0.0 copy-done.2
  27.1 2.5 mul.70
  29.5 4.7 %mul.71 = f32[384,2048]{1,0:T(8,128)} reshape(f32[64,6,2048]{2,1,0:T(8,128)} %mul.70) | data formatting | bytes 6291456 | tf_op jit(solution)/shard_map/mul | solution.py:86
  34.3 0.0 copy-done.3
  34.3 0.1 copy.30
  34.4 0.1 mul.68
  34.5 4.6 %fusion.20 = bf16[64,8,2048]{2,1,0:T(8,128)(2,1)} fusion(f32[384,2048]{1,0:T(8,128)} %mul.71, f32[384]{0:T(512)S(1)} %mul.68, s32[384]{0:T(512)S(1)} %multiply_add_fusion.1), kind=kOutput, calls=%fused_computation.23 | convolution fusion | flops 808124416 | bytes 5245952 | tf_op jit(solution)/shard_map/dot_general | solution.py:87
  39.2 39.1 %all-to-all-done = bf16[64,8,2048]{2,1,0:T(8,128)(2,1)} async-done(((bf16[64,8,2048]{2,1,0:T(8,128)(2,1)}), bf16[64,8,2048]{2,1,0:T(8,128)(2,1)}, u32[]{:S(2)}, u32[]{:S(2)}) %all-to-all-start) | async-done | bytes 2097184 | tf_op jit(solution)/shard_map/all_to_all | solution.py:44
  78.2 6.0 %all-to-all-start.1 = ((bf16[64,8,2048]{2,1,0:T(8,128)(2,1)}), bf16[64,8,2048]{2,1,0:T(8,128)(2,1)}, u32[]{:S(2)}, u32[]{:S(2)}) async-start(bf16[64,8,2048]{2,1,0:T(8,128)(2,1)} %fusion.20), calls=%async_computation.1 | async-start | bytes 4194304 | tf_op jit(solution)/shard_map/all_to_all | solution.py:44
  84.2 0.2 reduce-scatter.3.cloned.1.call-start
  84.5 0.0 copy-start.4
  84.5 4.5 %fusion.12 = f32[512,768]{1,0:T(8,128)S(1)} fusion(bf16[1,2048,768]{2,1,0:T(8,128)(2,1)} %param.11, bf16[64,8,2048]{2,1,0:T(8,128)(2,1)} %all-to-all-done), kind=kOutput, calls=%fused_computation.16 | convolution fusion | flops 1610612736 | bytes 6815744 | tf_op jit(solution)/shard_map/dot_general | solution.py:16
  88.9 0.0 copy-done.4
  89.0 0.0 copy-start.9
  89.0 5.2 %multiply_convert_fusion.4 = (bf16[512,768]{1,0:T(8,128)(2,1)S(1)}, f32[512,768]{1,0:T(8,128)}) fusion(f32[512,768]{1,0:T(8,128)S(1)} %fusion.12, bf16[1,2048,768]{2,1,0:T(8,128)(2,1)S(1)} %copy-done.4, bf16[64,8,2048]{2,1,0:T(8,128)(2,1)} %all-to-all-done), kind=kOutput, calls=%fused_computation.44 | convolution fusion | flops 1612972032 | bytes 9175040 | tf_op jit(solution)/shard_map/dot_general | solution.py:17
  94.2 0.0 copy-done.9
  94.2 0.0 copy-done
  94.2 3.1 %fusion.14 = bf16[512,2048]{1,0:T(8,128)(2,1)} fusion(bf16[512,768]{1,0:T(8,128)(2,1)S(1)} %get-tuple-element.11, bf16[1,768,2048]{2,1,0:T(8,128)(2,1)S(1)} %copy-done), kind=kOutput, calls=%fused_computation.19 | convolution fusion | flops 1611661312 | bytes 6029312 | tf_op jit(solution)/shard_map/dot_general | solution.py:93
  97.3 0.0 copy-done.8
  97.3 38.1 %all-to-all-done.1 = bf16[64,8,2048]{2,1,0:T(8,128)(2,1)} async-done(((bf16[64,8,2048]{2,1,0:T(8,128)(2,1)}), bf16[64,8,2048]{2,1,0:T(8,128)(2,1)}, u32[]{:S(2)}, u32[]{:S(2)}) %all-to-all-start.1) | async-done | bytes 2097184 | tf_op jit(solution)/shard_map/all_to_all | solution.py:44
  135.4 5.6 %multiply_convert_fusion.3 = (bf16[512,768]{1,0:T(8,128)(2,1)S(1)}, bf16[512,768]{1,0:T(8,128)(2,1)}) fusion(f32[512,768]{1,0:T(8,128)} %copy-done.9, f32[512,768]{1,0:T(8,128)} %get-tuple-element.14, bf16[1,768,2048]{2,1,0:T(8,128)(2,1)S(1)} %copy-done, bf16[64,8,2048]{2,1,0:T(8,128)(2,1)} %all-to-all-done.1), kind=kOutput, calls=%fused_computation.41 | convolution fusion | flops 1615724544 | bytes 9961472 | tf_op jit(solution)/shard_map/dot_general | solution.py:24
  141.0 0.9 copy-done.6
  141.9 5.1 %convolution_convert_fusion.1 = bf16[2048,768]{1,0:T(8,128)(2,1)} fusion(bf16[512,768]{1,0:T(8,128)(2,1)S(1)} %get-tuple-element.19, bf16[64,8,2048]{2,1,0:T(8,128)(2,1)} %all-to-all-done), kind=kOutput, calls=%fused_computation.4 | convolution fusion | flops 1612185600 | bytes 6029312 | tf_op jit(solution)/shard_map/dot_general | solution.py:38
  147.0 0.0 reduce-scatter.3.cloned.1.call-update
  147.0 6.0 %all-to-all-start.2 = ((bf16[64,8,2048]{2,1,0:T(8,128)(2,1)}), bf16[64,8,2048]{2,1,0:T(8,128)(2,1)}, u32[]{:S(2)}, u32[]{:S(2)}) async-start(bf16[64,8,2048]{2,1,0:T(8,128)(2,1)} %bitcast.109), calls=%async_computation.2 | async-start | bytes 4194304 | tf_op jit(solution)/shard_map/all_to_all | solution.py:44
  153.0 0.3 reduce-scatter.5.cloned.1.call-start
  153.3 5.3 %convolution_convert_fusion = bf16[2048,768]{1,0:T(8,128)(2,1)} fusion(bf16[512,768]{1,0:T(8,128)(2,1)} %get-tuple-element.20, bf16[64,8,2048]{2,1,0:T(8,128)(2,1)} %all-to-all-done), kind=kOutput, calls=%fused_computation.3 | convolution fusion | flops 1612185600 | bytes 6029312 | tf_op jit(solution)/shard_map/dot_general | solution.py:38
  158.6 0.0 reduce-scatter.5.cloned.1.call-update
  158.6 0.0 copy-start.5
  158.6 0.0 copy-start.7
  158.6 4.1 %fusion.6 = f32[512,2048]{1,0:T(8,128)S(1)} fusion(bf16[512,768]{1,0:T(8,128)(2,1)} %get-tuple-element.20, bf16[1,2048,768]{2,1,0:T(8,128)(2,1)} %param.12), kind=kOutput, calls=%fused_computation.10 | convolution fusion | flops 1610612736 | bytes 8126464 | tf_op jit(solution)/shard_map/dot_general | solution.py:31
  162.7 3.1 %fusion.21 = bf16[64,8,2048]{2,1,0:T(8,128)(2,1)} fusion(f32[512,2048]{1,0:T(8,128)S(1)} %fusion.6, bf16[512,768]{1,0:T(8,128)(2,1)S(1)} %copy-done.7, bf16[1,2048,768]{2,1,0:T(8,128)(2,1)S(1)} %copy-done.5), kind=kOutput, calls=%fused_computation.24 | convolution fusion | flops 1612709888 | bytes 10223616 | tf_op jit(solution)/shard_map/dot_general | solution.py:30
  165.9 38.3 %all-to-all-done.2 = bf16[64,8,2048]{2,1,0:T(8,128)(2,1)} async-done(((bf16[64,8,2048]{2,1,0:T(8,128)(2,1)}), bf16[64,8,2048]{2,1,0:T(8,128)(2,1)}, u32[]{:S(2)}, u32[]{:S(2)}) %all-to-all-start.2) | async-done | bytes 2097184 | tf_op jit(solution)/shard_map/all_to_all | solution.py:44
  204.2 6.0 %all-to-all-start.3 = ((bf16[64,8,2048]{2,1,0:T(8,128)(2,1)}), bf16[64,8,2048]{2,1,0:T(8,128)(2,1)}, u32[]{:S(2)}, u32[]{:S(2)}) async-start(bf16[64,8,2048]{2,1,0:T(8,128)(2,1)} %fusion.21), calls=%async_computation.3 | async-start | bytes 4194304 | tf_op jit(solution)/shard_map/all_to_all | solution.py:44
  210.2 3.7 %convolution_convert_fusion.2 = bf16[768,2048]{1,0:T(8,128)(2,1)S(1)} fusion(bf16[512,768]{1,0:T(8,128)(2,1)} %copy-done.8, bf16[64,8,2048]{2,1,0:T(8,128)(2,1)} %all-to-all-done.1), kind=kOutput, calls=%fused_computation.5 | convolution fusion | flops 1612185600 | bytes 6029312 | tf_op jit(solution)/shard_map/dot_general | solution.py:38
  213.9 1.7 copy-done.1
  215.6 1.2 dynamic-slice_bitcast_fusion.1
  216.9 1.3 collective-permute-start
  218.2 0.1 copy.32
  218.3 1.5 collective-permute-start.2
  219.8 24.3 %collective-permute-done = bf16[192,2048]{1,0:T(8,128)(2,1)} collective-permute-done((bf16[192,2048]{1,0:T(8,128)(2,1)}, bf16[192,2048]{1,0:T(8,128)(2,1)}, u32[]{:S(2)}, u32[]{:S(2)}) %collective-permute-start) | collective-permute-done | bytes 786464 | tf_op jit(solution)/shard_map/ppermute | solution.py:62
  244.1 2.5 fusion.33
  246.6 0.0 collective-permute-start.1
  246.6 2.6 fusion.25
  249.2 1.3 fusion
  250.6 0.9 copy.39
  251.4 9.9 %all-to-all-done.3 = bf16[64,8,2048]{2,1,0:T(8,128)(2,1)} async-done(((bf16[64,8,2048]{2,1,0:T(8,128)(2,1)}), bf16[64,8,2048]{2,1,0:T(8,128)(2,1)}, u32[]{:S(2)}, u32[]{:S(2)}) %all-to-all-start.3) | async-done | bytes 2097184 | tf_op jit(solution)/shard_map/all_to_all | solution.py:44
  261.4 2.8 %convolution_convert_fusion.5 = bf16[64,2048]{1,0:T(8,128)(2,1)} fusion(bf16[64,512]{1,0:T(8,128)(2,1)S(1)} %fusion.39, bf16[64,8,2048]{2,1,0:T(8,128)(2,1)} %all-to-all-done.3), kind=kOutput, calls=%fused_computation.25 | convolution fusion | flops 134348800 | bytes 2424832 | tf_op jit(solution)/shard_map/dot_general | solution.py:117
  264.1 0.0 collective-permute-done.2
  264.1 2.4 collective-permute-done.1
  266.6 2.9 %fusion.37 = bf16[1,192,2048]{2,1,0:T(8,128)(2,1)} fusion(bf16[192,2048]{1,0:T(8,128)(2,1)} %collective-permute-done.2, bf16[192,2048]{1,0:T(8,128)(2,1)} %collective-permute-done.1, bf16[4,192,2048]{2,1,0:T(8,128)(2,1)} %bitcast.108, s32[]{:T(128)S(6)} %select_n.33), kind=kLoop, calls=%fused_computation.45 | loop fusion | flops 2359296 | bytes 3145732 | tf_op jit(solution)/shard_map/broadcast_in_dim | solution.py:114
  (12 shorter events, 0.1 us)
Async XLA Ops:
  7.2 87.0 %copy-start = (bf16[1,768,2048]{2,1,0:T(8,128)(2,1)S(1)}, bf16[1,768,2048]{2,1,0:T(8,128)(2,1)}, u32[]{:S(2)}) copy-start(bf16[1,768,2048]{2,1,0:T(8,128)(2,1)} %param.13) | copy-start | bytes 9437188
  13.8 13.3 %copy-start.2 = (bf16[64,2048]{1,0:T(8,128)(2,1)S(1)}, bf16[64,2048]{1,0:T(8,128)(2,1)}, u32[]{:S(2)}) copy-start(bf16[64,2048]{1,0:T(8,128)(2,1)} %param.10) | copy-start | bytes 786436
  13.8 64.5 %all-to-all-start = ((bf16[64,8,2048]{2,1,0:T(8,128)(2,1)}), bf16[64,8,2048]{2,1,0:T(8,128)(2,1)}, u32[]{:S(2)}, u32[]{:S(2)}) async-start(bf16[64,8,2048]{2,1,0:T(8,128)(2,1)} %fusion.19), calls=%async_computation | async-start | bytes 4194304 | tf_op jit(solution)/shard_map/all_to_all | solution.py:44
  29.5 4.8 %copy-start.3 = (f32[64,6]{0,1:T(8,128)S(1)}, f32[64,6]{0,1:T(8,128)}, u32[]{:S(2)}) copy-start(f32[64,6]{0,1:T(8,128)} %param.9) | copy-start | bytes 4612
  78.2 57.2 %all-to-all-start.1 = ((bf16[64,8,2048]{2,1,0:T(8,128)(2,1)}), bf16[64,8,2048]{2,1,0:T(8,128)(2,1)}, u32[]{:S(2)}, u32[]{:S(2)}) async-start(bf16[64,8,2048]{2,1,0:T(8,128)(2,1)} %fusion.20), calls=%async_computation.1 | async-start | bytes 4194304 | tf_op jit(solution)/shard_map/all_to_all | solution.py:44
  84.2 185.2 %reduce-scatter.3.cloned.1.call-start = ((), (), s32[]{:S(2)}) async-start(), calls=%async_computation.6 | async-start | bytes 3932160 | tf_op jit(solution)/shard_map/reduce_scatter | solution.py:105
  84.5 4.5 %copy-start.4 = (bf16[1,2048,768]{2,1,0:T(8,128)(2,1)S(1)}, bf16[1,2048,768]{2,1,0:T(8,128)(2,1)}, u32[]{:S(2)}) copy-start(bf16[1,2048,768]{2,1,0:T(8,128)(2,1)} %param.12) | copy-start | bytes 9437188
  89.0 5.2 %copy-start.9 = (f32[512,768]{1,0:T(8,128)}, f32[512,768]{1,0:T(8,128)S(1)}, u32[]{:S(2)}) copy-start(f32[512,768]{1,0:T(8,128)S(1)} %fusion.12) | copy-start | bytes 4718596
  94.2 3.1 %copy-start.8 = (bf16[512,768]{1,0:T(8,128)(2,1)}, bf16[512,768]{1,0:T(8,128)(2,1)S(1)}, u32[]{:S(2)}) copy-start(bf16[512,768]{1,0:T(8,128)(2,1)S(1)} %get-tuple-element.11) | copy-start | bytes 2359300
  141.0 0.9 copy-start.6
  147.0 57.2 %all-to-all-start.2 = ((bf16[64,8,2048]{2,1,0:T(8,128)(2,1)}), bf16[64,8,2048]{2,1,0:T(8,128)(2,1)}, u32[]{:S(2)}, u32[]{:S(2)}) async-start(bf16[64,8,2048]{2,1,0:T(8,128)(2,1)} %bitcast.109), calls=%async_computation.2 | async-start | bytes 4194304 | tf_op jit(solution)/shard_map/all_to_all | solution.py:44
  153.0 116.4 %reduce-scatter.5.cloned.1.call-start = ((), (), s32[]{:S(2)}) async-start(), calls=%async_computation.7 | async-start | bytes 3932160 | tf_op jit(solution)/shard_map/reduce_scatter | solution.py:108
  158.6 4.1 %copy-start.5 = (bf16[1,2048,768]{2,1,0:T(8,128)(2,1)S(1)}, bf16[1,2048,768]{2,1,0:T(8,128)(2,1)}, u32[]{:S(2)}) copy-start(bf16[1,2048,768]{2,1,0:T(8,128)(2,1)} %param.11) | copy-start | bytes 9437188
  158.6 4.1 %copy-start.7 = (bf16[512,768]{1,0:T(8,128)(2,1)S(1)}, bf16[512,768]{1,0:T(8,128)(2,1)}, u32[]{:S(2)}) copy-start(bf16[512,768]{1,0:T(8,128)(2,1)} %copy-done.6) | copy-start | bytes 2359300
  204.2 57.2 %all-to-all-start.3 = ((bf16[64,8,2048]{2,1,0:T(8,128)(2,1)}), bf16[64,8,2048]{2,1,0:T(8,128)(2,1)}, u32[]{:S(2)}, u32[]{:S(2)}) async-start(bf16[64,8,2048]{2,1,0:T(8,128)(2,1)} %fusion.21), calls=%async_computation.3 | async-start | bytes 4194304 | tf_op jit(solution)/shard_map/all_to_all | solution.py:44
  213.9 1.7 copy-start.1
  216.9 27.2 %collective-permute-start = (bf16[192,2048]{1,0:T(8,128)(2,1)}, bf16[192,2048]{1,0:T(8,128)(2,1)}, u32[]{:S(2)}, u32[]{:S(2)}) collective-permute-start(bf16[192,2048]{1,0:T(8,128)(2,1)} %get-tuple-element.17), channel_id=1, source_target_pairs={{0,1},{1,2},{2,3},{3,0},{4,5},{5,6},{6,7},{7,4},{8,9},{9,10},{10,1... | collective-permute-start | bytes 2359304 | tf_op jit(solution)/shard_map/ppermute | solution.py:62
  218.3 45.8 %collective-permute-start.2 = (bf16[192,2048]{1,0:T(8,128)(2,1)}, bf16[192,2048]{1,0:T(8,128)(2,1)}, u32[]{:S(2)}, u32[]{:S(2)}) collective-permute-start(bf16[192,2048]{1,0:T(8,128)(2,1)} %get-tuple-element.18), channel_id=1, source_target_pairs={{0,3},{1,0},{2,1},{3,2},{4,7},{5,4},{6,5},{7,6},{8,11},{9,8},{10,9... | collective-permute-start | bytes 2359304 | tf_op jit(solution)/shard_map/ppermute | solution.py:64
  246.6 20.0 %collective-permute-start.1 = (bf16[192,2048]{1,0:T(8,128)(2,1)}, bf16[192,2048]{1,0:T(8,128)(2,1)}, u32[]{:S(2)}, u32[]{:S(2)}) collective-permute-start(bf16[192,2048]{1,0:T(8,128)(2,1)} %fusion.33), channel_id=1, source_target_pairs={{0,1},{1,2},{2,3},{3,0},{4,5},{5,6},{6,7},{7,4},{8,9},{9,10},{10,1... | collective-permute-start | bytes 2359304 | tf_op jit(solution)/shard_map/ppermute | solution.py:64
Sparse Core Ops, SparseCore 0:
  147.1 37.5 reduce-scatter.2
  187.8 46.2 reduce-scatter.4

commit v10 on v9

--- a/solution.py
+++ b/solution.py
@@ -100,7 +100,6 @@
     back_rows, d_gate, d_up = backward_rows(
         grads_in, pre_gate, pre_up, gate_weight, up_weight, down_weight
     )
-    returned_grad = exchange(back_rows.reshape(experts, capacity, features)).reshape(-1, features)
 
     grad_gate = lax.psum_scatter(
         outer_sum(slot_rows, d_gate).astype(jnp.bfloat16), "replica", scatter_dimension=0, tiled=True
@@ -108,9 +107,10 @@
     grad_up = lax.psum_scatter(
         outer_sum(slot_rows, d_up).astype(jnp.bfloat16), "replica", scatter_dimension=0, tiled=True
     )[None]
-    part_down, returned = lax.optimization_barrier(
-        (outer_sum(activation, grads_in).astype(jnp.bfloat16), returned)
+    part_down, back_rows = lax.optimization_barrier(
+        (outer_sum(activation, grads_in).astype(jnp.bfloat16), back_rows)
     )
+    returned_grad = exchange(back_rows.reshape(experts, capacity, features)).reshape(-1, features)
     grad_down = chain_reduce_scatter(part_down)[None]
     picked = jnp.einsum("tkp,pd->tkd", pick3, returned, preferred_element_type=jnp.float32)
     combined = jnp.einsum("tk,tkd->td", gate_probs, picked).astype(jnp.bfloat16)

time: 277 us -> 285 us (1.029)
  waiting for transfers between devices: 152 us -> 160 us
    ppermute x3, waiting for transfers between devices: 26.7 us -> 48.2 us  [chain_reduce_scatter(): lax.ppermute(acc.astype(jnp.bfloat16), 'replica', perm).astype(jnp.float32)]
    all_to_all x4, waiting for transfers between devices: 125 us -> 112 us  [exchange(): lax.all_to_all(blocks, 'expert', split_axis=0, concat_axis=0, tiled=True)]
  transfers between devices with their start and end apart: 9 -> 9, of which waited for: 6 -> 5; matrix products, arithmetic and copies ran while one was open for 20% -> 20% of each run, Pallas kernels for 0% -> 0%
where the time goes in v10:
time: 285 us; the launch traced here: 284 us
  waiting for transfers between devices  160 us (56%)
  matrix products  53.7 us (19%)
  starting transfers between devices  34.6 us (12%)
  between operations  14.3 us (5%)
  local copies, waits for them, and re-layouts  14 us (5%)
  other arithmetic  7.33 us (3%)
    all_to_all x4, waiting for transfers between devices, exchange(): lax.all_to_all(blocks, 'expert', split_axis=0, concat_axis=0, tiled=True)  112 us
    ppermute x3, waiting for transfers between devices, chain_reduce_scatter(): lax.ppermute(acc.astype(jnp.bfloat16), 'replica', perm).astype(jnp.float32)  48.2 us
    all_to_all x4, starting transfers between devices, exchange(): lax.all_to_all(blocks, 'expert', split_axis=0, concat_axis=0, tiled=True)  31.3 us
    dot_general x3, matrix products, outer_sum(): lax.dot_general(left, right, (((0,), (0,)), ((), ())), preferred_element_...  15.9 us
    mul x3, local copies, waits for them, and re-layouts, per_device(): gate_probs[:, :, None] * out_cot[:, None, :].astype(jnp.float32)  7.36 us
  transfers between devices with their start and end apart: 9, of which 5 were waited for; matrix products, arithmetic and copies ran while one was open for 20% of the time, Pallas kernels for 0%

profile of v10, /device:TPU:1, one launch (start us, length us, event | category | flops | bytes accessed | tf_op | source)
XLA Modules:
  0.0 284.0 jit_solution(7835619089250816717)
XLA Ops:
  7.2 0.0 copy-start
  7.2 0.9 copy.29
  8.1 0.1 eq.72
  8.2 0.1 eq.76
  8.4 0.9 reduce-window.6
  9.3 0.2 slice_reduce_fusion
  9.6 0.1 fusion.43
  9.7 0.1 reduce_sum.24
  9.8 0.1 copy.32
  9.9 0.7 multiply_add_fusion
  10.6 0.1 fusion.38
  10.8 3.1 %fusion.19 = bf16[64,8,2048]{2,1,0:T(8,128)(2,1)} fusion(bf16[64,512]{1,0:T(8,128)(2,1)S(1)} %fusion.38, bf16[64,2048]{1,0:T(8,128)(2,1)} %param.7), kind=kOutput, calls=%fused_computation.22 | convolution fusion | flops 135266304 | bytes 2424832 | tf_op jit(solution)/shard_map/dot_general | solution.py:84
  13.9 13.3 %all-to-all-start = ((bf16[64,8,2048]{2,1,0:T(8,128)(2,1)}), bf16[64,8,2048]{2,1,0:T(8,128)(2,1)}, u32[]{:S(2)}, u32[]{:S(2)}) async-start(bf16[64,8,2048]{2,1,0:T(8,128)(2,1)} %fusion.19), calls=%async_computation | async-start | bytes 4194304 | tf_op jit(solution)/shard_map/all_to_all | solution.py:44
  27.2 0.0 copy-done.1
  27.2 2.5 mul.70
  29.7 4.8 %mul.71 = f32[384,2048]{1,0:T(8,128)} reshape(f32[64,6,2048]{2,1,0:T(8,128)} %mul.70) | data formatting | bytes 6291456 | tf_op jit(solution)/shard_map/mul | solution.py:86
  34.4 0.0 copy-done.2
  34.4 0.1 copy.33
  34.5 0.1 mul.68
  34.7 4.6 %fusion.20 = bf16[64,8,2048]{2,1,0:T(8,128)(2,1)} fusion(f32[384,2048]{1,0:T(8,128)} %mul.71, f32[384]{0:T(512)S(1)} %mul.68, s32[384]{0:T(512)S(1)} %multiply_add_fusion.1), kind=kOutput, calls=%fused_computation.23 | convolution fusion | flops 808124416 | bytes 5245952 | tf_op jit(solution)/shard_map/dot_general | solution.py:87
  39.3 39.1 %all-to-all-done = bf16[64,8,2048]{2,1,0:T(8,128)(2,1)} async-done(((bf16[64,8,2048]{2,1,0:T(8,128)(2,1)}), bf16[64,8,2048]{2,1,0:T(8,128)(2,1)}, u32[]{:S(2)}, u32[]{:S(2)}) %all-to-all-start) | async-done | bytes 2097184 | tf_op jit(solution)/shard_map/all_to_all | solution.py:44
  78.4 6.0 %all-to-all-start.2 = ((bf16[64,8,2048]{2,1,0:T(8,128)(2,1)}), bf16[64,8,2048]{2,1,0:T(8,128)(2,1)}, u32[]{:S(2)}, u32[]{:S(2)}) async-start(bf16[64,8,2048]{2,1,0:T(8,128)(2,1)} %fusion.20), calls=%async_computation.2 | async-start | bytes 4194304 | tf_op jit(solution)/shard_map/all_to_all | solution.py:44
  84.4 0.2 reduce-scatter.3.cloned.1.call-start
  84.6 0.0 copy-start.3
  84.6 4.5 %fusion.12 = f32[512,768]{1,0:T(8,128)S(1)} fusion(bf16[1,2048,768]{2,1,0:T(8,128)(2,1)} %param.11, bf16[64,8,2048]{2,1,0:T(8,128)(2,1)} %all-to-all-done), kind=kOutput, calls=%fused_computation.16 | convolution fusion | flops 1610612736 | bytes 6815744 | tf_op jit(solution)/shard_map/dot_general | solution.py:16
  89.1 0.0 copy-done.3
  89.1 0.0 copy-start.10
  89.1 5.2 %multiply_convert_fusion.4 = (bf16[512,768]{1,0:T(8,128)(2,1)S(1)}, f32[512,768]{1,0:T(8,128)}) fusion(f32[512,768]{1,0:T(8,128)S(1)} %fusion.12, bf16[1,2048,768]{2,1,0:T(8,128)(2,1)S(1)} %copy-done.3, bf16[64,8,2048]{2,1,0:T(8,128)(2,1)} %all-to-all-done), kind=kOutput, calls=%fused_computation.43 | convolution fusion | flops 1612972032 | bytes 9175040 | tf_op jit(solution)/shard_map/dot_general | solution.py:17
  94.3 0.0 copy-done.10
  94.3 3.1 %fusion.14 = bf16[512,2048]{1,0:T(8,128)(2,1)} fusion(bf16[512,768]{1,0:T(8,128)(2,1)S(1)} %get-tuple-element.12, bf16[1,768,2048]{2,1,0:T(8,128)(2,1)S(1)} %copy-done), kind=kOutput, calls=%fused_computation.19 | convolution fusion | flops 1611661312 | bytes 6029312 | tf_op jit(solution)/shard_map/dot_general | solution.py:93
  97.4 0.0 copy-done.9
  97.4 38.1 %all-to-all-done.2 = bf16[64,8,2048]{2,1,0:T(8,128)(2,1)} async-done(((bf16[64,8,2048]{2,1,0:T(8,128)(2,1)}), bf16[64,8,2048]{2,1,0:T(8,128)(2,1)}, u32[]{:S(2)}, u32[]{:S(2)}) %all-to-all-start.2) | async-done | bytes 2097184 | tf_op jit(solution)/shard_map/all_to_all | solution.py:44
  135.5 5.6 %multiply_convert_fusion.3 = (bf16[512,768]{1,0:T(8,128)(2,1)S(1)}, bf16[512,768]{1,0:T(8,128)(2,1)}) fusion(f32[512,768]{1,0:T(8,128)} %copy-done.10, f32[512,768]{1,0:T(8,128)} %get-tuple-element.13, bf16[1,768,2048]{2,1,0:T(8,128)(2,1)S(1)} %copy-done, bf16[64,8,2048]{2,1,0:T(8,128)(2,1)} %all-to-all-done.2), kind=kOutput, calls=%fused_computation.40 | convolution fusion | flops 1615724544 | bytes 9961472 | tf_op jit(solution)/shard_map/dot_general | solution.py:24
  141.1 0.9 copy-done.6
  142.0 5.1 %convolution_convert_fusion.1 = bf16[2048,768]{1,0:T(8,128)(2,1)} fusion(bf16[512,768]{1,0:T(8,128)(2,1)S(1)} %get-tuple-element.19, bf16[64,8,2048]{2,1,0:T(8,128)(2,1)} %all-to-all-done), kind=kOutput, calls=%fused_computation.4 | convolution fusion | flops 1612185600 | bytes 6029312 | tf_op jit(solution)/shard_map/dot_general | solution.py:38
  147.1 0.0 reduce-scatter.3.cloned.1.call-update
  147.1 6.0 %all-to-all-start.1 = ((bf16[64,8,2048]{2,1,0:T(8,128)(2,1)}), bf16[64,8,2048]{2,1,0:T(8,128)(2,1)}, u32[]{:S(2)}, u32[]{:S(2)}) async-start(bf16[64,8,2048]{2,1,0:T(8,128)(2,1)} %bitcast.111), calls=%async_computation.1 | async-start | bytes 4194304 | tf_op jit(solution)/shard_map/all_to_all | solution.py:44
  153.1 0.3 reduce-scatter.5.cloned.1.call-start
  153.4 5.3 %convolution_convert_fusion = bf16[2048,768]{1,0:T(8,128)(2,1)} fusion(bf16[512,768]{1,0:T(8,128)(2,1)} %get-tuple-element.20, bf16[64,8,2048]{2,1,0:T(8,128)(2,1)} %all-to-all-done), kind=kOutput, calls=%fused_computation.3 | convolution fusion | flops 1612185600 | bytes 6029312 | tf_op jit(solution)/shard_map/dot_general | solution.py:38
  158.7 0.0 reduce-scatter.5.cloned.1.call-update
  158.7 0.0 copy-start.4
  158.7 0.0 copy-start.8
  158.7 5.5 %convolution_convert_fusion.2 = bf16[768,2048]{1,0:T(8,128)(2,1)} fusion(bf16[512,768]{1,0:T(8,128)(2,1)} %copy-done.9, bf16[64,8,2048]{2,1,0:T(8,128)(2,1)} %all-to-all-done.2), kind=kOutput, calls=%fused_computation.5 | convolution fusion | flops 1612185600 | bytes 6029312 | tf_op jit(solution)/shard_map/dot_general | solution.py:38
  164.3 1.8 fusion.6
  166.1 0.1 copy-done.5
  166.2 0.2 copy-done.7
  166.4 3.3 %add_convert_fusion = bf16[512,2048]{1,0:T(8,128)(2,1)} fusion(f32[512,2048]{1,0:T(8,128)S(1)} %fusion.6, bf16[512,768]{1,0:T(8,128)(2,1)S(1)} %copy-done.7, bf16[1,2048,768]{2,1,0:T(8,128)(2,1)S(1)} %copy-done.5), kind=kOutput, calls=%fused_computation.2 | convolution fusion | flops 1612709888 | bytes 10223616 | tf_op jit(solution)/shard_map/dot_general | solution.py:30
  169.7 34.6 %all-to-all-done.1 = bf16[64,8,2048]{2,1,0:T(8,128)(2,1)} async-done(((bf16[64,8,2048]{2,1,0:T(8,128)(2,1)}), bf16[64,8,2048]{2,1,0:T(8,128)(2,1)}, u32[]{:S(2)}, u32[]{:S(2)}) %all-to-all-start.1) | async-done | bytes 2097184 | tf_op jit(solution)/shard_map/all_to_all | solution.py:44
  204.3 6.0 %all-to-all-start.3 = ((bf16[64,8,2048]{2,1,0:T(8,128)(2,1)}), bf16[64,8,2048]{2,1,0:T(8,128)(2,1)}, u32[]{:S(2)}, u32[]{:S(2)}) async-start(bf16[64,8,2048]{2,1,0:T(8,128)(2,1)} %bitcast.110), calls=%async_computation.3 | async-start | bytes 4194304 | tf_op jit(solution)/shard_map/all_to_all | solution.py:44
  210.3 2.7 dynamic-slice_bitcast_fusion.1
  213.1 1.3 collective-permute-start
  214.4 1.4 collective-permute-start.2
  215.8 28.4 %collective-permute-done = bf16[192,2048]{1,0:T(8,128)(2,1)} collective-permute-done((bf16[192,2048]{1,0:T(8,128)(2,1)}, bf16[192,2048]{1,0:T(8,128)(2,1)}, u32[]{:S(2)}, u32[]{:S(2)}) %collective-permute-start) | collective-permute-done | bytes 786464 | tf_op jit(solution)/shard_map/ppermute | solution.py:62
  244.2 2.5 fusion.30
  246.7 0.0 collective-permute-start.1
  246.7 0.1 copy.35
  246.8 0.0 collective-permute-done.2
  246.9 19.8 %collective-permute-done.1 = bf16[192,2048]{1,0:T(8,128)(2,1)} collective-permute-done((bf16[192,2048]{1,0:T(8,128)(2,1)}, bf16[192,2048]{1,0:T(8,128)(2,1)}, u32[]{:S(2)}, u32[]{:S(2)}) %collective-permute-start.1) | collective-permute-done | bytes 786464 | tf_op jit(solution)/shard_map/ppermute | solution.py:64
  266.7 2.9 %fusion.34 = bf16[1,192,2048]{2,1,0:T(8,128)(2,1)} fusion(bf16[192,2048]{1,0:T(8,128)(2,1)} %collective-permute-done.2, bf16[192,2048]{1,0:T(8,128)(2,1)} %collective-permute-done.1, bf16[4,192,2048]{2,1,0:T(8,128)(2,1)} %bitcast.109, s32[]{:T(128)S(6)} %select_n.33), kind=kLoop, calls=%fused_computation.44 | loop fusion | flops 2359296 | bytes 3145732 | tf_op jit(solution)/shard_map/broadcast_in_dim | solution.py:114
  269.6 2.6 fusion.21
  272.2 1.3 fusion
  273.5 0.9 copy.42
  274.4 0.0 all-to-all-done.3
  274.4 2.8 convolution_convert_fusion.5
  (14 shorter events, 0.1 us)
Async XLA Ops:
  7.2 87.1 %copy-start = (bf16[1,768,2048]{2,1,0:T(8,128)(2,1)S(1)}, bf16[1,768,2048]{2,1,0:T(8,128)(2,1)}, u32[]{:S(2)}) copy-start(bf16[1,768,2048]{2,1,0:T(8,128)(2,1)} %param.13) | copy-start | bytes 9437188
  13.9 13.3 %copy-start.1 = (bf16[64,2048]{1,0:T(8,128)(2,1)S(1)}, bf16[64,2048]{1,0:T(8,128)(2,1)}, u32[]{:S(2)}) copy-start(bf16[64,2048]{1,0:T(8,128)(2,1)} %param.10) | copy-start | bytes 786436
  13.9 64.5 %all-to-all-start = ((bf16[64,8,2048]{2,1,0:T(8,128)(2,1)}), bf16[64,8,2048]{2,1,0:T(8,128)(2,1)}, u32[]{:S(2)}, u32[]{:S(2)}) async-start(bf16[64,8,2048]{2,1,0:T(8,128)(2,1)} %fusion.19), calls=%async_computation | async-start | bytes 4194304 | tf_op jit(solution)/shard_map/all_to_all | solution.py:44
  29.7 4.8 %copy-start.2 = (f32[64,6]{0,1:T(8,128)S(1)}, f32[64,6]{0,1:T(8,128)}, u32[]{:S(2)}) copy-start(f32[64,6]{0,1:T(8,128)} %param.9) | copy-start | bytes 4612
  78.4 57.2 %all-to-all-start.2 = ((bf16[64,8,2048]{2,1,0:T(8,128)(2,1)}), bf16[64,8,2048]{2,1,0:T(8,128)(2,1)}, u32[]{:S(2)}, u32[]{:S(2)}) async-start(bf16[64,8,2048]{2,1,0:T(8,128)(2,1)} %fusion.20), calls=%async_computation.2 | async-start | bytes 4194304 | tf_op jit(solution)/shard_map/all_to_all | solution.py:44
  84.4 192.8 %reduce-scatter.3.cloned.1.call-start = ((), (), s32[]{:S(2)}) async-start(), calls=%async_computation.6 | async-start | bytes 3932160 | tf_op jit(solution)/shard_map/reduce_scatter | solution.py:104
  84.6 4.5 %copy-start.3 = (bf16[1,2048,768]{2,1,0:T(8,128)(2,1)S(1)}, bf16[1,2048,768]{2,1,0:T(8,128)(2,1)}, u32[]{:S(2)}) copy-start(bf16[1,2048,768]{2,1,0:T(8,128)(2,1)} %param.12) | copy-start | bytes 9437188
  89.1 5.2 %copy-start.10 = (f32[512,768]{1,0:T(8,128)}, f32[512,768]{1,0:T(8,128)S(1)}, u32[]{:S(2)}) copy-start(f32[512,768]{1,0:T(8,128)S(1)} %fusion.12) | copy-start | bytes 4718596
  94.3 3.1 %copy-start.9 = (bf16[512,768]{1,0:T(8,128)(2,1)}, bf16[512,768]{1,0:T(8,128)(2,1)S(1)}, u32[]{:S(2)}) copy-start(bf16[512,768]{1,0:T(8,128)(2,1)S(1)} %get-tuple-element.12) | copy-start | bytes 2359300
  141.1 0.9 copy-start.6
  147.1 57.2 %all-to-all-start.1 = ((bf16[64,8,2048]{2,1,0:T(8,128)(2,1)}), bf16[64,8,2048]{2,1,0:T(8,128)(2,1)}, u32[]{:S(2)}, u32[]{:S(2)}) async-start(bf16[64,8,2048]{2,1,0:T(8,128)(2,1)} %bitcast.111), calls=%async_computation.1 | async-start | bytes 4194304 | tf_op jit(solution)/shard_map/all_to_all | solution.py:44
  153.1 124.0 %reduce-scatter.5.cloned.1.call-start = ((), (), s32[]{:S(2)}) async-start(), calls=%async_computation.7 | async-start | bytes 3932160 | tf_op jit(solution)/shard_map/reduce_scatter | solution.py:107
  158.7 5.6 %copy-start.4 = (bf16[1,2048,768]{2,1,0:T(8,128)(2,1)S(1)}, bf16[1,2048,768]{2,1,0:T(8,128)(2,1)}, u32[]{:S(2)}) copy-start(bf16[1,2048,768]{2,1,0:T(8,128)(2,1)} %param.12) | copy-start | bytes 9437188
  158.7 5.5 %copy-start.8 = (bf16[512,768]{1,0:T(8,128)(2,1)S(1)}, bf16[512,768]{1,0:T(8,128)(2,1)}, u32[]{:S(2)}) copy-start(bf16[512,768]{1,0:T(8,128)(2,1)} %get-tuple-element.20) | copy-start | bytes 2359300
  164.3 1.9 copy-start.5
  164.3 2.1 copy-start.7
  204.3 70.1 %all-to-all-start.3 = ((bf16[64,8,2048]{2,1,0:T(8,128)(2,1)}), bf16[64,8,2048]{2,1,0:T(8,128)(2,1)}, u32[]{:S(2)}, u32[]{:S(2)}) async-start(bf16[64,8,2048]{2,1,0:T(8,128)(2,1)} %bitcast.110), calls=%async_computation.3 | async-start | bytes 4194304 | tf_op jit(solution)/shard_map/all_to_all | solution.py:44
  213.1 31.1 %collective-permute-start = (bf16[192,2048]{1,0:T(8,128)(2,1)}, bf16[192,2048]{1,0:T(8,128)(2,1)}, u32[]{:S(2)}, u32[]{:S(2)}) collective-permute-start(bf16[192,2048]{1,0:T(8,128)(2,1)} %get-tuple-element.17), channel_id=1, source_target_pairs={{0,1},{1,2},{2,3},{3,0},{4,5},{5,6},{6,7},{7,4},{8,9},{9,10},{10,1... | collective-permute-start | bytes 2359304 | tf_op jit(solution)/shard_map/ppermute | solution.py:62
  214.4 32.5 %collective-permute-start.2 = (bf16[192,2048]{1,0:T(8,128)(2,1)}, bf16[192,2048]{1,0:T(8,128)(2,1)}, u32[]{:S(2)}, u32[]{:S(2)}) collective-permute-start(bf16[192,2048]{1,0:T(8,128)(2,1)} %get-tuple-element.18), channel_id=1, source_target_pairs={{0,3},{1,0},{2,1},{3,2},{4,7},{5,4},{6,5},{7,6},{8,11},{9,8},{10,9... | collective-permute-start | bytes 2359304 | tf_op jit(solution)/shard_map/ppermute | solution.py:64
  246.7 20.0 %collective-permute-start.1 = (bf16[192,2048]{1,0:T(8,128)(2,1)}, bf16[192,2048]{1,0:T(8,128)(2,1)}, u32[]{:S(2)}, u32[]{:S(2)}) collective-permute-start(bf16[192,2048]{1,0:T(8,128)(2,1)} %fusion.30), channel_id=1, source_target_pairs={{0,1},{1,2},{2,3},{3,0},{4,5},{5,6},{6,7},{7,4},{8,9},{9,10},{10,1... | collective-permute-start | bytes 2359304 | tf_op jit(solution)/shard_map/ppermute | solution.py:64
Sparse Core Ops, SparseCore 0:
  147.2 37.5 reduce-scatter.2
  187.9 50.1 reduce-scatter.4

commit v11 on v2

--- a/solution.py
+++ b/solution.py
@@ -86,21 +86,25 @@
     grad_tokens = jnp.dot(owner, returned_grad, preferred_element_type=jnp.float32).astype(
         jnp.bfloat16
     )
-    gate_up_grad = jnp.concatenate([d_gate, d_up], axis=1)
     gate_up_sum = lax.psum_scatter(
-        outer_sum(slot_rows, gate_up_grad).astype(jnp.bfloat16),
+        jnp.einsum(
+            "rd,krh->kdh",
+            slot_rows,
+            jnp.stack([d_gate, d_up]),
+            preferred_element_type=jnp.float32,
+        ).astype(jnp.bfloat16),
         "replica",
-        scatter_dimension=0,
+        scatter_dimension=1,
         tiled=True,
-    ).astype(jnp.float32)
+    )
     down_sum = lax.psum_scatter(
         outer_sum(activation, grads_in).astype(jnp.bfloat16),
         "replica",
         scatter_dimension=0,
         tiled=True,
     )
-    grad_gate = gate_up_sum[:, :hidden].astype(jnp.bfloat16)[None]
-    grad_up = gate_up_sum[:, hidden:].astype(jnp.bfloat16)[None]
+    grad_gate = gate_up_sum[0][None]
+    grad_up = gate_up_sum[1][None]
     grad_down = down_sum[None]
     return (combined, grad_tokens, grad_gate, grad_up, grad_down)
 

time: 276 us -> 280 us (1.014)
  local copies, waits for them, and re-layouts: 13.8 us -> 18.4 us
    dot_general x2 -> x1, matrix products: 12.5 us -> 5.37 us  [outer_sum(): lax.dot_general(left, right, (((0,), (0,)), ((), ())), preferred_element_...]
    dot_general x0 -> x1, matrix products: none -> 6.99 us  [per_device(): jnp.einsum('rd,krh->kdh', slot_rows, jnp.stack([d_gate, d_up]), preferred...]
    unnamed x23 -> x25, local copies, waits for them, and re-layouts: 2.31 us -> 6.88 us
  transfers between devices with their start and end apart: 6 -> 6, of which waited for: 4 -> 4; matrix products, arithmetic and copies ran while one was open for 17% -> 19% of each run, Pallas kernels for 0% -> 0%
where the time goes in v11:
time: 280 us; the launch traced here: 279 us
  waiting for transfers between devices  162 us (58%)
  matrix products  51.6 us (18%)
  starting transfers between devices  31.8 us (11%)
  local copies, waits for them, and re-layouts  18.4 us (7%)
  between operations  14.3 us (5%)
    all_to_all x4, waiting for transfers between devices, exchange(): lax.all_to_all(blocks, 'expert', split_axis=0, concat_axis=0, tiled=True)  161 us
    all_to_all x4, starting transfers between devices, exchange(): lax.all_to_all(blocks, 'expert', split_axis=0, concat_axis=0, tiled=True)  31.3 us
    mul x3, local copies, waits for them, and re-layouts, per_device(): gate_probs[:, :, None] * out_cot[:, None, :].astype(jnp.float32)  7.35 us
    dot_general x1, matrix products, per_device(): jnp.einsum('rd,krh->kdh', slot_rows, jnp.stack([d_gate, d_up]), preferred...  6.99 us
    unnamed x25, local copies, waits for them, and re-layouts  6.88 us
  transfers between devices with their start and end apart: 6, of which 4 were waited for; matrix products, arithmetic and copies ran while one was open for 19% of the time, Pallas kernels for 0%

profile of v11, /device:TPU:1, one launch (start us, length us, event | category | flops | bytes accessed | tf_op | source)
XLA Modules:
  0.0 279.5 jit_solution(5476347238761128774)
XLA Ops:
  7.2 0.0 copy-start
  7.2 0.9 copy.38
  8.1 0.1 eq.67
  8.2 0.1 eq.71
  8.4 0.9 reduce-window.6
  9.3 0.2 slice_reduce_fusion
  9.6 0.1 fusion.44
  9.7 0.1 reduce_sum.24
  9.8 0.1 copy.41
  9.9 0.7 multiply_add_fusion
  10.6 0.1 fusion.39
  10.8 3.0 %fusion.19 = bf16[64,8,2048]{2,1,0:T(8,128)(2,1)} fusion(bf16[64,512]{1,0:T(8,128)(2,1)S(1)} %fusion.39, bf16[64,2048]{1,0:T(8,128)(2,1)} %param.7), kind=kOutput, calls=%fused_computation.21 | convolution fusion | flops 135266304 | bytes 2424832 | tf_op jit(solution)/shard_map/dot_general | solution.py:63
  13.8 0.0 copy-start.2
  13.8 0.0 copy-start.1
  13.8 13.3 %all-to-all-start = ((bf16[64,8,2048]{2,1,0:T(8,128)(2,1)}), bf16[64,8,2048]{2,1,0:T(8,128)(2,1)}, u32[]{:S(2)}, u32[]{:S(2)}) async-start(bf16[64,8,2048]{2,1,0:T(8,128)(2,1)} %fusion.19), calls=%async_computation | async-start | bytes 4194304 | tf_op jit(solution)/shard_map/all_to_all | solution.py:44
  27.1 0.0 copy-done.2
  27.1 0.1 copy.42
  27.2 0.1 mul.68
  27.3 0.0 copy-done.1
  27.3 2.5 mul.70
  29.8 4.7 %mul.71 = f32[384,2048]{1,0:T(8,128)} reshape(f32[64,6,2048]{2,1,0:T(8,128)} %mul.70) | data formatting | bytes 6291456 | tf_op jit(solution)/shard_map/mul | solution.py:65
  34.5 4.6 %fusion.20 = bf16[64,8,2048]{2,1,0:T(8,128)(2,1)} fusion(f32[384,2048]{1,0:T(8,128)} %mul.71, f32[384]{0:T(512)S(1)} %mul.68, s32[384]{0:T(512)S(1)} %multiply_add_fusion.1), kind=kOutput, calls=%fused_computation.22 | convolution fusion | flops 808124416 | bytes 5245952 | tf_op jit(solution)/shard_map/dot_general | solution.py:66
  39.2 39.1 %all-to-all-done = bf16[64,8,2048]{2,1,0:T(8,128)(2,1)} async-done(((bf16[64,8,2048]{2,1,0:T(8,128)(2,1)}), bf16[64,8,2048]{2,1,0:T(8,128)(2,1)}, u32[]{:S(2)}, u32[]{:S(2)}) %all-to-all-start) | async-done | bytes 2097184 | tf_op jit(solution)/shard_map/all_to_all | solution.py:44
  78.2 6.0 %all-to-all-start.2 = ((bf16[64,8,2048]{2,1,0:T(8,128)(2,1)}), bf16[64,8,2048]{2,1,0:T(8,128)(2,1)}, u32[]{:S(2)}, u32[]{:S(2)}) async-start(bf16[64,8,2048]{2,1,0:T(8,128)(2,1)} %fusion.20), calls=%async_computation.2 | async-start | bytes 4194304 | tf_op jit(solution)/shard_map/all_to_all | solution.py:44
  84.3 0.2 reduce-scatter.3.cloned.1.call-start
  84.5 0.0 copy-start.3
  84.5 4.5 %fusion.12 = f32[512,768]{1,0:T(8,128)S(1)} fusion(bf16[1,2048,768]{2,1,0:T(8,128)(2,1)} %param.11, bf16[64,8,2048]{2,1,0:T(8,128)(2,1)} %all-to-all-done), kind=kOutput, calls=%fused_computation.15 | convolution fusion | flops 1610612736 | bytes 6815744 | tf_op jit(solution)/shard_map/dot_general | solution.py:16
  89.0 0.0 copy-done.3
  89.0 0.0 copy-start.9
  89.0 5.2 %multiply_convert_fusion.4 = (bf16[512,768]{1,0:T(8,128)(2,1)S(1)}, f32[512,768]{1,0:T(8,128)}) fusion(f32[512,768]{1,0:T(8,128)S(1)} %fusion.12, bf16[1,2048,768]{2,1,0:T(8,128)(2,1)S(1)} %copy-done.3, bf16[64,8,2048]{2,1,0:T(8,128)(2,1)} %all-to-all-done), kind=kOutput, calls=%fused_computation.40 | convolution fusion | flops 1612972032 | bytes 9175040 | tf_op jit(solution)/shard_map/dot_general | solution.py:17
  94.1 0.0 copy-done.9
  94.1 0.0 copy-start.8
  94.1 0.0 copy-done
  94.2 3.3 %fusion.14 = bf16[512,2048]{1,0:T(8,128)(2,1)} fusion(bf16[512,768]{1,0:T(8,128)(2,1)S(1)} %get-tuple-element.12, bf16[1,768,2048]{2,1,0:T(8,128)(2,1)S(1)} %copy-done), kind=kOutput, calls=%fused_computation.18 | convolution fusion | flops 1611661312 | bytes 6029312 | tf_op jit(solution)/shard_map/dot_general | solution.py:72
  97.4 0.0 copy-done.8
  97.4 38.0 %all-to-all-done.2 = bf16[64,8,2048]{2,1,0:T(8,128)(2,1)} async-done(((bf16[64,8,2048]{2,1,0:T(8,128)(2,1)}), bf16[64,8,2048]{2,1,0:T(8,128)(2,1)}, u32[]{:S(2)}, u32[]{:S(2)}) %all-to-all-start.2) | async-done | bytes 2097184 | tf_op jit(solution)/shard_map/all_to_all | solution.py:44
  135.4 4.7 %multiply_convert_fusion.3 = (bf16[512,768]{1,0:T(8,128)(2,1)S(1)}, bf16[512,768]{1,0:T(8,128)(2,1)S(1)}) fusion(f32[512,768]{1,0:T(8,128)} %copy-done.9, f32[512,768]{1,0:T(8,128)} %get-tuple-element.10, bf16[1,768,2048]{2,1,0:T(8,128)(2,1)S(1)} %copy-done, bf16[64,8,2048]{2,1,0:T(8,128)(2,1)} %all-to-all-done.2), kind=kOutput, calls=%fused_computation.37 | convolution fusion | flops 1615724544 | bytes 9961472 | tf_op jit(solution)/shard_map/dot_general | solution.py:24
  140.2 0.0 copy-start.5
  140.2 0.0 copy-start.7
  140.2 0.9 copy-done.5
  141.0 0.3 copy-done.7
  141.3 7.0 %convert_bitcast_fusion = bf16[2,2048,768]{1,2,0:T(8,128)(2,1)} fusion(bf16[64,8,2048]{2,1,0:T(8,128)(2,1)} %all-to-all-done, bf16[1,512,768]{2,1,0:T(8,128)(2,1)S(1)} %bitcast.104, bf16[1,512,768]{2,1,0:T(8,128)(2,1)S(1)} %bitcast.103), kind=kOutput, calls=%fused_computation | convolution fusion | flops 3225157632 | bytes 9961472 | tf_op jit(solution)/shard_map/rd,krh->kdh/dot_general | solution.py:90
  148.3 0.0 reduce-scatter.3.cloned.1.call-update
  148.3 6.0 %all-to-all-start.1 = ((bf16[64,8,2048]{2,1,0:T(8,128)(2,1)}), bf16[64,8,2048]{2,1,0:T(8,128)(2,1)}, u32[]{:S(2)}, u32[]{:S(2)}) async-start(bf16[64,8,2048]{2,1,0:T(8,128)(2,1)} %bitcast.98), calls=%async_computation.1 | async-start | bytes 4194304 | tf_op jit(solution)/shard_map/all_to_all | solution.py:44
  154.3 0.3 reduce-scatter.5.cloned.1.call-start
  154.6 5.4 %convolution_convert_fusion = bf16[768,2048]{1,0:T(8,128)(2,1)} fusion(bf16[512,768]{1,0:T(8,128)(2,1)} %copy-done.8, bf16[64,8,2048]{2,1,0:T(8,128)(2,1)} %all-to-all-done.2), kind=kOutput, calls=%fused_computation.4 | convolution fusion | flops 1612185600 | bytes 6029312 | tf_op jit(solution)/shard_map/dot_general | solution.py:38
  160.0 0.0 reduce-scatter.5.cloned.1.call-update
  160.0 0.0 copy-start.4
  160.0 0.0 copy-start.6
  160.0 4.1 %fusion.6 = f32[512,2048]{1,0:T(8,128)S(1)} fusion(bf16[512,768]{1,0:T(8,128)(2,1)} %copy-done.7, bf16[1,2048,768]{2,1,0:T(8,128)(2,1)} %param.12), kind=kOutput, calls=%fused_computation.9 | convolution fusion | flops 1610612736 | bytes 8126464 | tf_op jit(solution)/shard_map/dot_general | solution.py:31
  164.1 0.0 copy-done.4
  164.1 0.0 copy-done.6
  164.1 3.1 %fusion.21 = bf16[64,8,2048]{2,1,0:T(8,128)(2,1)} fusion(f32[512,2048]{1,0:T(8,128)S(1)} %fusion.6, bf16[512,768]{1,0:T(8,128)(2,1)S(1)} %copy-done.6, bf16[1,2048,768]{2,1,0:T(8,128)(2,1)S(1)} %copy-done.4), kind=kOutput, calls=%fused_computation.23 | convolution fusion | flops 1612709888 | bytes 10223616 | tf_op jit(solution)/shard_map/dot_general | solution.py:30
  167.3 38.2 %all-to-all-done.1 = bf16[64,8,2048]{2,1,0:T(8,128)(2,1)} async-done(((bf16[64,8,2048]{2,1,0:T(8,128)(2,1)}), bf16[64,8,2048]{2,1,0:T(8,128)(2,1)}, u32[]{:S(2)}, u32[]{:S(2)}) %all-to-all-start.1) | async-done | bytes 2097184 | tf_op jit(solution)/shard_map/all_to_all | solution.py:44
  205.5 6.0 %all-to-all-start.3 = ((bf16[64,8,2048]{2,1,0:T(8,128)(2,1)}), bf16[64,8,2048]{2,1,0:T(8,128)(2,1)}, u32[]{:S(2)}, u32[]{:S(2)}) async-start(bf16[64,8,2048]{2,1,0:T(8,128)(2,1)} %fusion.21), calls=%async_computation.3 | async-start | bytes 4194304 | tf_op jit(solution)/shard_map/all_to_all | solution.py:44
  211.5 0.1 copy.47
  211.6 2.6 fusion.25
  214.2 1.3 fusion
  215.6 0.9 copy.55
  216.4 46.2 %all-to-all-done.3 = bf16[64,8,2048]{2,1,0:T(8,128)(2,1)} async-done(((bf16[64,8,2048]{2,1,0:T(8,128)(2,1)}), bf16[64,8,2048]{2,1,0:T(8,128)(2,1)}, u32[]{:S(2)}, u32[]{:S(2)}) %all-to-all-start.3) | async-done | bytes 2097184 | tf_op jit(solution)/shard_map/all_to_all | solution.py:44
  262.7 2.8 convolution_convert_fusion.3
  265.4 2.6 fusion.47
  268.1 2.3 copy.45
  270.4 2.3 copy.44
  (5 shorter events, 0.1 us)
Async XLA Ops:
  7.2 87.0 %copy-start = (bf16[1,768,2048]{2,1,0:T(8,128)(2,1)S(1)}, bf16[1,768,2048]{2,1,0:T(8,128)(2,1)}, u32[]{:S(2)}) copy-start(bf16[1,768,2048]{2,1,0:T(8,128)(2,1)} %param.13) | copy-start | bytes 9437188
  13.8 13.3 %copy-start.2 = (f32[64,6]{0,1:T(8,128)S(1)}, f32[64,6]{0,1:T(8,128)}, u32[]{:S(2)}) copy-start(f32[64,6]{0,1:T(8,128)} %param.9) | copy-start | bytes 4612
  13.8 13.6 %copy-start.1 = (bf16[64,2048]{1,0:T(8,128)(2,1)S(1)}, bf16[64,2048]{1,0:T(8,128)(2,1)}, u32[]{:S(2)}) copy-start(bf16[64,2048]{1,0:T(8,128)(2,1)} %param.10) | copy-start | bytes 786436
  13.8 64.5 %all-to-all-start = ((bf16[64,8,2048]{2,1,0:T(8,128)(2,1)}), bf16[64,8,2048]{2,1,0:T(8,128)(2,1)}, u32[]{:S(2)}, u32[]{:S(2)}) async-start(bf16[64,8,2048]{2,1,0:T(8,128)(2,1)} %fusion.19), calls=%async_computation | async-start | bytes 4194304 | tf_op jit(solution)/shard_map/all_to_all | solution.py:44
  78.2 57.2 %all-to-all-start.2 = ((bf16[64,8,2048]{2,1,0:T(8,128)(2,1)}), bf16[64,8,2048]{2,1,0:T(8,128)(2,1)}, u32[]{:S(2)}, u32[]{:S(2)}) async-start(bf16[64,8,2048]{2,1,0:T(8,128)(2,1)} %fusion.20), calls=%async_computation.2 | async-start | bytes 4194304 | tf_op jit(solution)/shard_map/all_to_all | solution.py:44
  84.3 181.2 %reduce-scatter.3.cloned.1.call-start = ((), (), s32[]{:S(2)}) async-start(), calls=%async_computation.6 | async-start | bytes 7864320 | tf_op jit(solution)/shard_map/reduce_scatter | solution.py:89
  84.5 4.5 %copy-start.3 = (bf16[1,2048,768]{2,1,0:T(8,128)(2,1)S(1)}, bf16[1,2048,768]{2,1,0:T(8,128)(2,1)}, u32[]{:S(2)}) copy-start(bf16[1,2048,768]{2,1,0:T(8,128)(2,1)} %param.12) | copy-start | bytes 9437188
  89.0 5.2 %copy-start.9 = (f32[512,768]{1,0:T(8,128)}, f32[512,768]{1,0:T(8,128)S(1)}, u32[]{:S(2)}) copy-start(f32[512,768]{1,0:T(8,128)S(1)} %fusion.12) | copy-start | bytes 4718596
  94.1 3.3 %copy-start.8 = (bf16[512,768]{1,0:T(8,128)(2,1)}, bf16[512,768]{1,0:T(8,128)(2,1)S(1)}, u32[]{:S(2)}) copy-start(bf16[512,768]{1,0:T(8,128)(2,1)S(1)} %get-tuple-element.12) | copy-start | bytes 2359300
  140.2 0.9 copy-start.5
  140.2 1.1 copy-start.7
  148.3 57.2 %all-to-all-start.1 = ((bf16[64,8,2048]{2,1,0:T(8,128)(2,1)}), bf16[64,8,2048]{2,1,0:T(8,128)(2,1)}, u32[]{:S(2)}, u32[]{:S(2)}) async-start(bf16[64,8,2048]{2,1,0:T(8,128)(2,1)} %bitcast.98), calls=%async_computation.1 | async-start | bytes 4194304 | tf_op jit(solution)/shard_map/all_to_all | solution.py:44
  154.3 118.3 %reduce-scatter.5.cloned.1.call-start = ((), (), s32[]{:S(2)}) async-start(), calls=%async_computation.7 | async-start | bytes 3932160 | tf_op jit(solution)/shard_map/reduce_scatter | solution.py:100
  160.0 4.1 %copy-start.4 = (bf16[1,2048,768]{2,1,0:T(8,128)(2,1)S(1)}, bf16[1,2048,768]{2,1,0:T(8,128)(2,1)}, u32[]{:S(2)}) copy-start(bf16[1,2048,768]{2,1,0:T(8,128)(2,1)} %param.11) | copy-start | bytes 9437188
  160.0 4.1 %copy-start.6 = (bf16[512,768]{1,0:T(8,128)(2,1)S(1)}, bf16[512,768]{1,0:T(8,128)(2,1)}, u32[]{:S(2)}) copy-start(bf16[512,768]{1,0:T(8,128)(2,1)} %copy-done.5) | copy-start | bytes 2359300
  205.5 57.2 %all-to-all-start.3 = ((bf16[64,8,2048]{2,1,0:T(8,128)(2,1)}), bf16[64,8,2048]{2,1,0:T(8,128)(2,1)}, u32[]{:S(2)}, u32[]{:S(2)}) async-start(bf16[64,8,2048]{2,1,0:T(8,128)(2,1)} %fusion.21), calls=%async_computation.3 | async-start | bytes 4194304 | tf_op jit(solution)/shard_map/all_to_all | solution.py:44
Sparse Core Ops, SparseCore 0:
  148.4 63.1 reduce-scatter.2
  214.8 40.5 reduce-scatter.4

commit v12 on v2

--- a/solution.py
+++ b/solution.py
@@ -60,7 +60,10 @@
     )
     pick3 = pick.reshape(tok_rows, top_count, total_rows)
     owner = jnp.sum(pick3, axis=1)
-    outgoing = jnp.dot(owner.T, tokens, preferred_element_type=jnp.float32).astype(jnp.bfloat16)
+    taken = (owner > 0).astype(jnp.int32)
+    source = jnp.sum(taken * jnp.arange(tok_rows, dtype=jnp.int32)[:, None], axis=0)
+    source = source + tok_rows * (1 - jnp.sum(taken, axis=0))
+    outgoing = jnp.take(tokens, source, axis=0, mode="fill", fill_value=0)
     slot_rows = exchange(outgoing.reshape(experts, capacity, features)).reshape(-1, features)
     scaled = (gate_probs[:, :, None] * out_cot[:, None, :].astype(jnp.float32)).astype(jnp.bfloat16)
     grad_out = jnp.dot(

time: 276 us -> 282 us (1.022)
  other arithmetic: 1.93 us -> 6.96 us
  local copies, waits for them, and re-layouts: 13.8 us -> 17.2 us
  matrix products: 51.8 us -> 48.7 us
    gather x0 -> x1, local copies, waits for them, and re-layouts: none -> 3.33 us  [per_device(): outgoing = jnp.take(tokens, source, axis=0, mode='fill', fill_value=0)]
    select_n x0 -> x2, other arithmetic: none -> 3.13 us  [per_device(): outgoing = jnp.take(tokens, source, axis=0, mode='fill', fill_value=0)]
    dot_general x1 -> x0, matrix products: 3 us -> none  [per_device(): jnp.dot(owner.T, tokens, preferred_element_type=jnp.float32)]
where the time goes in v12:
time: 282 us; the launch traced here: 281 us
  waiting for transfers between devices  162 us (57%)
  matrix products  48.7 us (17%)
  starting transfers between devices  31.8 us (11%)
  local copies, waits for them, and re-layouts  17.2 us (6%)
  between operations  14.3 us (5%)
  other arithmetic  6.96 us (2%)
    all_to_all x4, waiting for transfers between devices, exchange(): lax.all_to_all(blocks, 'expert', split_axis=0, concat_axis=0, tiled=True)  161 us
    all_to_all x4, starting transfers between devices, exchange(): lax.all_to_all(blocks, 'expert', split_axis=0, concat_axis=0, tiled=True)  31.3 us
    dot_general x2, matrix products, outer_sum(): lax.dot_general(left, right, (((0,), (0,)), ((), ())), preferred_element_...  12.5 us
    mul x3, local copies, waits for them, and re-layouts, per_device(): gate_probs[:, :, None] * out_cot[:, None, :].astype(jnp.float32)  7.34 us
  transfers between devices with their start and end apart: 6, of which 4 were waited for; matrix products, arithmetic and copies ran while one was open for 17% of the time, Pallas kernels for 0%

profile of v12, /device:TPU:1, one launch (start us, length us, event | category | flops | bytes accessed | tf_op | source)
XLA Modules:
  0.0 280.5 jit_solution(10800106653089101428)
XLA Ops:
  7.2 0.0 copy-start
  7.2 0.0 copy-start.1
  7.2 0.9 copy.29
  8.1 0.1 eq.67
  8.3 0.1 eq.71
  8.4 0.7 fusion.44
  9.1 2.1 reduce-window.6
  11.2 0.2 slice_reduce_fusion
  11.4 0.1 fusion.43
  11.5 0.1 reduce_sum.42
  11.7 0.1 copy.32
  11.8 0.7 multiply_add_fusion
  12.5 0.1 fusion.38
  12.7 0.1 add.66
  12.8 0.0 copy-done.1
  12.8 3.3 %gather_fusion = bf16[512,2048]{1,0:T(8,128)(2,1)} fusion(bf16[64,2048]{1,0:T(8,128)(2,1)S(1)} %copy-done.1, s32[1024]{0:T(1024)S(1)} %pad_clamp_fusion), kind=kCustom, calls=%fused_computation | custom fusion | bytes 4196352 | tf_op jit(solution)/shard_map/jit(_take)/gather | solution.py:66
  16.2 3.1 %bitcast_select_fusion = bf16[64,8,2048]{2,1,0:T(8,128)(2,1)} fusion(bf16[512,2048]{1,0:T(8,128)(2,1)} %gather_fusion, pred[64,8]{1,0:T(8,128)(4,1)S(1)} %compare_and_fusion), kind=kLoop, calls=%fused_computation.32 | loop fusion | flops 1048576 | bytes 4194816 | tf_op jit(solution)/shard_map/jit(_take)/select_n | solution.py:66
  19.3 13.3 %all-to-all-start = ((bf16[64,8,2048]{2,1,0:T(8,128)(2,1)}), bf16[64,8,2048]{2,1,0:T(8,128)(2,1)}, u32[]{:S(2)}, u32[]{:S(2)}) async-start(bf16[64,8,2048]{2,1,0:T(8,128)(2,1)} %bitcast_select_fusion), calls=%async_computation | async-start | bytes 4194304 | tf_op jit(solution)/shard_map/all_to_all | solution.py:44
  32.6 0.0 copy-done.3
  32.6 0.1 copy.33
  32.7 0.1 mul.104
  32.8 0.0 copy-done.2
  32.8 2.4 mul.106
  35.3 4.8 %mul.107 = f32[384,2048]{1,0:T(8,128)} reshape(f32[64,6,2048]{2,1,0:T(8,128)} %mul.106) | data formatting | bytes 6291456 | tf_op jit(solution)/shard_map/mul | solution.py:68
  40.1 4.6 %fusion.19 = bf16[64,8,2048]{2,1,0:T(8,128)(2,1)} fusion(f32[384,2048]{1,0:T(8,128)} %mul.107, f32[384]{0:T(512)S(1)} %mul.104, s32[384]{0:T(512)S(1)} %multiply_add_fusion.1), kind=kOutput, calls=%fused_computation.21 | convolution fusion | flops 808124416 | bytes 5245952 | tf_op jit(solution)/shard_map/dot_general | solution.py:69
  44.7 39.1 %all-to-all-done = bf16[64,8,2048]{2,1,0:T(8,128)(2,1)} async-done(((bf16[64,8,2048]{2,1,0:T(8,128)(2,1)}), bf16[64,8,2048]{2,1,0:T(8,128)(2,1)}, u32[]{:S(2)}, u32[]{:S(2)}) %all-to-all-start) | async-done | bytes 2097184 | tf_op jit(solution)/shard_map/all_to_all | solution.py:44
  83.8 6.0 %all-to-all-start.2 = ((bf16[64,8,2048]{2,1,0:T(8,128)(2,1)}), bf16[64,8,2048]{2,1,0:T(8,128)(2,1)}, u32[]{:S(2)}, u32[]{:S(2)}) async-start(bf16[64,8,2048]{2,1,0:T(8,128)(2,1)} %fusion.19), calls=%async_computation.2 | async-start | bytes 4194304 | tf_op jit(solution)/shard_map/all_to_all | solution.py:44
  89.8 0.2 reduce-scatter.3.cloned.1.call-start
  90.0 0.0 copy-start.4
  90.0 4.5 %fusion.12 = f32[512,768]{1,0:T(8,128)S(1)} fusion(bf16[1,2048,768]{2,1,0:T(8,128)(2,1)} %param.11, bf16[64,8,2048]{2,1,0:T(8,128)(2,1)} %all-to-all-done), kind=kOutput, calls=%fused_computation.16 | convolution fusion | flops 1610612736 | bytes 6815744 | tf_op jit(solution)/shard_map/dot_general | solution.py:16
  94.5 0.0 copy-done.4
  94.5 0.0 copy-start.10
  94.5 5.2 %multiply_convert_fusion.4 = (bf16[512,768]{1,0:T(8,128)(2,1)S(1)}, f32[512,768]{1,0:T(8,128)}) fusion(f32[512,768]{1,0:T(8,128)S(1)} %fusion.12, bf16[1,2048,768]{2,1,0:T(8,128)(2,1)S(1)} %copy-done.4, bf16[64,8,2048]{2,1,0:T(8,128)(2,1)} %all-to-all-done), kind=kOutput, calls=%fused_computation.40 | convolution fusion | flops 1612972032 | bytes 9175040 | tf_op jit(solution)/shard_map/dot_general | solution.py:17
  99.7 0.0 copy-done.10
  99.7 0.0 copy-done
  99.7 3.3 %fusion.14 = bf16[512,2048]{1,0:T(8,128)(2,1)} fusion(bf16[512,768]{1,0:T(8,128)(2,1)S(1)} %get-tuple-element.12, bf16[1,768,2048]{2,1,0:T(8,128)(2,1)S(1)} %copy-done), kind=kOutput, calls=%fused_computation.19 | convolution fusion | flops 1611661312 | bytes 6029312 | tf_op jit(solution)/shard_map/dot_general | solution.py:75
  102.9 0.0 copy-done.9
  102.9 38.0 %all-to-all-done.2 = bf16[64,8,2048]{2,1,0:T(8,128)(2,1)} async-done(((bf16[64,8,2048]{2,1,0:T(8,128)(2,1)}), bf16[64,8,2048]{2,1,0:T(8,128)(2,1)}, u32[]{:S(2)}, u32[]{:S(2)}) %all-to-all-start.2) | async-done | bytes 2097184 | tf_op jit(solution)/shard_map/all_to_all | solution.py:44
  140.9 4.7 %multiply_convert_fusion.3 = (bf16[512,768]{1,0:T(8,128)(2,1)S(1)}, bf16[512,768]{1,0:T(8,128)(2,1)S(1)}) fusion(f32[512,768]{1,0:T(8,128)} %copy-done.10, f32[512,768]{1,0:T(8,128)} %get-tuple-element.10, bf16[1,768,2048]{2,1,0:T(8,128)(2,1)S(1)} %copy-done, bf16[64,8,2048]{2,1,0:T(8,128)(2,1)} %all-to-all-done.2), kind=kOutput, calls=%fused_computation.37 | convolution fusion | flops 1615724544 | bytes 9961472 | tf_op jit(solution)/shard_map/dot_general | solution.py:24
  145.7 0.0 copy-start.6
  145.7 0.0 copy-start.8
  145.7 0.9 copy-done.6
  146.5 0.3 copy-done.8
  146.8 7.1 %convolution_convert_fusion = bf16[2048,1536]{1,0:T(8,128)(2,1)} fusion(bf16[64,8,2048]{2,1,0:T(8,128)(2,1)} %all-to-all-done, bf16[512,768]{1,0:T(8,128)(2,1)S(1)} %get-tuple-element.16, bf16[512,768]{1,0:T(8,128)(2,1)S(1)} %get-tuple-element.15), kind=kOutput, calls=%fused_computation.1 | convolution fusion | flops 3227516928 | bytes 9961472 | tf_op jit(solution)/shard_map/dot_general | solution.py:38
  153.9 0.0 reduce-scatter.3.cloned.1.call-update
  153.9 6.0 %all-to-all-start.1 = ((bf16[64,8,2048]{2,1,0:T(8,128)(2,1)}), bf16[64,8,2048]{2,1,0:T(8,128)(2,1)}, u32[]{:S(2)}, u32[]{:S(2)}) async-start(bf16[64,8,2048]{2,1,0:T(8,128)(2,1)} %bitcast.96), calls=%async_computation.1 | async-start | bytes 4194304 | tf_op jit(solution)/shard_map/all_to_all | solution.py:44
  160.0 0.3 reduce-scatter.5.cloned.1.call-start
  160.2 5.4 %convolution_convert_fusion.1 = bf16[768,2048]{1,0:T(8,128)(2,1)} fusion(bf16[512,768]{1,0:T(8,128)(2,1)} %copy-done.9, bf16[64,8,2048]{2,1,0:T(8,128)(2,1)} %all-to-all-done.2), kind=kOutput, calls=%fused_computation.5 | convolution fusion | flops 1612185600 | bytes 6029312 | tf_op jit(solution)/shard_map/dot_general | solution.py:38
  165.6 0.0 reduce-scatter.5.cloned.1.call-update
  165.6 0.0 copy-start.5
  165.6 0.0 copy-start.7
  165.7 4.1 %fusion.6 = f32[512,2048]{1,0:T(8,128)S(1)} fusion(bf16[512,768]{1,0:T(8,128)(2,1)} %copy-done.8, bf16[1,2048,768]{2,1,0:T(8,128)(2,1)} %param.12), kind=kOutput, calls=%fused_computation.10 | convolution fusion | flops 1610612736 | bytes 8126464 | tf_op jit(solution)/shard_map/dot_general | solution.py:31
  169.8 0.0 copy-done.5
  169.8 0.0 copy-done.7
  169.8 3.2 %fusion.20 = bf16[64,8,2048]{2,1,0:T(8,128)(2,1)} fusion(f32[512,2048]{1,0:T(8,128)S(1)} %fusion.6, bf16[512,768]{1,0:T(8,128)(2,1)S(1)} %copy-done.7, bf16[1,2048,768]{2,1,0:T(8,128)(2,1)S(1)} %copy-done.5), kind=kOutput, calls=%fused_computation.22 | convolution fusion | flops 1612709888 | bytes 10223616 | tf_op jit(solution)/shard_map/dot_general | solution.py:30
  172.9 38.2 %all-to-all-done.1 = bf16[64,8,2048]{2,1,0:T(8,128)(2,1)} async-done(((bf16[64,8,2048]{2,1,0:T(8,128)(2,1)}), bf16[64,8,2048]{2,1,0:T(8,128)(2,1)}, u32[]{:S(2)}, u32[]{:S(2)}) %all-to-all-start.1) | async-done | bytes 2097184 | tf_op jit(solution)/shard_map/all_to_all | solution.py:44
  211.1 6.0 %all-to-all-start.3 = ((bf16[64,8,2048]{2,1,0:T(8,128)(2,1)}), bf16[64,8,2048]{2,1,0:T(8,128)(2,1)}, u32[]{:S(2)}, u32[]{:S(2)}) async-start(bf16[64,8,2048]{2,1,0:T(8,128)(2,1)} %fusion.20), calls=%async_computation.3 | async-start | bytes 4194304 | tf_op jit(solution)/shard_map/all_to_all | solution.py:44
  217.1 0.1 copy.35
  217.3 2.6 fusion.23
  219.9 1.3 fusion
  221.2 0.9 copy.42
  222.1 46.2 %all-to-all-done.3 = bf16[64,8,2048]{2,1,0:T(8,128)(2,1)} async-done(((bf16[64,8,2048]{2,1,0:T(8,128)(2,1)}), bf16[64,8,2048]{2,1,0:T(8,128)(2,1)}, u32[]{:S(2)}, u32[]{:S(2)}) %all-to-all-start.3) | async-done | bytes 2097184 | tf_op jit(solution)/shard_map/all_to_all | solution.py:44
  268.3 2.8 convolution_convert_fusion.3
  271.1 2.6 slice_bitcast_fusion
  (12 shorter events, 0.1 us)
Async XLA Ops:
  7.2 92.5 %copy-start = (bf16[1,768,2048]{2,1,0:T(8,128)(2,1)S(1)}, bf16[1,768,2048]{2,1,0:T(8,128)(2,1)}, u32[]{:S(2)}) copy-start(bf16[1,768,2048]{2,1,0:T(8,128)(2,1)} %param.13) | copy-start | bytes 9437188
  7.2 5.6 %copy-start.1 = (bf16[64,2048]{1,0:T(8,128)(2,1)S(1)}, bf16[64,2048]{1,0:T(8,128)(2,1)}, u32[]{:S(2)}) copy-start(bf16[64,2048]{1,0:T(8,128)(2,1)} %param.7) | copy-start | bytes 786436
  19.3 13.3 %copy-start.3 = (f32[64,6]{0,1:T(8,128)S(1)}, f32[64,6]{0,1:T(8,128)}, u32[]{:S(2)}) copy-start(f32[64,6]{0,1:T(8,128)} %param.9) | copy-start | bytes 4612
  19.3 13.6 %copy-start.2 = (bf16[64,2048]{1,0:T(8,128)(2,1)S(1)}, bf16[64,2048]{1,0:T(8,128)(2,1)}, u32[]{:S(2)}) copy-start(bf16[64,2048]{1,0:T(8,128)(2,1)} %param.10) | copy-start | bytes 786436
  19.3 64.5 %all-to-all-start = ((bf16[64,8,2048]{2,1,0:T(8,128)(2,1)}), bf16[64,8,2048]{2,1,0:T(8,128)(2,1)}, u32[]{:S(2)}, u32[]{:S(2)}) async-start(bf16[64,8,2048]{2,1,0:T(8,128)(2,1)} %bitcast_select_fusion), calls=%async_computation | async-start | bytes 4194304 | tf_op jit(solution)/shard_map/all_to_all | solution.py:44
  83.8 57.2 %all-to-all-start.2 = ((bf16[64,8,2048]{2,1,0:T(8,128)(2,1)}), bf16[64,8,2048]{2,1,0:T(8,128)(2,1)}, u32[]{:S(2)}, u32[]{:S(2)}) async-start(bf16[64,8,2048]{2,1,0:T(8,128)(2,1)} %fusion.19), calls=%async_computation.2 | async-start | bytes 4194304 | tf_op jit(solution)/shard_map/all_to_all | solution.py:44
  89.8 181.3 %reduce-scatter.3.cloned.1.call-start = ((), (), s32[]{:S(2)}) async-start(), calls=%async_computation.6 | async-start | bytes 7864320 | tf_op jit(solution)/shard_map/reduce_scatter | solution.py:93
  90.0 4.5 %copy-start.4 = (bf16[1,2048,768]{2,1,0:T(8,128)(2,1)S(1)}, bf16[1,2048,768]{2,1,0:T(8,128)(2,1)}, u32[]{:S(2)}) copy-start(bf16[1,2048,768]{2,1,0:T(8,128)(2,1)} %param.12) | copy-start | bytes 9437188
  94.5 5.2 %copy-start.10 = (f32[512,768]{1,0:T(8,128)}, f32[512,768]{1,0:T(8,128)S(1)}, u32[]{:S(2)}) copy-start(f32[512,768]{1,0:T(8,128)S(1)} %fusion.12) | copy-start | bytes 4718596
  99.7 3.3 %copy-start.9 = (bf16[512,768]{1,0:T(8,128)(2,1)}, bf16[512,768]{1,0:T(8,128)(2,1)S(1)}, u32[]{:S(2)}) copy-start(bf16[512,768]{1,0:T(8,128)(2,1)S(1)} %get-tuple-element.12) | copy-start | bytes 2359300
  145.7 0.9 copy-start.6
  145.7 1.1 copy-start.8
  153.9 57.2 %all-to-all-start.1 = ((bf16[64,8,2048]{2,1,0:T(8,128)(2,1)}), bf16[64,8,2048]{2,1,0:T(8,128)(2,1)}, u32[]{:S(2)}, u32[]{:S(2)}) async-start(bf16[64,8,2048]{2,1,0:T(8,128)(2,1)} %bitcast.96), calls=%async_computation.1 | async-start | bytes 4194304 | tf_op jit(solution)/shard_map/all_to_all | solution.py:44
  160.0 113.7 %reduce-scatter.5.cloned.1.call-start = ((), (), s32[]{:S(2)}) async-start(), calls=%async_computation.7 | async-start | bytes 3932160 | tf_op jit(solution)/shard_map/reduce_scatter | solution.py:99
  165.6 4.1 %copy-start.5 = (bf16[1,2048,768]{2,1,0:T(8,128)(2,1)S(1)}, bf16[1,2048,768]{2,1,0:T(8,128)(2,1)}, u32[]{:S(2)}) copy-start(bf16[1,2048,768]{2,1,0:T(8,128)(2,1)} %param.11) | copy-start | bytes 9437188
  165.6 4.1 %copy-start.7 = (bf16[512,768]{1,0:T(8,128)(2,1)S(1)}, bf16[512,768]{1,0:T(8,128)(2,1)}, u32[]{:S(2)}) copy-start(bf16[512,768]{1,0:T(8,128)(2,1)} %copy-done.6) | copy-start | bytes 2359300
  211.1 57.2 %all-to-all-start.3 = ((bf16[64,8,2048]{2,1,0:T(8,128)(2,1)}), bf16[64,8,2048]{2,1,0:T(8,128)(2,1)}, u32[]{:S(2)}, u32[]{:S(2)}) async-start(bf16[64,8,2048]{2,1,0:T(8,128)(2,1)} %fusion.20), calls=%async_computation.3 | async-start | bytes 4194304 | tf_op jit(solution)/shard_map/all_to_all | solution.py:44
Sparse Core Ops, SparseCore 0:
  154.1 63.1 reduce-scatter.2
  220.4 40.5 reduce-scatter.4

commit v13 on v2

--- a/solution.py
+++ b/solution.py
@@ -7,7 +7,11 @@
 def slots(routes, experts, capacity):
     flat_ids = routes.reshape(-1)
     one_hot = (flat_ids[:, None] == jnp.arange(experts, dtype=jnp.int32)[None, :]).astype(jnp.int32)
-    before = jnp.cumsum(one_hot, axis=0) - one_hot
+    rows = flat_ids.shape[0]
+    lower = jnp.arange(rows)[:, None] > jnp.arange(rows)[None, :]
+    before = jnp.dot(
+        lower.astype(jnp.bfloat16), one_hot.astype(jnp.bfloat16), preferred_element_type=jnp.float32
+    ).astype(jnp.int32)
     slot_rank = jnp.sum(before * one_hot, axis=1)
     return flat_ids * capacity + slot_rank
 

time: 276 us -> 275 us (level)
  transfers between devices with their start and end apart: 6 -> 6, of which waited for: 4 -> 4; matrix products, arithmetic and copies ran while one was open for 17% -> 18% of each run, Pallas kernels for 0% -> 0%
where the time goes in v13:
time: 275 us; the launch traced here: 274 us
  waiting for transfers between devices  161 us (59%)
  matrix products  52 us (19%)
  starting transfers between devices  31.8 us (12%)
  between operations  14.2 us (5%)
  local copies, waits for them, and re-layouts  13.5 us (5%)
    all_to_all x4, waiting for transfers between devices, exchange(): lax.all_to_all(blocks, 'expert', split_axis=0, concat_axis=0, tiled=True)  161 us
    all_to_all x4, starting transfers between devices, exchange(): lax.all_to_all(blocks, 'expert', split_axis=0, concat_axis=0, tiled=True)  31.3 us
    dot_general x2, matrix products, outer_sum(): lax.dot_general(left, right, (((0,), (0,)), ((), ())), preferred_element_...  12.6 us
    mul x3, local copies, waits for them, and re-layouts, per_device(): gate_probs[:, :, None] * out_cot[:, None, :].astype(jnp.float32)  7.37 us
  transfers between devices with their start and end apart: 6, of which 4 were waited for; matrix products, arithmetic and copies ran while one was open for 18% of the time, Pallas kernels for 0%

profile of v13, /device:TPU:1, one launch (start us, length us, event | category | flops | bytes accessed | tf_op | source)
XLA Modules:
  0.0 273.9 jit_solution(16262838052512966228)
XLA Ops:
  7.2 0.0 copy-start
  7.2 0.9 copy.25
  8.1 0.1 eq.57
  8.2 0.2 fusion.37
  8.5 0.1 reduce_sum.24
  8.6 0.1 copy.26
  8.7 0.7 multiply_add_fusion
  9.4 0.1 fusion.41
  9.5 3.0 %fusion.19 = bf16[64,8,2048]{2,1,0:T(8,128)(2,1)} fusion(bf16[64,512]{1,0:T(8,128)(2,1)S(1)} %fusion.41, bf16[64,2048]{1,0:T(8,128)(2,1)} %param.7), kind=kOutput, calls=%fused_computation.21 | convolution fusion | flops 135266304 | bytes 2424832 | tf_op jit(solution)/shard_map/dot_general | solution.py:67
  12.6 0.0 copy-start.2
  12.6 0.0 copy-start.1
  12.6 13.3 %all-to-all-start = ((bf16[64,8,2048]{2,1,0:T(8,128)(2,1)}), bf16[64,8,2048]{2,1,0:T(8,128)(2,1)}, u32[]{:S(2)}, u32[]{:S(2)}) async-start(bf16[64,8,2048]{2,1,0:T(8,128)(2,1)} %fusion.19), calls=%async_computation | async-start | bytes 4194304 | tf_op jit(solution)/shard_map/all_to_all | solution.py:48
  25.9 0.0 copy-done.2
  25.9 0.1 copy.27
  26.0 0.1 mul.68
  26.1 0.0 copy-done.1
  26.1 2.5 mul.70
  28.6 4.8 %mul.71 = f32[384,2048]{1,0:T(8,128)} reshape(f32[64,6,2048]{2,1,0:T(8,128)} %mul.70) | data formatting | bytes 6291456 | tf_op jit(solution)/shard_map/mul | solution.py:69
  33.4 4.6 %fusion.20 = bf16[64,8,2048]{2,1,0:T(8,128)(2,1)} fusion(f32[384,2048]{1,0:T(8,128)} %mul.71, f32[384]{0:T(512)S(1)} %mul.68, s32[384]{0:T(512)S(1)} %multiply_add_fusion.1), kind=kOutput, calls=%fused_computation.22 | convolution fusion | flops 808124416 | bytes 5245952 | tf_op jit(solution)/shard_map/dot_general | solution.py:70
  38.0 39.1 %all-to-all-done = bf16[64,8,2048]{2,1,0:T(8,128)(2,1)} async-done(((bf16[64,8,2048]{2,1,0:T(8,128)(2,1)}), bf16[64,8,2048]{2,1,0:T(8,128)(2,1)}, u32[]{:S(2)}, u32[]{:S(2)}) %all-to-all-start) | async-done | bytes 2097184 | tf_op jit(solution)/shard_map/all_to_all | solution.py:48
  77.0 6.0 %all-to-all-start.2 = ((bf16[64,8,2048]{2,1,0:T(8,128)(2,1)}), bf16[64,8,2048]{2,1,0:T(8,128)(2,1)}, u32[]{:S(2)}, u32[]{:S(2)}) async-start(bf16[64,8,2048]{2,1,0:T(8,128)(2,1)} %fusion.20), calls=%async_computation.2 | async-start | bytes 4194304 | tf_op jit(solution)/shard_map/all_to_all | solution.py:48
  83.0 0.2 reduce-scatter.3.cloned.1.call-start
  83.3 0.0 copy-start.3
  83.3 4.5 %fusion.12 = f32[512,768]{1,0:T(8,128)S(1)} fusion(bf16[1,2048,768]{2,1,0:T(8,128)(2,1)} %param.11, bf16[64,8,2048]{2,1,0:T(8,128)(2,1)} %all-to-all-done), kind=kOutput, calls=%fused_computation.15 | convolution fusion | flops 1610612736 | bytes 6815744 | tf_op jit(solution)/shard_map/dot_general | solution.py:20
  87.7 0.0 copy-done.3
  87.8 0.0 copy-start.9
  87.8 5.2 %multiply_convert_fusion.4 = (bf16[512,768]{1,0:T(8,128)(2,1)S(1)}, f32[512,768]{1,0:T(8,128)}) fusion(f32[512,768]{1,0:T(8,128)S(1)} %fusion.12, bf16[1,2048,768]{2,1,0:T(8,128)(2,1)S(1)} %copy-done.3, bf16[64,8,2048]{2,1,0:T(8,128)(2,1)} %all-to-all-done), kind=kOutput, calls=%fused_computation.40 | convolution fusion | flops 1612972032 | bytes 9175040 | tf_op jit(solution)/shard_map/dot_general | solution.py:21
  92.9 0.0 copy-done.9
  93.0 0.0 copy-start.8
  93.0 0.0 copy-done
  93.0 3.3 %fusion.14 = bf16[512,2048]{1,0:T(8,128)(2,1)} fusion(bf16[512,768]{1,0:T(8,128)(2,1)S(1)} %get-tuple-element.12, bf16[1,768,2048]{2,1,0:T(8,128)(2,1)S(1)} %copy-done), kind=kOutput, calls=%fused_computation.18 | convolution fusion | flops 1611661312 | bytes 6029312 | tf_op jit(solution)/shard_map/dot_general | solution.py:76
  96.2 0.0 copy-done.8
  96.2 38.0 %all-to-all-done.2 = bf16[64,8,2048]{2,1,0:T(8,128)(2,1)} async-done(((bf16[64,8,2048]{2,1,0:T(8,128)(2,1)}), bf16[64,8,2048]{2,1,0:T(8,128)(2,1)}, u32[]{:S(2)}, u32[]{:S(2)}) %all-to-all-start.2) | async-done | bytes 2097184 | tf_op jit(solution)/shard_map/all_to_all | solution.py:48
  134.2 4.7 %multiply_convert_fusion.3 = (bf16[512,768]{1,0:T(8,128)(2,1)S(1)}, bf16[512,768]{1,0:T(8,128)(2,1)S(1)}) fusion(f32[512,768]{1,0:T(8,128)} %copy-done.9, f32[512,768]{1,0:T(8,128)} %get-tuple-element.10, bf16[1,768,2048]{2,1,0:T(8,128)(2,1)S(1)} %copy-done, bf16[64,8,2048]{2,1,0:T(8,128)(2,1)} %all-to-all-done.2), kind=kOutput, calls=%fused_computation.37 | convolution fusion | flops 1615724544 | bytes 9961472 | tf_op jit(solution)/shard_map/dot_general | solution.py:28
  138.9 0.0 copy-start.5
  138.9 0.0 copy-start.7
  139.0 0.9 copy-done.5
  139.8 0.3 copy-done.7
  140.1 7.2 %convolution_convert_fusion = bf16[2048,1536]{1,0:T(8,128)(2,1)} fusion(bf16[64,8,2048]{2,1,0:T(8,128)(2,1)} %all-to-all-done, bf16[512,768]{1,0:T(8,128)(2,1)S(1)} %get-tuple-element.14, bf16[512,768]{1,0:T(8,128)(2,1)S(1)} %get-tuple-element.13), kind=kOutput, calls=%fused_computation | convolution fusion | flops 3227516928 | bytes 9961472 | tf_op jit(solution)/shard_map/dot_general | solution.py:42
  147.3 0.0 reduce-scatter.3.cloned.1.call-update
  147.3 6.0 %all-to-all-start.1 = ((bf16[64,8,2048]{2,1,0:T(8,128)(2,1)}), bf16[64,8,2048]{2,1,0:T(8,128)(2,1)}, u32[]{:S(2)}, u32[]{:S(2)}) async-start(bf16[64,8,2048]{2,1,0:T(8,128)(2,1)} %bitcast.76), calls=%async_computation.1 | async-start | bytes 4194304 | tf_op jit(solution)/shard_map/all_to_all | solution.py:48
  153.3 0.3 reduce-scatter.5.cloned.1.call-start
  153.6 5.4 %convolution_convert_fusion.1 = bf16[768,2048]{1,0:T(8,128)(2,1)} fusion(bf16[512,768]{1,0:T(8,128)(2,1)} %copy-done.8, bf16[64,8,2048]{2,1,0:T(8,128)(2,1)} %all-to-all-done.2), kind=kOutput, calls=%fused_computation.4 | convolution fusion | flops 1612185600 | bytes 6029312 | tf_op jit(solution)/shard_map/dot_general | solution.py:42
  159.0 0.0 reduce-scatter.5.cloned.1.call-update
  159.0 0.0 copy-start.4
  159.0 0.0 copy-start.6
  159.0 4.1 %fusion.6 = f32[512,2048]{1,0:T(8,128)S(1)} fusion(bf16[512,768]{1,0:T(8,128)(2,1)} %copy-done.7, bf16[1,2048,768]{2,1,0:T(8,128)(2,1)} %param.12), kind=kOutput, calls=%fused_computation.9 | convolution fusion | flops 1610612736 | bytes 8126464 | tf_op jit(solution)/shard_map/dot_general | solution.py:35
  163.1 0.0 copy-done.4
  163.1 0.0 copy-done.6
  163.1 3.1 %fusion.21 = bf16[64,8,2048]{2,1,0:T(8,128)(2,1)} fusion(f32[512,2048]{1,0:T(8,128)S(1)} %fusion.6, bf16[512,768]{1,0:T(8,128)(2,1)S(1)} %copy-done.6, bf16[1,2048,768]{2,1,0:T(8,128)(2,1)S(1)} %copy-done.4), kind=kOutput, calls=%fused_computation.23 | convolution fusion | flops 1612709888 | bytes 10223616 | tf_op jit(solution)/shard_map/dot_general | solution.py:34
  166.3 38.2 %all-to-all-done.1 = bf16[64,8,2048]{2,1,0:T(8,128)(2,1)} async-done(((bf16[64,8,2048]{2,1,0:T(8,128)(2,1)}), bf16[64,8,2048]{2,1,0:T(8,128)(2,1)}, u32[]{:S(2)}, u32[]{:S(2)}) %all-to-all-start.1) | async-done | bytes 2097184 | tf_op jit(solution)/shard_map/all_to_all | solution.py:48
  204.5 6.0 %all-to-all-start.3 = ((bf16[64,8,2048]{2,1,0:T(8,128)(2,1)}), bf16[64,8,2048]{2,1,0:T(8,128)(2,1)}, u32[]{:S(2)}, u32[]{:S(2)}) async-start(bf16[64,8,2048]{2,1,0:T(8,128)(2,1)} %fusion.21), calls=%async_computation.3 | async-start | bytes 4194304 | tf_op jit(solution)/shard_map/all_to_all | solution.py:48
  210.5 0.1 copy.29
  210.6 2.6 fusion.24
  213.2 1.3 fusion
  214.6 0.9 copy.34
  215.4 46.2 %all-to-all-done.3 = bf16[64,8,2048]{2,1,0:T(8,128)(2,1)} async-done(((bf16[64,8,2048]{2,1,0:T(8,128)(2,1)}), bf16[64,8,2048]{2,1,0:T(8,128)(2,1)}, u32[]{:S(2)}, u32[]{:S(2)}) %all-to-all-start.3) | async-done | bytes 2097184 | tf_op jit(solution)/shard_map/all_to_all | solution.py:48
  261.6 2.8 %convolution_convert_fusion.4 = bf16[64,2048]{1,0:T(8,128)(2,1)} fusion(bf16[64,512]{1,0:T(8,128)(2,1)S(1)} %fusion.41, bf16[64,8,2048]{2,1,0:T(8,128)(2,1)} %all-to-all-done.3), kind=kOutput, calls=%fused_computation.24 | convolution fusion | flops 134348800 | bytes 2424832 | tf_op jit(solution)/shard_map/dot_general | solution.py:90
  264.4 0.0 reduce-scatter.3.cloned.1.call-done
  264.4 2.6 slice_bitcast_fusion
  267.0 0.0 reduce-scatter.5.cloned.1.call-done
  (1 shorter events, 0.0 us)
Async XLA Ops:
  7.2 85.8 %copy-start = (bf16[1,768,2048]{2,1,0:T(8,128)(2,1)S(1)}, bf16[1,768,2048]{2,1,0:T(8,128)(2,1)}, u32[]{:S(2)}) copy-start(bf16[1,768,2048]{2,1,0:T(8,128)(2,1)} %param.13) | copy-start | bytes 9437188
  12.6 13.3 %copy-start.2 = (f32[64,6]{0,1:T(8,128)S(1)}, f32[64,6]{0,1:T(8,128)}, u32[]{:S(2)}) copy-start(f32[64,6]{0,1:T(8,128)} %param.9) | copy-start | bytes 4612
  12.6 13.6 %copy-start.1 = (bf16[64,2048]{1,0:T(8,128)(2,1)S(1)}, bf16[64,2048]{1,0:T(8,128)(2,1)}, u32[]{:S(2)}) copy-start(bf16[64,2048]{1,0:T(8,128)(2,1)} %param.10) | copy-start | bytes 786436
  12.6 64.5 %all-to-all-start = ((bf16[64,8,2048]{2,1,0:T(8,128)(2,1)}), bf16[64,8,2048]{2,1,0:T(8,128)(2,1)}, u32[]{:S(2)}, u32[]{:S(2)}) async-start(bf16[64,8,2048]{2,1,0:T(8,128)(2,1)} %fusion.19), calls=%async_computation | async-start | bytes 4194304 | tf_op jit(solution)/shard_map/all_to_all | solution.py:48
  77.0 57.2 %all-to-all-start.2 = ((bf16[64,8,2048]{2,1,0:T(8,128)(2,1)}), bf16[64,8,2048]{2,1,0:T(8,128)(2,1)}, u32[]{:S(2)}, u32[]{:S(2)}) async-start(bf16[64,8,2048]{2,1,0:T(8,128)(2,1)} %fusion.20), calls=%async_computation.2 | async-start | bytes 4194304 | tf_op jit(solution)/shard_map/all_to_all | solution.py:48
  83.0 181.4 %reduce-scatter.3.cloned.1.call-start = ((), (), s32[]{:S(2)}) async-start(), calls=%async_computation.6 | async-start | bytes 7864320 | tf_op jit(solution)/shard_map/reduce_scatter | solution.py:94
  83.3 4.5 %copy-start.3 = (bf16[1,2048,768]{2,1,0:T(8,128)(2,1)S(1)}, bf16[1,2048,768]{2,1,0:T(8,128)(2,1)}, u32[]{:S(2)}) copy-start(bf16[1,2048,768]{2,1,0:T(8,128)(2,1)} %param.12) | copy-start | bytes 9437188
  87.8 5.2 %copy-start.9 = (f32[512,768]{1,0:T(8,128)}, f32[512,768]{1,0:T(8,128)S(1)}, u32[]{:S(2)}) copy-start(f32[512,768]{1,0:T(8,128)S(1)} %fusion.12) | copy-start | bytes 4718596
  93.0 3.3 %copy-start.8 = (bf16[512,768]{1,0:T(8,128)(2,1)}, bf16[512,768]{1,0:T(8,128)(2,1)S(1)}, u32[]{:S(2)}) copy-start(bf16[512,768]{1,0:T(8,128)(2,1)S(1)} %get-tuple-element.12) | copy-start | bytes 2359300
  138.9 0.9 copy-start.5
  138.9 1.1 copy-start.7
  147.3 57.2 %all-to-all-start.1 = ((bf16[64,8,2048]{2,1,0:T(8,128)(2,1)}), bf16[64,8,2048]{2,1,0:T(8,128)(2,1)}, u32[]{:S(2)}, u32[]{:S(2)}) async-start(bf16[64,8,2048]{2,1,0:T(8,128)(2,1)} %bitcast.76), calls=%async_computation.1 | async-start | bytes 4194304 | tf_op jit(solution)/shard_map/all_to_all | solution.py:48
  153.3 113.7 %reduce-scatter.5.cloned.1.call-start = ((), (), s32[]{:S(2)}) async-start(), calls=%async_computation.7 | async-start | bytes 3932160 | tf_op jit(solution)/shard_map/reduce_scatter | solution.py:100
  159.0 4.1 %copy-start.4 = (bf16[1,2048,768]{2,1,0:T(8,128)(2,1)S(1)}, bf16[1,2048,768]{2,1,0:T(8,128)(2,1)}, u32[]{:S(2)}) copy-start(bf16[1,2048,768]{2,1,0:T(8,128)(2,1)} %param.11) | copy-start | bytes 9437188
  159.0 4.1 %copy-start.6 = (bf16[512,768]{1,0:T(8,128)(2,1)S(1)}, bf16[512,768]{1,0:T(8,128)(2,1)}, u32[]{:S(2)}) copy-start(bf16[512,768]{1,0:T(8,128)(2,1)} %copy-done.5) | copy-start | bytes 2359300
  204.5 57.2 %all-to-all-start.3 = ((bf16[64,8,2048]{2,1,0:T(8,128)(2,1)}), bf16[64,8,2048]{2,1,0:T(8,128)(2,1)}, u32[]{:S(2)}, u32[]{:S(2)}) async-start(bf16[64,8,2048]{2,1,0:T(8,128)(2,1)} %fusion.21), calls=%async_computation.3 | async-start | bytes 4194304 | tf_op jit(solution)/shard_map/all_to_all | solution.py:48
Sparse Core Ops, SparseCore 0:
  147.4 63.1 reduce-scatter.2
  213.8 40.5 reduce-scatter.4

commit v14 on v13

--- a/solution.py
+++ b/solution.py
@@ -64,7 +64,12 @@
     )
     pick3 = pick.reshape(tok_rows, top_count, total_rows)
     owner = jnp.sum(pick3, axis=1)
-    outgoing = jnp.dot(owner.T, tokens, preferred_element_type=jnp.float32).astype(jnp.bfloat16)
+    slot_owner = jnp.sum(
+        jnp.arange(total_rows, dtype=positions.dtype)[:, None, None]
+        == positions.reshape(1, tok_rows, top_count),
+        axis=2,
+    ).astype(jnp.bfloat16)
+    outgoing = jnp.dot(slot_owner, tokens, preferred_element_type=jnp.float32).astype(jnp.bfloat16)
     slot_rows = exchange(outgoing.reshape(experts, capacity, features)).reshape(-1, features)
     scaled = (gate_probs[:, :, None] * out_cot[:, None, :].astype(jnp.float32)).astype(jnp.bfloat16)
     grad_out = jnp.dot(

time: 275 us -> 275 us (level)
  no operation moved by 1% of the time
where the time goes in v14:
time: 275 us; the launch traced here: 274 us
  waiting for transfers between devices  161 us (59%)
  matrix products  52 us (19%)
  starting transfers between devices  31.8 us (12%)
  between operations  14.2 us (5%)
  local copies, waits for them, and re-layouts  13.5 us (5%)
    all_to_all x4, waiting for transfers between devices, exchange(): lax.all_to_all(blocks, 'expert', split_axis=0, concat_axis=0, tiled=True)  161 us
    all_to_all x4, starting transfers between devices, exchange(): lax.all_to_all(blocks, 'expert', split_axis=0, concat_axis=0, tiled=True)  31.3 us
    dot_general x2, matrix products, outer_sum(): lax.dot_general(left, right, (((0,), (0,)), ((), ())), preferred_element_...  12.5 us
    mul x3, local copies, waits for them, and re-layouts, per_device(): gate_probs[:, :, None] * out_cot[:, None, :].astype(jnp.float32)  7.34 us
  transfers between devices with their start and end apart: 6, of which 4 were waited for; matrix products, arithmetic and copies ran while one was open for 18% of the time, Pallas kernels for 0%

profile of v14, /device:TPU:1, one launch (start us, length us, event | category | flops | bytes accessed | tf_op | source)
XLA Modules:
  0.0 273.8 jit_solution(5900754703749483381)
XLA Ops:
  7.2 0.0 copy-start
  7.2 0.9 copy.27
  8.1 0.1 eq.70
  8.2 0.2 fusion.37
  8.5 0.1 reduce_sum.33
  8.6 0.1 copy.28
  8.7 0.7 multiply_add_fusion
  9.4 0.1 convert_reduce_fusion
  9.5 3.0 %fusion.19 = bf16[64,8,2048]{2,1,0:T(8,128)(2,1)} fusion(bf16[64,2048]{1,0:T(8,128)(2,1)} %param.7, s32[512,64]{0,1:T(8,128)S(1)} %convert_reduce_fusion), kind=kOutput, calls=%fused_computation.21 | convolution fusion | flops 135299072 | bytes 2490368 | tf_op jit(solution)/shard_map/dot_general | solution.py:72
  12.5 0.0 copy-start.2
  12.6 0.0 copy-start.1
  12.6 13.3 %all-to-all-start = ((bf16[64,8,2048]{2,1,0:T(8,128)(2,1)}), bf16[64,8,2048]{2,1,0:T(8,128)(2,1)}, u32[]{:S(2)}, u32[]{:S(2)}) async-start(bf16[64,8,2048]{2,1,0:T(8,128)(2,1)} %fusion.19), calls=%async_computation | async-start | bytes 4194304 | tf_op jit(solution)/shard_map/all_to_all | solution.py:48
  25.9 0.0 copy-done.2
  25.9 0.1 copy.29
  26.0 0.1 mul.70
  26.1 0.0 copy-done.1
  26.1 2.5 mul.72
  28.6 4.7 %mul.73 = f32[384,2048]{1,0:T(8,128)} reshape(f32[64,6,2048]{2,1,0:T(8,128)} %mul.72) | data formatting | bytes 6291456 | tf_op jit(solution)/shard_map/mul | solution.py:74
  33.3 4.6 %fusion.20 = bf16[64,8,2048]{2,1,0:T(8,128)(2,1)} fusion(f32[384,2048]{1,0:T(8,128)} %mul.73, f32[384]{0:T(512)S(1)} %mul.70, s32[384]{0:T(512)S(1)} %multiply_add_fusion.1), kind=kOutput, calls=%fused_computation.22 | convolution fusion | flops 808124416 | bytes 5245952 | tf_op jit(solution)/shard_map/dot_general | solution.py:75
  37.9 39.1 %all-to-all-done = bf16[64,8,2048]{2,1,0:T(8,128)(2,1)} async-done(((bf16[64,8,2048]{2,1,0:T(8,128)(2,1)}), bf16[64,8,2048]{2,1,0:T(8,128)(2,1)}, u32[]{:S(2)}, u32[]{:S(2)}) %all-to-all-start) | async-done | bytes 2097184 | tf_op jit(solution)/shard_map/all_to_all | solution.py:48
  77.0 6.0 %all-to-all-start.2 = ((bf16[64,8,2048]{2,1,0:T(8,128)(2,1)}), bf16[64,8,2048]{2,1,0:T(8,128)(2,1)}, u32[]{:S(2)}, u32[]{:S(2)}) async-start(bf16[64,8,2048]{2,1,0:T(8,128)(2,1)} %fusion.20), calls=%async_computation.2 | async-start | bytes 4194304 | tf_op jit(solution)/shard_map/all_to_all | solution.py:48
  83.0 0.2 reduce-scatter.3.cloned.1.call-start
  83.3 0.0 copy-start.3
  83.3 4.5 %fusion.12 = f32[512,768]{1,0:T(8,128)S(1)} fusion(bf16[1,2048,768]{2,1,0:T(8,128)(2,1)} %param.11, bf16[64,8,2048]{2,1,0:T(8,128)(2,1)} %all-to-all-done), kind=kOutput, calls=%fused_computation.15 | convolution fusion | flops 1610612736 | bytes 6815744 | tf_op jit(solution)/shard_map/dot_general | solution.py:20
  87.7 0.0 copy-done.3
  87.8 0.0 copy-start.9
  87.8 5.2 %multiply_convert_fusion.4 = (bf16[512,768]{1,0:T(8,128)(2,1)S(1)}, f32[512,768]{1,0:T(8,128)}) fusion(f32[512,768]{1,0:T(8,128)S(1)} %fusion.12, bf16[1,2048,768]{2,1,0:T(8,128)(2,1)S(1)} %copy-done.3, bf16[64,8,2048]{2,1,0:T(8,128)(2,1)} %all-to-all-done), kind=kOutput, calls=%fused_computation.40 | convolution fusion | flops 1612972032 | bytes 9175040 | tf_op jit(solution)/shard_map/dot_general | solution.py:21
  92.9 0.0 copy-done.9
  92.9 0.0 copy-start.8
  92.9 0.0 copy-done
  93.0 3.3 %fusion.14 = bf16[512,2048]{1,0:T(8,128)(2,1)} fusion(bf16[512,768]{1,0:T(8,128)(2,1)S(1)} %get-tuple-element.12, bf16[1,768,2048]{2,1,0:T(8,128)(2,1)S(1)} %copy-done), kind=kOutput, calls=%fused_computation.18 | convolution fusion | flops 1611661312 | bytes 6029312 | tf_op jit(solution)/shard_map/dot_general | solution.py:81
  96.2 0.0 copy-done.8
  96.2 38.0 %all-to-all-done.2 = bf16[64,8,2048]{2,1,0:T(8,128)(2,1)} async-done(((bf16[64,8,2048]{2,1,0:T(8,128)(2,1)}), bf16[64,8,2048]{2,1,0:T(8,128)(2,1)}, u32[]{:S(2)}, u32[]{:S(2)}) %all-to-all-start.2) | async-done | bytes 2097184 | tf_op jit(solution)/shard_map/all_to_all | solution.py:48
  134.2 4.7 %multiply_convert_fusion.3 = (bf16[512,768]{1,0:T(8,128)(2,1)S(1)}, bf16[512,768]{1,0:T(8,128)(2,1)S(1)}) fusion(f32[512,768]{1,0:T(8,128)} %copy-done.9, f32[512,768]{1,0:T(8,128)} %get-tuple-element.10, bf16[1,768,2048]{2,1,0:T(8,128)(2,1)S(1)} %copy-done, bf16[64,8,2048]{2,1,0:T(8,128)(2,1)} %all-to-all-done.2), kind=kOutput, calls=%fused_computation.37 | convolution fusion | flops 1615724544 | bytes 9961472 | tf_op jit(solution)/shard_map/dot_general | solution.py:28
  138.9 0.0 copy-start.5
  138.9 0.0 copy-start.7
  139.0 0.9 copy-done.5
  139.8 0.3 copy-done.7
  140.1 7.1 %convolution_convert_fusion = bf16[2048,1536]{1,0:T(8,128)(2,1)} fusion(bf16[64,8,2048]{2,1,0:T(8,128)(2,1)} %all-to-all-done, bf16[512,768]{1,0:T(8,128)(2,1)S(1)} %get-tuple-element.14, bf16[512,768]{1,0:T(8,128)(2,1)S(1)} %get-tuple-element.13), kind=kOutput, calls=%fused_computation | convolution fusion | flops 3227516928 | bytes 9961472 | tf_op jit(solution)/shard_map/dot_general | solution.py:42
  147.2 0.0 reduce-scatter.3.cloned.1.call-update
  147.2 6.0 %all-to-all-start.1 = ((bf16[64,8,2048]{2,1,0:T(8,128)(2,1)}), bf16[64,8,2048]{2,1,0:T(8,128)(2,1)}, u32[]{:S(2)}, u32[]{:S(2)}) async-start(bf16[64,8,2048]{2,1,0:T(8,128)(2,1)} %bitcast.75), calls=%async_computation.1 | async-start | bytes 4194304 | tf_op jit(solution)/shard_map/all_to_all | solution.py:48
  153.3 0.3 reduce-scatter.5.cloned.1.call-start
  153.5 5.4 %convolution_convert_fusion.1 = bf16[768,2048]{1,0:T(8,128)(2,1)} fusion(bf16[512,768]{1,0:T(8,128)(2,1)} %copy-done.8, bf16[64,8,2048]{2,1,0:T(8,128)(2,1)} %all-to-all-done.2), kind=kOutput, calls=%fused_computation.4 | convolution fusion | flops 1612185600 | bytes 6029312 | tf_op jit(solution)/shard_map/dot_general | solution.py:42
  158.9 0.0 reduce-scatter.5.cloned.1.call-update
  159.0 0.0 copy-start.4
  159.0 0.0 copy-start.6
  159.0 4.1 %fusion.6 = f32[512,2048]{1,0:T(8,128)S(1)} fusion(bf16[512,768]{1,0:T(8,128)(2,1)} %copy-done.7, bf16[1,2048,768]{2,1,0:T(8,128)(2,1)} %param.12), kind=kOutput, calls=%fused_computation.9 | convolution fusion | flops 1610612736 | bytes 8126464 | tf_op jit(solution)/shard_map/dot_general | solution.py:35
  163.1 0.0 copy-done.4
  163.1 0.0 copy-done.6
  163.1 3.1 %fusion.21 = bf16[64,8,2048]{2,1,0:T(8,128)(2,1)} fusion(f32[512,2048]{1,0:T(8,128)S(1)} %fusion.6, bf16[512,768]{1,0:T(8,128)(2,1)S(1)} %copy-done.6, bf16[1,2048,768]{2,1,0:T(8,128)(2,1)S(1)} %copy-done.4), kind=kOutput, calls=%fused_computation.23 | convolution fusion | flops 1612709888 | bytes 10223616 | tf_op jit(solution)/shard_map/dot_general | solution.py:34
  166.3 38.2 %all-to-all-done.1 = bf16[64,8,2048]{2,1,0:T(8,128)(2,1)} async-done(((bf16[64,8,2048]{2,1,0:T(8,128)(2,1)}), bf16[64,8,2048]{2,1,0:T(8,128)(2,1)}, u32[]{:S(2)}, u32[]{:S(2)}) %all-to-all-start.1) | async-done | bytes 2097184 | tf_op jit(solution)/shard_map/all_to_all | solution.py:48
  204.4 6.0 %all-to-all-start.3 = ((bf16[64,8,2048]{2,1,0:T(8,128)(2,1)}), bf16[64,8,2048]{2,1,0:T(8,128)(2,1)}, u32[]{:S(2)}, u32[]{:S(2)}) async-start(bf16[64,8,2048]{2,1,0:T(8,128)(2,1)} %fusion.21), calls=%async_computation.3 | async-start | bytes 4194304 | tf_op jit(solution)/shard_map/all_to_all | solution.py:48
  210.5 0.1 copy.31
  210.6 0.1 fusion.41
  210.7 2.6 fusion.24
  213.3 1.3 fusion
  214.7 0.9 copy.36
  215.6 46.1 %all-to-all-done.3 = bf16[64,8,2048]{2,1,0:T(8,128)(2,1)} async-done(((bf16[64,8,2048]{2,1,0:T(8,128)(2,1)}), bf16[64,8,2048]{2,1,0:T(8,128)(2,1)}, u32[]{:S(2)}, u32[]{:S(2)}) %all-to-all-start.3) | async-done | bytes 2097184 | tf_op jit(solution)/shard_map/all_to_all | solution.py:48
  261.6 2.8 %convolution_convert_fusion.4 = bf16[64,2048]{1,0:T(8,128)(2,1)} fusion(bf16[64,512]{1,0:T(8,128)(2,1)S(1)} %fusion.41, bf16[64,8,2048]{2,1,0:T(8,128)(2,1)} %all-to-all-done.3), kind=kOutput, calls=%fused_computation.24 | convolution fusion | flops 134348800 | bytes 2424832 | tf_op jit(solution)/shard_map/dot_general | solution.py:95
  264.4 0.0 reduce-scatter.3.cloned.1.call-done
  264.4 2.6 slice_bitcast_fusion
  267.0 0.0 reduce-scatter.5.cloned.1.call-done
  (1 shorter events, 0.0 us)
Async XLA Ops:
  7.2 85.8 %copy-start = (bf16[1,768,2048]{2,1,0:T(8,128)(2,1)S(1)}, bf16[1,768,2048]{2,1,0:T(8,128)(2,1)}, u32[]{:S(2)}) copy-start(bf16[1,768,2048]{2,1,0:T(8,128)(2,1)} %param.13) | copy-start | bytes 9437188
  12.5 13.3 %copy-start.2 = (f32[64,6]{0,1:T(8,128)S(1)}, f32[64,6]{0,1:T(8,128)}, u32[]{:S(2)}) copy-start(f32[64,6]{0,1:T(8,128)} %param.9) | copy-start | bytes 4612
  12.6 13.6 %copy-start.1 = (bf16[64,2048]{1,0:T(8,128)(2,1)S(1)}, bf16[64,2048]{1,0:T(8,128)(2,1)}, u32[]{:S(2)}) copy-start(bf16[64,2048]{1,0:T(8,128)(2,1)} %param.10) | copy-start | bytes 786436
  12.6 64.5 %all-to-all-start = ((bf16[64,8,2048]{2,1,0:T(8,128)(2,1)}), bf16[64,8,2048]{2,1,0:T(8,128)(2,1)}, u32[]{:S(2)}, u32[]{:S(2)}) async-start(bf16[64,8,2048]{2,1,0:T(8,128)(2,1)} %fusion.19), calls=%async_computation | async-start | bytes 4194304 | tf_op jit(solution)/shard_map/all_to_all | solution.py:48
  77.0 57.2 %all-to-all-start.2 = ((bf16[64,8,2048]{2,1,0:T(8,128)(2,1)}), bf16[64,8,2048]{2,1,0:T(8,128)(2,1)}, u32[]{:S(2)}, u32[]{:S(2)}) async-start(bf16[64,8,2048]{2,1,0:T(8,128)(2,1)} %fusion.20), calls=%async_computation.2 | async-start | bytes 4194304 | tf_op jit(solution)/shard_map/all_to_all | solution.py:48
  83.0 181.4 %reduce-scatter.3.cloned.1.call-start = ((), (), s32[]{:S(2)}) async-start(), calls=%async_computation.6 | async-start | bytes 7864320 | tf_op jit(solution)/shard_map/reduce_scatter | solution.py:99
  83.3 4.5 %copy-start.3 = (bf16[1,2048,768]{2,1,0:T(8,128)(2,1)S(1)}, bf16[1,2048,768]{2,1,0:T(8,128)(2,1)}, u32[]{:S(2)}) copy-start(bf16[1,2048,768]{2,1,0:T(8,128)(2,1)} %param.12) | copy-start | bytes 9437188
  87.8 5.2 %copy-start.9 = (f32[512,768]{1,0:T(8,128)}, f32[512,768]{1,0:T(8,128)S(1)}, u32[]{:S(2)}) copy-start(f32[512,768]{1,0:T(8,128)S(1)} %fusion.12) | copy-start | bytes 4718596
  92.9 3.3 %copy-start.8 = (bf16[512,768]{1,0:T(8,128)(2,1)}, bf16[512,768]{1,0:T(8,128)(2,1)S(1)}, u32[]{:S(2)}) copy-start(bf16[512,768]{1,0:T(8,128)(2,1)S(1)} %get-tuple-element.12) | copy-start | bytes 2359300
  138.9 0.9 copy-start.5
  138.9 1.1 copy-start.7
  147.2 57.2 %all-to-all-start.1 = ((bf16[64,8,2048]{2,1,0:T(8,128)(2,1)}), bf16[64,8,2048]{2,1,0:T(8,128)(2,1)}, u32[]{:S(2)}, u32[]{:S(2)}) async-start(bf16[64,8,2048]{2,1,0:T(8,128)(2,1)} %bitcast.75), calls=%async_computation.1 | async-start | bytes 4194304 | tf_op jit(solution)/shard_map/all_to_all | solution.py:48
  153.3 113.7 %reduce-scatter.5.cloned.1.call-start = ((), (), s32[]{:S(2)}) async-start(), calls=%async_computation.7 | async-start | bytes 3932160 | tf_op jit(solution)/shard_map/reduce_scatter | solution.py:105
  159.0 4.1 %copy-start.4 = (bf16[1,2048,768]{2,1,0:T(8,128)(2,1)S(1)}, bf16[1,2048,768]{2,1,0:T(8,128)(2,1)}, u32[]{:S(2)}) copy-start(bf16[1,2048,768]{2,1,0:T(8,128)(2,1)} %param.11) | copy-start | bytes 9437188
  159.0 4.1 %copy-start.6 = (bf16[512,768]{1,0:T(8,128)(2,1)S(1)}, bf16[512,768]{1,0:T(8,128)(2,1)}, u32[]{:S(2)}) copy-start(bf16[512,768]{1,0:T(8,128)(2,1)} %copy-done.5) | copy-start | bytes 2359300
  204.4 57.2 %all-to-all-start.3 = ((bf16[64,8,2048]{2,1,0:T(8,128)(2,1)}), bf16[64,8,2048]{2,1,0:T(8,128)(2,1)}, u32[]{:S(2)}, u32[]{:S(2)}) async-start(bf16[64,8,2048]{2,1,0:T(8,128)(2,1)} %fusion.21), calls=%async_computation.3 | async-start | bytes 4194304 | tf_op jit(solution)/shard_map/all_to_all | solution.py:48
Sparse Core Ops, SparseCore 0:
  147.4 63.1 reduce-scatter.2
  213.7 40.5 reduce-scatter.4
